TPU v7x, 256 devices: a whole 4x4x8 slice. The times are simulated.
256 devices in a mesh: pairs: 32 (over x, z), tm: 8 (over y, core).
Axes of the slice: x: 4, y: 4, z: 8, core: 2. Of those that a mesh axis runs over, the one named last changes fastest.
Arguments:
- traces: float32 [16, 2048, 6144], P('tm', 'pairs'), may hold values from -64 to 64
- station_slot: int32 [2048], replicated, may hold values from 0 to 2047, as said below
- pair_stations: int32 [2048, 2], P('pairs'), may hold values from 0 to 2047, as said below
Outputs:
- correlation_stack: float32 [2048, 2048], P('tm', 'pairs')
Inputs may be any that keep to these rules, and one draw needn't show every extreme that they name: `station_slot`: A permutation: rows r * 64 to (r + 1) * 64 - 1 of traces are the stations of owner r. `pair_stations`: in each block of 64 pairs (the pairs of one device), at most 8 of the 128 pair ends name stations whose station_slot // 64 is one value, and in every block one value is named by exactly 8 ends. A pair may name one station twice.
All inputs are finite; a program needn't handle non-finite values.
Results may differ from a plain program's by a relative error of at most 0.011.
Values may be sent and summed in bfloat16 or wider, within the bound.
No kernel may reach another device: no remote copies, remote signals or barrier semaphores. Data moves between devices by JAX's collectives and lax.ppermute only.
A program may use at most 64 MiB of HBM per device.

v0:
```python
import math

import jax
import jax.numpy as jnp
from jax import lax
from jax.sharding import PartitionSpec as P

F = 1536
FLO = 32
LAG = 1024


two_pi = 6.283185307179586


def tapered_rows(traces):
    length = traces.shape[-1]
    sample_times = lax.iota(jnp.int32, length).astype(jnp.float32)
    hann_window = 0.5 - 0.5 * jnp.cos((sample_times + 0.5) * (two_pi / length))
    centred = traces - jnp.mean(traces, axis=-1, keepdims=True)
    return (centred * hann_window).astype(jnp.bfloat16)


def forward_table(first_row, row_count, length, first_bin, bins):
    sample_times = first_row + lax.iota(jnp.int32, row_count)
    frequencies = first_bin + lax.iota(jnp.int32, bins)
    phases = sample_times[:, None] * frequencies[None, :] % length
    angles = phases.astype(jnp.float32) * (two_pi / length)
    return jnp.concatenate([jnp.cos(angles), -jnp.sin(angles)], axis=1).astype(jnp.bfloat16)


def whiten(spectrum, bins):
    real_part = spectrum[..., :bins]
    imag_part = spectrum[..., bins:]
    energy = real_part * real_part + imag_part * imag_part
    water_level = jnp.mean(energy, axis=-1, keepdims=True)
    scaling = lax.rsqrt(energy + 0.1 * water_level + 1e-06)
    return jnp.concatenate([real_part * scaling, imag_part * scaling], axis=-1).astype(jnp.bfloat16)


def whiten_spectra(tapered, first_bin, bins):
    length = tapered.shape[1]
    block_rows = min(512, length)

    def add_block(step_index, running):
        first_row = step_index * block_rows
        segment = lax.dynamic_slice_in_dim(tapered, first_row, block_rows, 1)
        cos_table = forward_table(first_row, block_rows, length, first_bin, bins)
        return running + jnp.dot(segment, cos_table, preferred_element_type=jnp.float32)

    spectrum = lax.fori_loop(
        0, length // block_rows, add_block, jnp.zeros((tapered.shape[0], 2 * bins), jnp.float32)
    )
    return whiten(spectrum, bins)


def cross_spectra(left_ends, right_ends, bins):
    left_real = left_ends[..., :bins].astype(jnp.float32)
    left_imag = left_ends[..., bins:].astype(jnp.float32)
    right_real = right_ends[..., :bins].astype(jnp.float32)
    right_imag = right_ends[..., bins:].astype(jnp.float32)
    return jnp.concatenate(
        [
            left_real * right_real + left_imag * right_imag,
            left_imag * right_real - left_real * right_imag,
        ],
        axis=-1,
    )


def lag_block(stacked, first_row, row_count, first_bin, bins, length, half_span):
    lag_values = first_row + lax.iota(jnp.int32, row_count) - half_span
    frequencies = first_bin + lax.iota(jnp.int32, bins)
    phases = lag_values[:, None] * frequencies[None, :] % length
    angles = phases.astype(jnp.float32) * (two_pi / length)
    lag_table = jnp.concatenate([jnp.cos(angles), -jnp.sin(angles)], axis=1)
    return lax.dot_general(
        lag_table,
        stacked,
        (((1,), (1,)), ((), ())),
        precision=lax.Precision.HIGHEST,
        preferred_element_type=jnp.float32,
    )


def lag_rows(stacked, row_count, block_rows, length):

    def one_block(block_index):
        return lag_block(stacked, block_index * block_rows, block_rows, FLO, F, length, LAG)

    pieces = lax.map(one_block, jnp.arange(row_count // block_rows, dtype=jnp.int32))
    return pieces.reshape(row_count, stacked.shape[0])


def on_device(traces, station_slot, pair_stations):
    window_count, station_count, length = traces.shape
    pair_count = pair_stations.shape[0]
    blocks = lax.axis_size("pairs")
    capacity = 4 * pair_count // blocks
    own_index = lax.axis_index("pairs")
    every_pair = lax.all_gather(pair_stations, "pairs", axis=0, tiled=True)
    slot_ids = station_slot[every_pair.reshape(blocks, 2 * pair_count)]
    owners = slot_ids // station_count
    local_rows = slot_ids % station_count
    onehot = (owners[:, :, None] == lax.iota(jnp.int32, blocks)[None, None, :]).astype(jnp.int32)
    end_ranks = jnp.sum((jnp.cumsum(onehot, axis=1) - onehot) * onehot, axis=2)
    wanted = (owners == own_index)[:, :, None] & (
        end_ranks[:, :, None] == lax.iota(jnp.int32, capacity)[None, None, :]
    )
    send_rows = jnp.sum(jnp.where(wanted, local_rows[:, :, None], 0), axis=1)
    own_owners = lax.dynamic_index_in_dim(owners, own_index, 0, keepdims=False)
    own_ranks = lax.dynamic_index_in_dim(end_ranks, own_index, 0, keepdims=False)
    positions = own_owners * capacity + own_ranks
    tapered = tapered_rows(traces).reshape(window_count * station_count, length)
    spectra = whiten_spectra(tapered, FLO, F).reshape(window_count, station_count, 2 * F)
    received = lax.all_to_all(
        spectra[:, send_rows], "pairs", split_axis=1, concat_axis=1, tiled=True
    )
    held_windows = received.shape[0]
    flattened = received.reshape(held_windows, blocks * capacity, 2 * F)
    pair_ends = flattened[:, positions].reshape(held_windows, pair_count, 2, 2 * F)
    cross_terms = cross_spectra(pair_ends[:, :, 0], pair_ends[:, :, 1], F)
    stacked = jnp.sum(cross_terms, axis=0)
    lag_share = 2 * LAG // lax.axis_size("tm")
    normalizer = 1.0 / math.sqrt(F * window_count * lax.axis_size("tm"))
    block_rows = min(256, lag_share)
    return lax.psum_scatter(
        lag_rows(stacked, lax.axis_size("tm") * lag_share, block_rows, length) * normalizer,
        "tm",
        scatter_dimension=0,
        tiled=True,
    )


def solution(mesh):
    in_specs = (P("tm", "pairs", None), P(), P("pairs", None))
    out_specs = P("tm", "pairs")
    return jax.shard_map(
        on_device, mesh=mesh, in_specs=in_specs, out_specs=out_specs, check_vma=False
    )
```

profile of v0, /device:TPU:1, one launch (start us, length us, event | category | flops | bytes accessed | tf_op | source)
XLA Modules:
  0.0 503.9 jit_solution(11358334564074070772)
XLA Ops:
  11.0 200.6 %while.29 = (s32[]{:T(128)}, f32[128,3072]{1,0:T(8,128)}, bf16[128,6144]{1,0:T(8,128)(2,1)}, s32[]{:T(128)}, s32[]{:T(128)}, /*index=5*/s32[]{:T(128)}, s32[]{:T(128)}) while((s32[]{:T(128)}, f32[128,3072]{1,0:T(8,128)}, bf16[128,6144]{1,0:T(8,128)(2,1)}, s32[]{:T(128)}, s32[]{:T(128)}, /*index=5*/s32[]{:T(128)}, s32[]{:T(128)}) %tuple.80), condition=%wide.region_2.3_spmd.clone, body=%wide.region_1.2_spmd.clone.sunk | while | flops 419170304 | bytes 9584781 | solution.py:51
  11.0 13.5 %cosine_convert_fusion.2 = (bf16[512,1536]{1,0:T(8,128)(2,1)S(1)}, bf16[512,1536]{1,0:T(8,128)(2,1)S(1)}) fusion(s32[1536]{0:T(1024)S(1)} %iota_add_fusion.7, s32[512]{0:T(512)S(1)} %iota_add_fusion.8), kind=kLoop, calls=%fused_computation.29.clone.1 | loop fusion | flops 9437184 | bytes 3153920 | tf_op jit(solution)/shard_map/convert
  27.2 13.5 %cosine_convert_fusion.2 = (bf16[512,1536]{1,0:T(8,128)(2,1)S(1)}, bf16[512,1536]{1,0:T(8,128)(2,1)S(1)}) fusion(s32[1536]{0:T(1024)S(1)} %iota_add_fusion.7, s32[512]{0:T(512)S(1)} %iota_add_fusion.8), kind=kLoop, calls=%fused_computation.29.clone.1 | loop fusion | flops 9437184 | bytes 3153920 | tf_op jit(solution)/shard_map/convert
  44.0 13.5 %cosine_convert_fusion.2 = (bf16[512,1536]{1,0:T(8,128)(2,1)S(1)}, bf16[512,1536]{1,0:T(8,128)(2,1)S(1)}) fusion(s32[1536]{0:T(1024)S(1)} %iota_add_fusion.7, s32[512]{0:T(512)S(1)} %iota_add_fusion.8), kind=kLoop, calls=%fused_computation.29.clone.1 | loop fusion | flops 9437184 | bytes 3153920 | tf_op jit(solution)/shard_map/convert
  60.8 13.5 %cosine_convert_fusion.2 = (bf16[512,1536]{1,0:T(8,128)(2,1)S(1)}, bf16[512,1536]{1,0:T(8,128)(2,1)S(1)}) fusion(s32[1536]{0:T(1024)S(1)} %iota_add_fusion.7, s32[512]{0:T(512)S(1)} %iota_add_fusion.8), kind=kLoop, calls=%fused_computation.29.clone.1 | loop fusion | flops 9437184 | bytes 3153920 | tf_op jit(solution)/shard_map/convert
  77.5 13.5 %cosine_convert_fusion.2 = (bf16[512,1536]{1,0:T(8,128)(2,1)S(1)}, bf16[512,1536]{1,0:T(8,128)(2,1)S(1)}) fusion(s32[1536]{0:T(1024)S(1)} %iota_add_fusion.7, s32[512]{0:T(512)S(1)} %iota_add_fusion.8), kind=kLoop, calls=%fused_computation.29.clone.1 | loop fusion | flops 9437184 | bytes 3153920 | tf_op jit(solution)/shard_map/convert
  94.3 13.5 %cosine_convert_fusion.2 = (bf16[512,1536]{1,0:T(8,128)(2,1)S(1)}, bf16[512,1536]{1,0:T(8,128)(2,1)S(1)}) fusion(s32[1536]{0:T(1024)S(1)} %iota_add_fusion.7, s32[512]{0:T(512)S(1)} %iota_add_fusion.8), kind=kLoop, calls=%fused_computation.29.clone.1 | loop fusion | flops 9437184 | bytes 3153920 | tf_op jit(solution)/shard_map/convert
  111.1 13.5 %cosine_convert_fusion.2 = (bf16[512,1536]{1,0:T(8,128)(2,1)S(1)}, bf16[512,1536]{1,0:T(8,128)(2,1)S(1)}) fusion(s32[1536]{0:T(1024)S(1)} %iota_add_fusion.7, s32[512]{0:T(512)S(1)} %iota_add_fusion.8), kind=kLoop, calls=%fused_computation.29.clone.1 | loop fusion | flops 9437184 | bytes 3153920 | tf_op jit(solution)/shard_map/convert
  127.8 13.5 %cosine_convert_fusion.2 = (bf16[512,1536]{1,0:T(8,128)(2,1)S(1)}, bf16[512,1536]{1,0:T(8,128)(2,1)S(1)}) fusion(s32[1536]{0:T(1024)S(1)} %iota_add_fusion.7, s32[512]{0:T(512)S(1)} %iota_add_fusion.8), kind=kLoop, calls=%fused_computation.29.clone.1 | loop fusion | flops 9437184 | bytes 3153920 | tf_op jit(solution)/shard_map/convert
  144.6 13.5 %cosine_convert_fusion.2 = (bf16[512,1536]{1,0:T(8,128)(2,1)S(1)}, bf16[512,1536]{1,0:T(8,128)(2,1)S(1)}) fusion(s32[1536]{0:T(1024)S(1)} %iota_add_fusion.7, s32[512]{0:T(512)S(1)} %iota_add_fusion.8), kind=kLoop, calls=%fused_computation.29.clone.1 | loop fusion | flops 9437184 | bytes 3153920 | tf_op jit(solution)/shard_map/convert
  161.4 13.5 %cosine_convert_fusion.2 = (bf16[512,1536]{1,0:T(8,128)(2,1)S(1)}, bf16[512,1536]{1,0:T(8,128)(2,1)S(1)}) fusion(s32[1536]{0:T(1024)S(1)} %iota_add_fusion.7, s32[512]{0:T(512)S(1)} %iota_add_fusion.8), kind=kLoop, calls=%fused_computation.29.clone.1 | loop fusion | flops 9437184 | bytes 3153920 | tf_op jit(solution)/shard_map/convert
  178.1 13.5 %cosine_convert_fusion.2 = (bf16[512,1536]{1,0:T(8,128)(2,1)S(1)}, bf16[512,1536]{1,0:T(8,128)(2,1)S(1)}) fusion(s32[1536]{0:T(1024)S(1)} %iota_add_fusion.7, s32[512]{0:T(512)S(1)} %iota_add_fusion.8), kind=kLoop, calls=%fused_computation.29.clone.1 | loop fusion | flops 9437184 | bytes 3153920 | tf_op jit(solution)/shard_map/convert
  194.9 13.5 %cosine_convert_fusion.2 = (bf16[512,1536]{1,0:T(8,128)(2,1)S(1)}, bf16[512,1536]{1,0:T(8,128)(2,1)S(1)}) fusion(s32[1536]{0:T(1024)S(1)} %iota_add_fusion.7, s32[512]{0:T(512)S(1)} %iota_add_fusion.8), kind=kLoop, calls=%fused_computation.29.clone.1 | loop fusion | flops 9437184 | bytes 3153920 | tf_op jit(solution)/shard_map/convert
  214.7 36.9 %all-gather = s32[32,64,2]{1,2,0:T(2,128)S(1)} all-gather(s32[1,64,2]{1,2,0:T(2,128)S(1)} %bitcast.77), channel_id=1, replica_groups=mesh['pairs'=32,'tm'=8] {'pairs'}, dimensions={0}, use_global_device_ids=true | all-gather | bytes 16896 | tf_op jit(solution)/shard_map/all_gather | solution.py:101
  251.8 23.0 %gather_fusion = s32[4096]{0:T(1024)S(1)} fusion(s32[2048]{0:T(1024)S(1)} %copy-done, s32[4096]{0:T(1024)S(1)} %bitcast_clamp_fusion), kind=kCustom, calls=%fused_computation | custom fusion | bytes 49152 | tf_op jit(solution)/shard_map/gather | solution.py:102
  279.8 12.9 %gather_fusion.1 = bf16[256,2,3072]{2,1,0:T(2,128)(2,1)} fusion(bf16[2,64,3072]{2,0,1:T(2,128)(2,1)S(1)} %pad_maximum_fusion, s32[1024]{0:T(1024)S(1)} %pad_clamp_fusion.1), kind=kCustom, calls=%fused_computation.1 | custom fusion | bytes 6292480 | tf_op jit(solution)/shard_map/gather | solution.py:117
  299.1 61.0 %all-to-all-done = bf16[2,32,8,3072]{3,0,2,1:T(2,128)(2,1)S(1)} async-done(((bf16[2,32,8,3072]{3,0,2,1:T(2,128)(2,1)}), bf16[2,32,8,3072]{3,0,2,1:T(2,128)(2,1)S(1)}, u32[]{:S(2)}, u32[]{:S(2)}) %all-to-all-start) | async-done | bytes 3145760 | tf_op jit(solution)/shard_map/all_to_all | solution.py:116
  368.9 86.6 %while.28 = (s32[]{:T(128)}, f32[8,256,64]{1,2,0:T(8,128)S(1)}, s32[8]{0:T(128)S(1)}, f32[64,3072]{1,0:T(8,128)S(1)}, s32[]{:T(128)}, /*index=5*/s32[1]{0:T(128)}) while((s32[]{:T(128)}, f32[8,256,64]{1,2,0:T(8,128)S(1)}, s32[8]{0:T(128)S(1)}, f32[64,3072]{1,0:T(8,128)S(1)}, s32[]{:T(128)}, /*index=5*/s32[1]{0:T(128)}) %tuple.81), condition=%wide.region_9.10_spmd, body=%wide.region_8.9_spmd.sunk | while | flops 608700416 | bytes 7157861 | solution.py:91
  370.3 6.4 %fusion.51 = (f32[256,1536]{1,0:T(8,128)S(1)}, f32[256,1536]{1,0:T(8,128)S(1)}) fusion(s32[1536]{0:T(1024)S(1)} %iota_add_fusion.6, s32[256]{0:T(256)S(1)} %add_add_fusion.2), kind=kLoop, calls=%fused_computation.14.clone.1 | loop fusion | flops 3932160 | bytes 3152896 | tf_op jit(solution)/shard_map/while/body/eval_jaxpr/cos | solution.py:76
  381.1 6.4 %fusion.51 = (f32[256,1536]{1,0:T(8,128)S(1)}, f32[256,1536]{1,0:T(8,128)S(1)}) fusion(s32[1536]{0:T(1024)S(1)} %iota_add_fusion.6, s32[256]{0:T(256)S(1)} %add_add_fusion.2), kind=kLoop, calls=%fused_computation.14.clone.1 | loop fusion | flops 3932160 | bytes 3152896 | tf_op jit(solution)/shard_map/while/body/eval_jaxpr/cos | solution.py:76
  391.9 6.4 %fusion.51 = (f32[256,1536]{1,0:T(8,128)S(1)}, f32[256,1536]{1,0:T(8,128)S(1)}) fusion(s32[1536]{0:T(1024)S(1)} %iota_add_fusion.6, s32[256]{0:T(256)S(1)} %add_add_fusion.2), kind=kLoop, calls=%fused_computation.14.clone.1 | loop fusion | flops 3932160 | bytes 3152896 | tf_op jit(solution)/shard_map/while/body/eval_jaxpr/cos | solution.py:76
  402.8 6.4 %fusion.51 = (f32[256,1536]{1,0:T(8,128)S(1)}, f32[256,1536]{1,0:T(8,128)S(1)}) fusion(s32[1536]{0:T(1024)S(1)} %iota_add_fusion.6, s32[256]{0:T(256)S(1)} %add_add_fusion.2), kind=kLoop, calls=%fused_computation.14.clone.1 | loop fusion | flops 3932160 | bytes 3152896 | tf_op jit(solution)/shard_map/while/body/eval_jaxpr/cos | solution.py:76
  413.6 6.4 %fusion.51 = (f32[256,1536]{1,0:T(8,128)S(1)}, f32[256,1536]{1,0:T(8,128)S(1)}) fusion(s32[1536]{0:T(1024)S(1)} %iota_add_fusion.6, s32[256]{0:T(256)S(1)} %add_add_fusion.2), kind=kLoop, calls=%fused_computation.14.clone.1 | loop fusion | flops 3932160 | bytes 3152896 | tf_op jit(solution)/shard_map/while/body/eval_jaxpr/cos | solution.py:76
  456.4 40.6 %reduce-scatter.2.cloned.1.call-done = f32[256,64]{0,1:T(8,128)} async-done(((f32[2048,64]{0,1:T(8,128)}), f32[256,64]{0,1:T(8,128)}) %reduce-scatter.2.cloned.1.call-update) | async-done | bytes 65552 | tf_op jit(solution)/shard_map/reduce_scatter | solution.py:127
  (119 shorter events, 115.6 us)
Async XLA Ops:
  6.5 245.2 %copy-start = (s32[2048]{0:T(1024)S(1)}, s32[2048]{0:T(1024)}, u32[]{:S(2)}) copy-start(s32[2048]{0:T(1024)} %param.8) | copy-start | bytes 24580
  6.7 2.8 copy-start.1
  211.7 1.9 copy-start.2
  213.5 1.1 copy-start.4
  292.6 67.4 %all-to-all-start = ((bf16[2,32,8,3072]{3,0,2,1:T(2,128)(2,1)}), bf16[2,32,8,3072]{3,0,2,1:T(2,128)(2,1)S(1)}, u32[]{:S(2)}, u32[]{:S(2)}) async-start(bf16[2,32,8,3072]{3,0,2,1:T(2,128)(2,1)} %bitcast.69), calls=%async_computation | async-start | bytes 6291456 | tf_op jit(solution)/shard_map/all_to_all | solution.py:116
  298.8 198.3 %reduce-scatter.2.cloned.1.call-start = ((), (), s32[]{:S(2)}) async-start(), calls=%async_computation.2 | async-start | bytes 589824 | tf_op jit(solution)/shard_map/reduce_scatter | solution.py:127
  367.9 1.0 copy-start.3
Sparse Core Ops, SparseCore 0:
  456.5 40.4 reduce-scatter.1
where the time goes:
time: 506 us; the launch traced here: 504 us
  other arithmetic  225 us (44%)
  waiting for transfers between devices  102 us (20%)
  matrix products  62.1 us (12%)
  local copies, waits for them, and re-layouts  52.5 us (10%)
  blocking collectives  36.9 us (7%)
  between operations  13.6 us (3%)
  starting transfers between devices  6.36 us (1%)
  loops' own time  5.98 us (1%)
    another operation x13, other arithmetic  163 us
    all_to_all x1, waiting for transfers between devices, on_device(): lax.all_to_all(spectra[:, send_rows], 'pairs', split_axis=1, concat_axis=...  61 us
    cos x8, other arithmetic, lag_block(): lag_table = jnp.concatenate([jnp.cos(angles), -jnp.sin(angles)], axis=1)  51.4 us
    reduce_scatter x1, waiting for transfers between devices, on_device(): lax.psum_scatter(lag_rows(stacked, lax.axis_size('tm') * lag_share, block...  40.6 us
    dot_general x12, matrix products, add_block(): jnp.dot(segment, cos_table, preferred_element_type=jnp.float32)  38.1 us
    all_gather x1, blocking collectives, on_device(): every_pair = lax.all_gather(pair_stations, 'pairs', axis=0, tiled=True)  36.9 us
    dot_general x8, matrix products, lag_block(): lax.dot_general(lag_table, stacked, (((1,), (1,)), ((), ())), precision=l...  23.9 us
    gather x1, local copies, waits for them, and re-layouts, on_device(): slot_ids = station_slot[every_pair.reshape(blocks, 2 * pair_count)]  23 us
  transfers between devices with their start and end apart: 2, of which 2 were waited for; matrix products, arithmetic and copies ran while one was open for 0% of the time, Pallas kernels for 0%

commit v1 on v0

v1 whole, which is shorter than its diff:
```python
import functools
import math

import jax
import jax.numpy as jnp
import ml_dtypes
import numpy as np
from jax import lax
from jax.experimental import pallas as pl
from jax.experimental.pallas import tpu as pltpu
from jax.sharding import PartitionSpec as P

F = 1536
FLO = 32
LAG = 1024
NS = 6144
RADIX = 12
SUB = NS // RADIX
DBINS = F // RADIX
STEPS = RADIX // 2
CAP = 8
ROOT3_2 = math.sqrt(3.0) / 2.0

TURNS = [0, 6] + [turn for step in range(1, STEPS) for turn in (step, RADIX - step)]
RESIDUES = [(turn - FLO) % RADIX for turn in TURNS]


def spectrum_tables():
    sub_times = np.arange(SUB, dtype=np.int64)[:, None]
    bins = np.arange(DBINS, dtype=np.int64)[None, :]
    tables = np.zeros((STEPS, 2 * SUB, 4 * DBINS), np.float64)
    for position, residue in enumerate(RESIDUES):
        step, half = divmod(position, 2)
        phases = sub_times * (FLO + residue + RADIX * bins) % NS
        angles = phases * (2.0 * np.pi / NS)
        cos_part, sin_part = np.cos(angles), np.sin(angles)
        columns = slice(half * 2 * DBINS, half * 2 * DBINS + DBINS)
        columns_imag = slice(half * 2 * DBINS + DBINS, (half + 1) * 2 * DBINS)
        if step == 0:
            rows = slice(half * SUB, (half + 1) * SUB)
            tables[step, rows, columns] = cos_part
            tables[step, rows, columns_imag] = -sin_part
        else:
            sign = 1.0 if half == 0 else -1.0
            tables[step, :SUB, columns] = cos_part
            tables[step, SUB:, columns] = sign * sin_part
            tables[step, :SUB, columns_imag] = -sin_part
            tables[step, SUB:, columns_imag] = sign * cos_part
    return tables.astype(ml_dtypes.bfloat16)


def hann_window():
    times = np.arange(NS, dtype=np.float64)
    return (0.5 - 0.5 * np.cos((times + 0.5) * (2.0 * np.pi / NS))).astype(np.float32)[None, :]


def lag_tables(normalizer):
    bins = np.arange(DBINS, dtype=np.int64)[:, None]
    sub_lags = np.arange(SUB, dtype=np.int64)[None, :]
    angles = (bins * sub_lags % SUB) * (2.0 * np.pi / SUB)
    cos_part, sin_part = np.cos(angles), np.sin(angles)
    inner = np.block([[cos_part, sin_part], [-sin_part, cos_part]]).astype(ml_dtypes.bfloat16)
    lags = np.arange(2 * LAG, dtype=np.int64)[None, :] - LAG
    first_bins = FLO + np.array(RESIDUES, dtype=np.int64)[:, None]
    outer_angles = (first_bins * lags % NS) * (2.0 * np.pi / NS)
    outer = np.stack([np.cos(outer_angles), -np.sin(outer_angles)], axis=1) * normalizer
    return inner, outer.reshape(2 * RADIX, 2 * LAG).astype(np.float32)


def request_kernel(slots_ref, pairs_ref, wanted_ref, places_ref):
    ends = 2 * pairs_ref.shape[1]
    rows = slots_ref.shape[0]
    windows = wanted_ref.shape[1] // CAP
    stations = wanted_ref.shape[2] // windows
    owners_count = wanted_ref.shape[0]
    sublane = lax.broadcasted_iota(jnp.int32, (ends, ends), 0)
    lane = lax.broadcasted_iota(jnp.int32, (ends, ends), 1)
    end_row = jnp.concatenate([pairs_ref[0:1, :], pairs_ref[1:2, :]], axis=1)
    end_column = jnp.sum(
        jnp.where(sublane == lane, jnp.broadcast_to(end_row, (ends, ends)), 0).astype(jnp.float32),
        axis=1,
        keepdims=True,
    ).astype(jnp.int32)
    lanes = lax.broadcasted_iota(jnp.int32, (ends, 128), 1)
    found = jnp.zeros((ends, 128), jnp.int32)
    for row in range(rows):
        slot_row = slots_ref[row : row + 1, :]
        found = found + jnp.where(end_column == lanes + row * 128, slot_row, 0)
    slot_column = jnp.sum(found.astype(jnp.float32), axis=1, keepdims=True).astype(jnp.int32)
    slot_square = jnp.broadcast_to(slot_column, (ends, ends))
    slot_row = jnp.sum(jnp.where(sublane == lane, slot_square, 0).astype(jnp.float32), axis=0, keepdims=True).astype(
        jnp.int32
    )
    owner_column = slot_column // stations
    owner_row = slot_row // stations
    local_row = slot_row - owner_row * stations
    same_owner = owner_column == owner_row
    rank_row = jnp.sum(
        jnp.where(same_owner & (sublane < lane), 1.0, 0.0), axis=0, keepdims=True
    ).astype(jnp.int32)
    rank_column = jnp.sum(
        jnp.where(same_owner & (lane < sublane), 1.0, 0.0), axis=1, keepdims=True
    ).astype(jnp.int32)
    places_ref[...] = jnp.broadcast_to(owner_column * (windows * CAP) + rank_column, places_ref.shape)
    owner_ids = lax.broadcasted_iota(jnp.int32, (owners_count, ends), 0)
    owned = owner_ids == owner_row
    column_ids = lax.broadcasted_iota(jnp.int32, (owners_count, windows * stations), 1)
    for rank in range(CAP):
        hit = owned & (rank_row == rank)
        row_wanted = jnp.sum(
            jnp.where(hit, local_row, 0).astype(jnp.float32), axis=1, keepdims=True
        ).astype(jnp.int32)
        for window in range(windows):
            picked = jnp.where(column_ids == row_wanted + window * stations, 1.0, 0.0)
            wanted_ref[:, window * CAP + rank, :] = picked


def requests(station_slot, pair_stations, blocks, windows, stations):
    pair_count = pair_stations.shape[0]
    return pl.pallas_call(
        request_kernel,
        out_shape=(
            jax.ShapeDtypeStruct((blocks, windows * CAP, windows * stations), jnp.float32),
            jax.ShapeDtypeStruct((2 * pair_count, 128), jnp.int32),
        ),
        name="requests",
    )(station_slot.reshape(-1, 128), pair_stations.T)


def spectrum_kernel(traces_ref, hann_ref, table_ref, out_ref, parts_ref, spectrum_ref):
    step = pl.program_id(0)
    row_count = traces_ref.shape[0]

    @pl.when(step == 0)
    def _():
        def one_group(group, carry):
            rows = pl.ds(pl.multiple_of(group * 16, 16), 16)
            partial_sum = traces_ref[rows, 0:128]
            for tile in range(1, NS // 128):
                partial_sum = partial_sum + traces_ref[rows, tile * 128 : (tile + 1) * 128]
            mean = jnp.sum(partial_sum, axis=1, keepdims=True) * (1.0 / NS)
            for tile in range(SUB // 128):
                x = []
                for block in range(RADIX):
                    columns = slice(block * SUB + tile * 128, block * SUB + (tile + 1) * 128)
                    x.append((traces_ref[rows, columns] - mean) * hann_ref[:, columns])
                u = [None] + [x[a] + x[RADIX - a] for a in range(1, 6)]
                v = [None] + [x[a] - x[RADIX - a] for a in range(1, 6)]
                e0, o0 = x[0] + x[6], x[0] - x[6]
                p, q = u[1] + u[5], u[2] + u[4]
                pd, qd = u[1] - u[5], u[2] - u[4]
                m, n = v[1] - v[5], v[2] - v[4]
                ms, ns = v[1] + v[5], v[2] + v[4]
                half_pq, half_diff = 0.5 * (p + q), 0.5 * (p - q)
                e_plus, e_minus = e0 + u[3], e0 - u[3]
                base = o0 + 0.5 * qd
                side = ROOT3_2 * pd
                imag_base = 0.5 * ms + v[3]
                imag_side = ROOT3_2 * ns
                parts = [
                    (e_plus + (p + q), e_minus - (p - q)),
                    (base + side, -(imag_base + imag_side)),
                    (e_minus + half_diff, -ROOT3_2 * (m + n)),
                    (o0 - qd, v[3] - ms),
                    (e_plus - half_pq, -ROOT3_2 * (m - n)),
                    (base - side, imag_side - imag_base),
                ]
                for index, (first, second) in enumerate(parts):
                    start = index * 2 * SUB + tile * 128
                    parts_ref[rows, start : start + 128] = first.astype(jnp.bfloat16)
                    parts_ref[rows, start + SUB : start + SUB + 128] = second.astype(jnp.bfloat16)
            return carry

        lax.fori_loop(0, row_count // 16, one_group, 0)

    for index in range(STEPS):

        @pl.when(step == index)
        def _(index=index):
            spectrum_ref[:, index * 512 : (index + 1) * 512] = jnp.dot(
                parts_ref[:, index * 1024 : (index + 1) * 1024],
                table_ref[0],
                preferred_element_type=jnp.float32,
            )

    @pl.when(step == STEPS - 1)
    def _():
        def one_group(group, carry):
            rows = pl.ds(pl.multiple_of(group * 16, 16), 16)
            total = jnp.zeros((16, 128), jnp.float32)
            for residue in range(RADIX):
                real_part = spectrum_ref[rows, residue * 256 : residue * 256 + 128]
                imag_part = spectrum_ref[rows, residue * 256 + 128 : residue * 256 + 256]
                total = total + (real_part * real_part + imag_part * imag_part)
            water_level = jnp.sum(total, axis=1, keepdims=True) * (1.0 / F)
            floor = 0.1 * water_level + 1e-06
            for residue in range(RADIX):
                real_part = spectrum_ref[rows, residue * 256 : residue * 256 + 128]
                imag_part = spectrum_ref[rows, residue * 256 + 128 : residue * 256 + 256]
                energy = real_part * real_part + imag_part * imag_part
                scaling = lax.rsqrt(energy + floor)
                out_ref[rows, residue * 256 : residue * 256 + 128] = (real_part * scaling).astype(jnp.bfloat16)
                out_ref[rows, residue * 256 + 128 : residue * 256 + 256] = (imag_part * scaling).astype(jnp.bfloat16)
            return carry

        lax.fori_loop(0, row_count // 16, one_group, 0)


def whitened_spectra(traces):
    rows = traces.shape[0]
    return pl.pallas_call(
        spectrum_kernel,
        out_shape=jax.ShapeDtypeStruct((rows, 2 * F), jnp.bfloat16),
        grid_spec=pltpu.PrefetchScalarGridSpec(
            num_scalar_prefetch=0,
            grid=(STEPS,),
            in_specs=[
                pl.BlockSpec((rows, NS), lambda s: (0, 0)),
                pl.BlockSpec((1, NS), lambda s: (0, 0)),
                pl.BlockSpec((1, 2 * SUB, 4 * DBINS), lambda s: (s, 0, 0)),
            ],
            out_specs=pl.BlockSpec((rows, 2 * F), lambda s: (0, 0)),
            scratch_shapes=[
                pltpu.VMEM((rows, NS), jnp.bfloat16),
                pltpu.VMEM((rows, 2 * F), jnp.float32),
            ],
        ),
        compiler_params=pltpu.CompilerParams(
            dimension_semantics=("arbitrary",), vmem_limit_bytes=48 << 20
        ),
        cost_estimate=pl.CostEstimate(
            flops=2 * rows * STEPS * 1024 * 512, bytes_accessed=11_000_000, transcendentals=rows * F
        ),
        name="whitened_spectra",
    )(traces, jnp.asarray(hann_window()), jnp.asarray(spectrum_tables()))


C_STEPS = 4
C_RES = RADIX // C_STEPS


def lag_kernel(places_ref, received_ref, inner_ref, outer_ref, out_ref, select_ref, sums_ref):
    step = pl.program_id(0)
    slots = received_ref.shape[0]
    ends = places_ref.shape[0]
    pairs = ends // 2
    windows = select_ref.shape[0] // ends

    @pl.when(step == 0)
    def _():
        lanes = lax.broadcasted_iota(jnp.int32, (ends, 128), 1)
        places = places_ref[...]
        for window in range(windows):
            for tile in range(slots // 128):
                hit = jnp.where(places + window * CAP == lanes + tile * 128, 1.0, 0.0)
                select_ref[window * ends : (window + 1) * ends, tile * 128 : (tile + 1) * 128] = hit.astype(
                    jnp.bfloat16
                )
        sums_ref[...] = jnp.zeros_like(sums_ref)

    picked = jnp.dot(select_ref[...], received_ref[...], preferred_element_type=jnp.float32)
    stacked = []
    for index in range(C_RES):
        real_sum = imag_sum = None
        for window in range(windows):
            left = slice(window * ends, window * ends + pairs)
            right = slice(window * ends + pairs, (window + 1) * ends)
            left_real = picked[left, index * 256 : index * 256 + 128]
            left_imag = picked[left, index * 256 + 128 : index * 256 + 256]
            right_real = picked[right, index * 256 : index * 256 + 128]
            right_imag = picked[right, index * 256 + 128 : index * 256 + 256]
            real_term = left_real * right_real + left_imag * right_imag
            imag_term = left_imag * right_real - left_real * right_imag
            real_sum = real_term if real_sum is None else real_sum + real_term
            imag_sum = imag_term if imag_sum is None else imag_sum + imag_term
        stacked.append(jnp.concatenate([real_sum, imag_sum], axis=1))
    stacked = jnp.concatenate(stacked, axis=0).astype(jnp.bfloat16)
    turned = jnp.dot(stacked, inner_ref[...], preferred_element_type=jnp.float32)
    outer = outer_ref[0]
    for period in range(2 * LAG // SUB):
        for tile in range(SUB // 128):
            lag_columns = slice(period * SUB + tile * 128, period * SUB + (tile + 1) * 128)
            total = sums_ref[:, lag_columns]
            for index in range(C_RES):
                rows = slice(index * pairs, (index + 1) * pairs)
                total = total + outer[2 * index : 2 * index + 1, lag_columns] * turned[rows, tile * 128 : (tile + 1) * 128]
                total = total + outer[2 * index + 1 : 2 * index + 2, lag_columns] * turned[
                    rows, SUB + tile * 128 : SUB + (tile + 1) * 128
                ]
            sums_ref[:, lag_columns] = total

    @pl.when(step == C_STEPS - 1)
    def _():
        share = out_ref.shape[2]
        for part in range(out_ref.shape[0]):
            out_ref[part] = sums_ref[:, part * share : (part + 1) * share].astype(out_ref.dtype)


def lag_sums(places, received, parts, normalizer):
    ends = places.shape[0]
    slots = received.shape[0]
    pairs = ends // 2
    windows = slots // (32 * CAP)
    inner, outer = lag_tables(normalizer)
    return pl.pallas_call(
        lag_kernel,
        out_shape=jax.ShapeDtypeStruct((parts, pairs, 2 * LAG // parts), jnp.bfloat16),
        grid_spec=pltpu.PrefetchScalarGridSpec(
            num_scalar_prefetch=0,
            grid=(C_STEPS,),
            in_specs=[
                pl.BlockSpec((ends, 128), lambda s: (0, 0)),
                pl.BlockSpec((slots, 256 * C_RES), lambda s: (0, s)),
                pl.BlockSpec((2 * DBINS, 2 * SUB), lambda s: (0, 0)),
                pl.BlockSpec((1, 2 * C_RES, 2 * LAG), lambda s: (s, 0, 0)),
            ],
            out_specs=pl.BlockSpec((parts, pairs, 2 * LAG // parts), lambda s: (0, 0, 0)),
            scratch_shapes=[
                pltpu.VMEM((windows * ends, slots), jnp.bfloat16),
                pltpu.VMEM((pairs, 2 * LAG), jnp.float32),
            ],
        ),
        compiler_params=pltpu.CompilerParams(
            dimension_semantics=("arbitrary",), vmem_limit_bytes=48 << 20
        ),
        cost_estimate=pl.CostEstimate(
            flops=2 * windows * ends * slots * 2 * F, bytes_accessed=5_000_000, transcendentals=0
        ),
        name="lag_sums",
    )(places, received, jnp.asarray(inner), jnp.asarray(outer.reshape(C_STEPS, 2 * C_RES, 2 * LAG)))


def total_kernel(parts_ref, out_ref):
    total = parts_ref[0].astype(jnp.float32)
    for part in range(1, parts_ref.shape[0]):
        total = total + parts_ref[part].astype(jnp.float32)
    out_ref[...] = total


def window_total(parts):
    return pl.pallas_call(
        total_kernel,
        out_shape=jax.ShapeDtypeStruct(parts.shape[1:], jnp.float32),
        name="window_total",
    )(parts).T


def on_device(traces, station_slot, pair_stations):
    window_count, station_count, length = traces.shape
    blocks = lax.axis_size("pairs")
    lag_parts = lax.axis_size("tm")
    normalizer = 1.0 / math.sqrt(F * window_count * lag_parts)
    wanted, places = requests(station_slot, pair_stations, blocks, window_count, station_count)
    picks = lax.all_to_all(wanted.astype(jnp.bfloat16), "pairs", split_axis=0, concat_axis=0, tiled=True)
    whitened = whitened_spectra(traces.reshape(window_count * station_count, length))
    rows = jnp.dot(
        picks.reshape(blocks * window_count * CAP, window_count * station_count),
        whitened,
        preferred_element_type=jnp.bfloat16,
    )
    received = lax.all_to_all(
        rows.reshape(blocks, window_count * CAP, 2 * F), "pairs", split_axis=0, concat_axis=0, tiled=True
    )
    sums = lag_sums(places, received.reshape(blocks * window_count * CAP, 2 * F), lag_parts, normalizer)
    parts = lax.all_to_all(sums, "tm", split_axis=0, concat_axis=0, tiled=True)
    return window_total(parts)


def solution(mesh):
    in_specs = (P("tm", "pairs", None), P(), P("pairs", None))
    out_specs = P("tm", "pairs")
    return jax.shard_map(
        on_device, mesh=mesh, in_specs=in_specs, out_specs=out_specs, check_vma=False
    )
```

time: 506 us -> 128 us (0.25)
  other arithmetic: 225 us -> 1.62 us
  waiting for transfers between devices: 102 us -> 0.01 us
  matrix products: 62.1 us -> 0.97 us
  blocking collectives: 36.9 us -> 94.7 us
  local copies, waits for them, and re-layouts: 52.5 us -> 2.64 us
  Pallas kernels: 0 us -> 15.1 us
  between operations: 13.6 us -> 0.08 us
  loops' own time: 5.98 us -> 0 us
  starting transfers between devices: 6.36 us -> 11.9 us
    another operation x14 -> x0, other arithmetic: 166 us -> none
    all_to_all x0 -> x2, blocking collectives: none -> 94.7 us  [the longest x1 78.8 us: on_device(): lax.all_to_all(rows.reshape(blocks, window_count * CAP, 2 * F), 'pairs',...]
    dot_general x20 -> x1, matrix products: 62.1 us -> 0.97 us  [on_device(): jnp.dot(picks.reshape(blocks * window_count * CAP, window_count * station...]
    all_to_all x1, waiting for transfers between devices: 61 us -> 0.01 us  [on_device(): lax.all_to_all(wanted.astype(jnp.bfloat16), 'pairs', split_axis=0, concat...]
    cos x8 -> x0, other arithmetic: 51.4 us -> none  [lag_block(): lag_table = jnp.concatenate([jnp.cos(angles), -jnp.sin(angles)], axis=1)]
    gather x3 -> x0, local copies, waits for them, and re-layouts: 40.7 us -> none  [the longest x1 23 us: on_device(): slot_ids = station_slot[every_pair.reshape(blocks, 2 * pair_count)]]
    reduce_scatter x1 -> x0, waiting for transfers between devices: 40.6 us -> none  [on_device(): lax.psum_scatter(lag_rows(stacked, lax.axis_size('tm') * lag_share, block...]
    all_gather x1 -> x0, blocking collectives: 36.9 us -> none  [on_device(): every_pair = lax.all_gather(pair_stations, 'pairs', axis=0, tiled=True)]
  transfers between devices with their start and end apart: 2 -> 1, of which waited for: 2 -> 0; matrix products, arithmetic and copies ran while one was open for 0% -> 0% of each run, Pallas kernels for 0% -> 6%
where the time goes in v1:
time: 128 us; the launch traced here: 127 us
  blocking collectives  94.7 us (74%)
  Pallas kernels  15.1 us (12%)
  starting transfers between devices  11.9 us (9%)
  local copies, waits for them, and re-layouts  2.64 us (2%)
  other arithmetic  1.62 us (1%)
    all_to_all x1, blocking collectives, on_device(): lax.all_to_all(rows.reshape(blocks, window_count * CAP, 2 * F), 'pairs',...  78.8 us
    all_to_all x1, blocking collectives, on_device(): parts = lax.all_to_all(sums, 'tm', split_axis=0, concat_axis=0, tiled=True)  16 us
    all_to_all x1, starting transfers between devices, on_device(): lax.all_to_all(wanted.astype(jnp.bfloat16), 'pairs', split_axis=0, concat...  11.9 us
    pallas_call x1, Pallas kernels, whitened_spectra(): pl.pallas_call(spectrum_kernel, out_shape=jax.ShapeDtypeStruct((rows, 2 *...  7.93 us
    pallas_call x1, Pallas kernels, lag_sums(): pl.pallas_call(lag_kernel, out_shape=jax.ShapeDtypeStruct((parts, pairs,...  3.5 us
    unnamed x10, local copies, waits for them, and re-layouts  2.64 us
  transfers between devices with their start and end apart: 1, of which 0 were waited for; matrix products, arithmetic and copies ran while one was open for 0% of the time, Pallas kernels for 6%

profile of v1, /device:TPU:1, one launch (start us, length us, event | category | flops | bytes accessed | tf_op | source)
XLA Modules:
  0.0 127.0 jit_solution(11127348196248513713)
XLA Ops:
  0.0 2.1 %requests.1 = (f32[32,16,128]{2,1,0:T(8,128)}, s32[128,128]{1,0:T(8,128)}) custom-call(s32[16,128]{1,0:T(8,128)} %bitcast.11, s32[2,64]{1,0:T(2,128)} %bitcast.12), custom_call_target="tpu_custom_call" | custom-call | tf_op jit(solution)/shard_map/requests/pallas_call | solution.py:120
  2.1 1.6 %convert_element_type.3 = bf16[32,16,128]{2,1,0:T(8,128)(2,1)} convert(f32[32,16,128]{2,1,0:T(8,128)} %get-tuple-element.8) | non-fusion elementwise | flops 65536 | bytes 393216 | tf_op jit(solution)/shard_map/convert_element_type | solution.py:354
  3.7 11.9 %all-to-all-start = ((bf16[32,16,128]{2,1,0:T(8,128)(2,1)}), bf16[32,16,128]{2,1,0:T(8,128)(2,1)S(1)}, u32[]{:S(2)}, u32[]{:S(2)}) async-start(bf16[32,16,128]{2,1,0:T(8,128)(2,1)} %convert_element_type.3), calls=%async_computation | async-start | bytes 262144 | tf_op jit(solution)/shard_map/all_to_all | solution.py:354
  15.6 0.0 copy-start
  15.6 1.9 %copy-done = f32[2,64,6144]{2,1,0:T(8,128)S(1)} copy-done((f32[2,64,6144]{2,1,0:T(8,128)S(1)}, f32[2,64,6144]{2,1,0:T(8,128)}, u32[]{:S(2)}) %copy-start) | copy-done | bytes 3145752
  17.5 0.0 copy-start.4
  17.5 0.7 copy-done.4
  18.2 7.9 %whitened_spectra.1 = bf16[128,3072]{1,0:T(8,128)(2,1)S(1)} custom-call(f32[128,6144]{1,0:T(8,128)S(1)} %bitcast.10, f32[1,6144]{1,0:T(1,128)S(1)} %copy-done.4, bf16[6,1024,512]{2,1,0:T(8,128)(2,1)} %constant.9.clone.table_ref), custom_call_target="tpu_custom_call" | custom-call | flops 805306368 | bytes 11000000 | tf_op jit(solution)/shard_map/whitened_spectra/pallas_call | solution.py:211
  26.1 0.0 all-to-all-done
  26.1 1.0 fusion
  27.1 0.0 copy-start.1
  27.1 0.0 copy-start.2
  27.1 0.0 copy-start.3
  27.2 78.8 %all_to_all.15 = bf16[32,16,3072]{2,1,0:T(8,128)(2,1)S(1)} all-to-all(bf16[32,16,3072]{2,1,0:T(8,128)(2,1)S(1)} %fusion), channel_id=1, replica_groups=mesh['pairs'=32,'tm'=8] {'pairs'}, dimensions={0} | all-to-all | bytes 6291456 | tf_op jit(solution)/shard_map/all_to_all | solution.py:361
  105.9 0.0 copy-done.1
  105.9 0.0 copy-done.2
  105.9 0.0 copy-done.3
  105.9 3.5 %lag_sums.1 = bf16[8,64,256]{2,1,0:T(8,128)(2,1)S(1)} custom-call(s32[128,128]{1,0:T(8,128)S(1)} %copy-done.3, bf16[512,3072]{1,0:T(8,128)(2,1)S(1)} %bitcast.9, bf16[256,1024]{1,0:T(8,128)(2,1)S(1)} %copy-done.1, f32[4,6,2048]{2,1,0:T(8,128)S(1)} %copy-done.2), custom_call_target="tpu_custom_call" | custom-call | flops 805306368 | bytes 5000000 | tf_op jit(solution)/shard_map/lag_sums/pallas_call | solution.py:305
  109.4 16.0 %all_to_all.16.parts_ref = bf16[8,64,256]{2,1,0:T(8,128)(2,1)} all-to-all(bf16[8,64,256]{2,1,0:T(8,128)(2,1)S(1)} %lag_sums.1), channel_id=1, replica_groups=mesh['pairs'=32,'tm'=8] {'tm'}, dimensions={0} | all-to-all | bytes 524288 | tf_op jit(solution)/shard_map/all_to_all | solution.py:365
  125.4 1.6 %window_total.1 = f32[64,256]{1,0:T(8,128)} custom-call(bf16[8,64,256]{2,1,0:T(8,128)(2,1)} %all_to_all.16.parts_ref), custom_call_target="tpu_custom_call" | custom-call | tf_op jit(solution)/shard_map/window_total/pallas_call | solution.py:341
Async XLA Ops:
  3.7 22.4 %all-to-all-start = ((bf16[32,16,128]{2,1,0:T(8,128)(2,1)}), bf16[32,16,128]{2,1,0:T(8,128)(2,1)S(1)}, u32[]{:S(2)}, u32[]{:S(2)}) async-start(bf16[32,16,128]{2,1,0:T(8,128)(2,1)} %convert_element_type.3), calls=%async_computation | async-start | bytes 262144 | tf_op jit(solution)/shard_map/all_to_all | solution.py:354
  15.6 1.9 %copy-start = (f32[2,64,6144]{2,1,0:T(8,128)S(1)}, f32[2,64,6144]{2,1,0:T(8,128)}, u32[]{:S(2)}) copy-start(f32[2,64,6144]{2,1,0:T(8,128)} %param.7) | copy-start | bytes 9437188
  17.5 0.7 copy-start.4
  27.1 78.8 %copy-start.1 = (bf16[256,1024]{1,0:T(8,128)(2,1)S(1)}, bf16[256,1024]{1,0:T(8,128)(2,1)}, u32[]{:S(2)}) copy-start(bf16[256,1024]{1,0:T(8,128)(2,1)} %constant.10.clone.inner_ref) | copy-start | bytes 1572868
  27.1 78.8 %copy-start.2 = (f32[4,6,2048]{2,1,0:T(8,128)S(1)}, f32[4,6,2048]{2,1,0:T(8,128)}, u32[]{:S(2)}) copy-start(f32[4,6,2048]{2,1,0:T(8,128)} %constant.11.clone.outer_ref) | copy-start | bytes 589828
  27.1 78.8 %copy-start.3 = (s32[128,128]{1,0:T(8,128)S(1)}, s32[128,128]{1,0:T(8,128)}, u32[]{:S(2)}) copy-start(s32[128,128]{1,0:T(8,128)} %get-tuple-element.7.places_ref) | copy-start | bytes 196612

commit v2 on v1

v2 whole, which is shorter than its diff:
```python
import math

import jax
import jax.numpy as jnp
import ml_dtypes
import numpy as np
from jax import lax
from jax.experimental import pallas as pl
from jax.experimental.pallas import tpu as pltpu
from jax.sharding import PartitionSpec as P

F = 1536
FLO = 32
LAG = 1024
NS = 6144
RADIX = 12
SUB = NS // RADIX
DBINS = F // RADIX
STEPS = RADIX // 2
CAP = 8
ROOT3_2 = math.sqrt(3.0) / 2.0

TURNS = [0, 6] + [turn for step in range(1, STEPS) for turn in (step, RADIX - step)]
RESIDUES = [(turn - FLO) % RADIX for turn in TURNS]


def spectrum_tables():
    sub_times = np.arange(SUB, dtype=np.int64)[:, None]
    bins = np.arange(DBINS, dtype=np.int64)[None, :]
    angles = (sub_times * bins % SUB) * (2.0 * np.pi / SUB)
    cos_part, sin_part = np.cos(angles), np.sin(angles)
    inner = np.block([[cos_part, -sin_part], [sin_part, cos_part]]).astype(ml_dtypes.bfloat16)
    first_bins = FLO + np.array(RESIDUES, dtype=np.int64)[:, None]
    turn_angles = (first_bins * sub_times[:, 0][None, :] % NS) * (2.0 * np.pi / NS)
    turns = np.stack([np.cos(turn_angles), np.sin(turn_angles)], axis=1)
    return inner, turns.reshape(2 * RADIX, SUB).astype(np.float32)


def hann_window():
    times = np.arange(NS, dtype=np.float64)
    return (0.5 - 0.5 * np.cos((times + 0.5) * (2.0 * np.pi / NS))).astype(np.float32)[None, :]


def lag_tables(normalizer):
    bins = np.arange(DBINS, dtype=np.int64)[:, None]
    sub_lags = np.arange(SUB, dtype=np.int64)[None, :]
    angles = (bins * sub_lags % SUB) * (2.0 * np.pi / SUB)
    cos_part, sin_part = np.cos(angles), np.sin(angles)
    inner = np.block([[cos_part, sin_part], [-sin_part, cos_part]]).astype(ml_dtypes.bfloat16)
    lags = np.arange(2 * LAG, dtype=np.int64)[None, :] - LAG
    first_bins = FLO + np.array(RESIDUES, dtype=np.int64)[:, None]
    outer_angles = (first_bins * lags % NS) * (2.0 * np.pi / NS)
    outer = np.stack([np.cos(outer_angles), -np.sin(outer_angles)], axis=1) * normalizer
    return inner, outer.reshape(2 * RADIX, 2 * LAG).astype(np.float32)


def request_kernel(slots_ref, pairs_ref, wanted_ref, places_ref):
    ends = 2 * pairs_ref.shape[1]
    windows = wanted_ref.shape[1] // CAP
    stations = wanted_ref.shape[2] // windows
    owners_count = wanted_ref.shape[0]
    sublane = lax.broadcasted_iota(jnp.int32, (ends, ends), 0)
    lane = lax.broadcasted_iota(jnp.int32, (ends, ends), 1)

    def to_column(row):
        square = jnp.broadcast_to(row, (ends, ends))
        return jnp.sum(jnp.where(sublane == lane, square, 0).astype(jnp.float32), axis=1, keepdims=True)

    end_row = jnp.concatenate([pairs_ref[0:1, :], pairs_ref[1:2, :]], axis=1)
    end_column = to_column(end_row).astype(jnp.int32)
    lanes = lax.broadcasted_iota(jnp.int32, (ends, 128), 1)
    found = jnp.zeros((ends, 128), jnp.int32)
    for row in range(slots_ref.shape[0]):
        found = found + jnp.where(end_column == lanes + row * 128, slots_ref[row : row + 1, :], 0)
    slot_column = jnp.sum(found.astype(jnp.float32), axis=1, keepdims=True).astype(jnp.int32)
    slot_square = jnp.broadcast_to(slot_column, (ends, ends))
    slot_row = jnp.sum(
        jnp.where(sublane == lane, slot_square, 0).astype(jnp.float32), axis=0, keepdims=True
    ).astype(jnp.int32)
    owner_column = slot_column // stations
    owner_row = slot_row // stations
    local_row = slot_row - owner_row * stations
    same_owner = owner_column == owner_row
    rank_row = jnp.sum(
        jnp.where(same_owner & (sublane < lane), 1.0, 0.0), axis=0, keepdims=True
    ).astype(jnp.int32)
    rank_column = jnp.sum(
        jnp.where(same_owner & (lane < sublane), 1.0, 0.0), axis=1, keepdims=True
    ).astype(jnp.int32)
    places_ref[...] = jnp.broadcast_to(owner_column * (windows * CAP) + rank_column, places_ref.shape)
    owned = lax.broadcasted_iota(jnp.int32, (owners_count, ends), 0) == owner_row
    column_ids = lax.broadcasted_iota(jnp.int32, (owners_count, 1, windows * stations), 2)
    picks = [[] for _ in range(windows)]
    for rank in range(CAP):
        hit = owned & (rank_row == rank)
        row_wanted = jnp.sum(
            jnp.where(hit, local_row, 0).astype(jnp.float32), axis=1, keepdims=True
        ).astype(jnp.int32)
        for window in range(windows):
            column = (row_wanted + window * stations)[:, :, None]
            picks[window].append(jnp.where(column_ids == column, 1.0, 0.0))
    wanted_ref[...] = jnp.concatenate(sum(picks, []), axis=1).astype(jnp.bfloat16)


def requests(station_slot, pair_stations, blocks, windows, stations):
    pair_count = pair_stations.shape[0]
    return pl.pallas_call(
        request_kernel,
        out_shape=(
            jax.ShapeDtypeStruct((blocks, windows * CAP, windows * stations), jnp.bfloat16),
            jax.ShapeDtypeStruct((2 * pair_count, 128), jnp.int32),
        ),
        name="requests",
    )(station_slot.reshape(-1, 128), pair_stations.T)


def spectrum_kernel(traces_ref, hann_ref, turns_ref, table_ref, out_ref, *scratch):
    count = len(scratch) // 2
    row_count = traces_ref.shape[0] // count
    tables = (hann_ref, turns_ref, table_ref)
    for part in range(count):
        transform_rows(part * row_count, row_count, traces_ref, *tables, out_ref, *scratch[2 * part : 2 * part + 2])


def transform_rows(
    base_row, row_count, traces_ref, hann_ref, turns_ref, table_ref, out_ref, parts_ref, spectrum_ref
):

    def one_group(group):
        first = group * 16
        rows = pl.ds(base_row + first, 16)
        partial_sum = traces_ref[rows, 0:128]
        for tile in range(1, NS // 128):
            partial_sum = partial_sum + traces_ref[rows, tile * 128 : (tile + 1) * 128]
        mean = jnp.sum(partial_sum, axis=1, keepdims=True) * (1.0 / NS)
        for tile in range(SUB // 128):
            x = []
            for block in range(RADIX):
                columns = slice(block * SUB + tile * 128, block * SUB + (tile + 1) * 128)
                x.append((traces_ref[rows, columns] - mean) * hann_ref[:, columns])
            u = [None] + [x[a] + x[RADIX - a] for a in range(1, 6)]
            v = [None] + [x[a] - x[RADIX - a] for a in range(1, 6)]
            e0, o0 = x[0] + x[6], x[0] - x[6]
            p, q = u[1] + u[5], u[2] + u[4]
            pd, qd = u[1] - u[5], u[2] - u[4]
            m, n = v[1] - v[5], v[2] - v[4]
            ms, ns = v[1] + v[5], v[2] + v[4]
            half_pq, half_diff = 0.5 * (p + q), 0.5 * (p - q)
            e_plus, e_minus = e0 + u[3], e0 - u[3]
            base = o0 + 0.5 * qd
            side = ROOT3_2 * pd
            imag_base = 0.5 * ms + v[3]
            imag_side = ROOT3_2 * ns
            real_parts = [
                e_plus + (p + q),
                base + side,
                e_minus + half_diff,
                o0 - qd,
                e_plus - half_pq,
                base - side,
                e_minus - (p - q),
            ]
            imag_parts = [
                None,
                -(imag_base + imag_side),
                -ROOT3_2 * (m + n),
                v[3] - ms,
                -ROOT3_2 * (m - n),
                imag_side - imag_base,
                None,
            ]
            lanes = slice(tile * 128, (tile + 1) * 128)
            imag_lanes = slice(SUB + tile * 128, SUB + (tile + 1) * 128)
            for position, turn in enumerate(TURNS):
                index = min(turn, RADIX - turn)
                real_part, imag_part = real_parts[index], imag_parts[index]
                cos_turn = turns_ref[2 * position : 2 * position + 1, lanes]
                sin_turn = turns_ref[2 * position + 1 : 2 * position + 2, lanes]
                if imag_part is None:
                    turned_real = real_part * cos_turn
                    turned_imag = -(real_part * sin_turn)
                elif index == turn:
                    turned_real = real_part * cos_turn + imag_part * sin_turn
                    turned_imag = imag_part * cos_turn - real_part * sin_turn
                else:
                    turned_real = real_part * cos_turn - imag_part * sin_turn
                    turned_imag = -(imag_part * cos_turn + real_part * sin_turn)
                target = pl.ds(position * row_count + first, 16)
                parts_ref[target, lanes] = turned_real.astype(jnp.bfloat16)
                parts_ref[target, imag_lanes] = turned_imag.astype(jnp.bfloat16)

    for group in range(row_count // 16):
        one_group(group)
    spectrum_ref[...] = jnp.dot(parts_ref[...], table_ref[...], preferred_element_type=jnp.float32)

    def whiten_group(group):
        first = group * 16
        rows = pl.ds(base_row + first, 16)
        total = jnp.zeros((16, DBINS), jnp.float32)
        for position in range(RADIX):
            source = pl.ds(position * row_count + first, 16)
            real_part, imag_part = spectrum_ref[source, :DBINS], spectrum_ref[source, DBINS:]
            total = total + (real_part * real_part + imag_part * imag_part)
        water_level = jnp.sum(total, axis=1, keepdims=True) * (1.0 / F)
        floor = 0.1 * water_level + 1e-06
        for position in range(RADIX):
            source = pl.ds(position * row_count + first, 16)
            real_part, imag_part = spectrum_ref[source, :DBINS], spectrum_ref[source, DBINS:]
            scaling = lax.rsqrt(real_part * real_part + imag_part * imag_part + floor)
            start = position * 2 * DBINS
            out_ref[rows, start : start + DBINS] = (real_part * scaling).astype(jnp.bfloat16)
            out_ref[rows, start + DBINS : start + 2 * DBINS] = (imag_part * scaling).astype(jnp.bfloat16)

    for group in range(row_count // 16):
        whiten_group(group)


PART_ROWS = 32
STEP_PARTS = 2


def whitened_spectra(traces):
    total = traces.shape[0]
    rows = PART_ROWS * STEP_PARTS
    table, turns = spectrum_tables()
    scratch = [
        pltpu.VMEM((RADIX * PART_ROWS, 2 * SUB), jnp.bfloat16),
        pltpu.VMEM((RADIX * PART_ROWS, 2 * DBINS), jnp.float32),
    ]
    return pl.pallas_call(
        spectrum_kernel,
        out_shape=jax.ShapeDtypeStruct((total, 2 * F), jnp.bfloat16),
        grid_spec=pltpu.PrefetchScalarGridSpec(
            num_scalar_prefetch=0,
            grid=(total // rows,),
            in_specs=[
                pl.BlockSpec((rows, NS), lambda s: (s, 0)),
                pl.BlockSpec((1, NS), lambda s: (0, 0)),
                pl.BlockSpec((2 * RADIX, SUB), lambda s: (0, 0)),
                pl.BlockSpec((2 * SUB, 2 * DBINS), lambda s: (0, 0)),
            ],
            out_specs=pl.BlockSpec((rows, 2 * F), lambda s: (s, 0)),
            scratch_shapes=scratch * STEP_PARTS,
        ),
        compiler_params=pltpu.CompilerParams(dimension_semantics=("arbitrary",)),
        cost_estimate=pl.CostEstimate(
            flops=2 * total * RADIX * 2 * SUB * 2 * DBINS,
            bytes_accessed=5_000_000,
            transcendentals=total * F,
        ),
        name="whitened_spectra",
    )(traces, jnp.asarray(hann_window()), jnp.asarray(turns), jnp.asarray(table))


C_STEPS = 4
C_RES = RADIX // C_STEPS


def lag_kernel(places_ref, received_ref, inner_ref, outer_ref, out_ref, select_ref, sums_ref):
    step = pl.program_id(0)
    slots = received_ref.shape[0]
    ends = places_ref.shape[0]
    pairs = ends // 2
    windows = select_ref.shape[0] // ends

    @pl.when(step == 0)
    def _():
        lanes = lax.broadcasted_iota(jnp.int32, (ends, 128), 1)
        places = places_ref[...]
        for window in range(windows):
            for tile in range(slots // 128):
                hit = jnp.where(places + window * CAP == lanes + tile * 128, 1.0, 0.0)
                select_ref[window * ends : (window + 1) * ends, tile * 128 : (tile + 1) * 128] = hit.astype(
                    jnp.bfloat16
                )
        sums_ref[...] = jnp.zeros_like(sums_ref)

    picked = jnp.dot(select_ref[...], received_ref[...], preferred_element_type=jnp.float32)
    stacked = []
    for index in range(C_RES):
        real_sum = imag_sum = None
        for window in range(windows):
            left = slice(window * ends, window * ends + pairs)
            right = slice(window * ends + pairs, (window + 1) * ends)
            left_real = picked[left, index * 256 : index * 256 + 128]
            left_imag = picked[left, index * 256 + 128 : index * 256 + 256]
            right_real = picked[right, index * 256 : index * 256 + 128]
            right_imag = picked[right, index * 256 + 128 : index * 256 + 256]
            real_term = left_real * right_real + left_imag * right_imag
            imag_term = left_imag * right_real - left_real * right_imag
            real_sum = real_term if real_sum is None else real_sum + real_term
            imag_sum = imag_term if imag_sum is None else imag_sum + imag_term
        stacked.append(jnp.concatenate([real_sum, imag_sum], axis=1))
    stacked = jnp.concatenate(stacked, axis=0).astype(jnp.bfloat16)
    turned = jnp.dot(stacked, inner_ref[...], preferred_element_type=jnp.float32)
    outer = outer_ref[0]
    for period in range(2 * LAG // SUB):
        for tile in range(SUB // 128):
            lag_columns = slice(period * SUB + tile * 128, period * SUB + (tile + 1) * 128)
            total = sums_ref[:, lag_columns]
            for index in range(C_RES):
                rows = slice(index * pairs, (index + 1) * pairs)
                total = total + outer[2 * index : 2 * index + 1, lag_columns] * turned[rows, tile * 128 : (tile + 1) * 128]
                total = total + outer[2 * index + 1 : 2 * index + 2, lag_columns] * turned[
                    rows, SUB + tile * 128 : SUB + (tile + 1) * 128
                ]
            sums_ref[:, lag_columns] = total

    @pl.when(step == C_STEPS - 1)
    def _():
        share = out_ref.shape[2]
        for part in range(out_ref.shape[0]):
            out_ref[part] = sums_ref[:, part * share : (part + 1) * share].astype(out_ref.dtype)


def lag_sums(places, received, parts, normalizer):
    ends = places.shape[0]
    slots = received.shape[0]
    pairs = ends // 2
    windows = slots // (32 * CAP)
    inner, outer = lag_tables(normalizer)
    return pl.pallas_call(
        lag_kernel,
        out_shape=jax.ShapeDtypeStruct((parts, pairs, 2 * LAG // parts), jnp.bfloat16),
        grid_spec=pltpu.PrefetchScalarGridSpec(
            num_scalar_prefetch=0,
            grid=(C_STEPS,),
            in_specs=[
                pl.BlockSpec((ends, 128), lambda s: (0, 0)),
                pl.BlockSpec((slots, 256 * C_RES), lambda s: (0, s)),
                pl.BlockSpec((2 * DBINS, 2 * SUB), lambda s: (0, 0)),
                pl.BlockSpec((1, 2 * C_RES, 2 * LAG), lambda s: (s, 0, 0)),
            ],
            out_specs=pl.BlockSpec((parts, pairs, 2 * LAG // parts), lambda s: (0, 0, 0)),
            scratch_shapes=[
                pltpu.VMEM((windows * ends, slots), jnp.bfloat16),
                pltpu.VMEM((pairs, 2 * LAG), jnp.float32),
            ],
        ),
        compiler_params=pltpu.CompilerParams(
            dimension_semantics=("arbitrary",), vmem_limit_bytes=32 << 20
        ),
        cost_estimate=pl.CostEstimate(
            flops=2 * windows * ends * slots * 2 * F, bytes_accessed=5_000_000, transcendentals=0
        ),
        name="lag_sums",
    )(places, received, jnp.asarray(inner), jnp.asarray(outer.reshape(C_STEPS, 2 * C_RES, 2 * LAG)))


def total_kernel(parts_ref, out_ref):
    total = parts_ref[0].astype(jnp.float32)
    for part in range(1, parts_ref.shape[0]):
        total = total + parts_ref[part].astype(jnp.float32)
    out_ref[...] = total


def window_total(parts):
    return pl.pallas_call(
        total_kernel,
        out_shape=jax.ShapeDtypeStruct(parts.shape[1:], jnp.float32),
        name="window_total",
    )(parts).T


def on_device(traces, station_slot, pair_stations):
    window_count, station_count, length = traces.shape
    blocks = lax.axis_size("pairs")
    lag_parts = lax.axis_size("tm")
    normalizer = 1.0 / math.sqrt(F * window_count * lag_parts)
    wanted, places = requests(station_slot, pair_stations, blocks, window_count, station_count)
    picks = lax.all_to_all(wanted, "pairs", split_axis=0, concat_axis=0, tiled=True)
    whitened = whitened_spectra(traces.reshape(window_count * station_count, length))
    rows = jnp.dot(
        picks.reshape(blocks * window_count * CAP, window_count * station_count),
        whitened,
        preferred_element_type=jnp.bfloat16,
    )
    received = lax.all_to_all(
        rows.reshape(blocks, window_count * CAP, 2 * F), "pairs", split_axis=0, concat_axis=0, tiled=True
    )
    sums = lag_sums(places, received.reshape(blocks * window_count * CAP, 2 * F), lag_parts, normalizer)
    parts = lax.all_to_all(sums, "tm", split_axis=0, concat_axis=0, tiled=True)
    return window_total(parts)


def solution(mesh):
    in_specs = (P("tm", "pairs", None), P(), P("pairs", None))
    out_specs = P("tm", "pairs")
    return jax.shard_map(
        on_device, mesh=mesh, in_specs=in_specs, out_specs=out_specs, check_vma=False
    )
```

time: 128 us -> 122 us (0.953)
  waiting for transfers between devices: 0.01 us -> 3.98 us
  blocking collectives: 94.7 us -> 90.8 us
  local copies, waits for them, and re-layouts: 2.64 us -> 0.02 us
  Pallas kernels: 15.1 us -> 12.5 us
  other arithmetic: 1.62 us -> 0 us
    all_to_all x1, waiting for transfers between devices: 0.01 us -> 3.98 us  [on_device(): lax.all_to_all(wanted, 'pairs', split_axis=0, concat_axis=0, tiled=True)]
    all_to_all x1, blocking collectives: 78.8 us -> 74.8 us  [on_device(): lax.all_to_all(rows.reshape(blocks, window_count * CAP, 2 * F), 'pairs',...]
    pallas_call x1, Pallas kernels: 7.93 us -> 5.17 us  [whitened_spectra(): pl.pallas_call(spectrum_kernel, out_shape=jax.ShapeDtypeStruct((total, 2...]
    unnamed x10 -> x6, local copies, waits for them, and re-layouts: 2.64 us -> 0.02 us
    convert_element_type x1 -> x0, other arithmetic: 1.62 us -> none  [on_device(): wanted.astype(jnp.bfloat16)]
  transfers between devices with their start and end apart: 1 -> 1, of which waited for: 0 -> 1; matrix products, arithmetic and copies ran while one was open for 0% -> 0% of each run, Pallas kernels for 6% -> 4%
where the time goes in v2:
time: 122 us; the launch traced here: 121 us
  blocking collectives  90.8 us (74%)
  Pallas kernels  12.5 us (10%)
  starting transfers between devices  11.9 us (10%)
  waiting for transfers between devices  3.98 us (3%)
  matrix products  2.1 us (2%)
    all_to_all x1, blocking collectives, on_device(): lax.all_to_all(rows.reshape(blocks, window_count * CAP, 2 * F), 'pairs',...  74.8 us
    all_to_all x1, blocking collectives, on_device(): parts = lax.all_to_all(sums, 'tm', split_axis=0, concat_axis=0, tiled=True)  16 us
    all_to_all x1, starting transfers between devices, on_device(): lax.all_to_all(wanted, 'pairs', split_axis=0, concat_axis=0, tiled=True)  11.9 us
    pallas_call x1, Pallas kernels, whitened_spectra(): pl.pallas_call(spectrum_kernel, out_shape=jax.ShapeDtypeStruct((total, 2...  5.17 us
    all_to_all x1, waiting for transfers between devices, on_device(): lax.all_to_all(wanted, 'pairs', split_axis=0, concat_axis=0, tiled=True)  3.98 us
    pallas_call x1, Pallas kernels, lag_sums(): pl.pallas_call(lag_kernel, out_shape=jax.ShapeDtypeStruct((parts, pairs,...  3.5 us
  transfers between devices with their start and end apart: 1, of which 1 were waited for; matrix products, arithmetic and copies ran while one was open for 0% of the time, Pallas kernels for 4%

profile of v2, /device:TPU:1, one launch (start us, length us, event | category | flops | bytes accessed | tf_op | source)
XLA Modules:
  0.0 121.2 jit_solution(15629521157126142626)
XLA Ops:
  0.0 2.2 %requests.1 = (bf16[32,16,128]{2,1,0:T(8,128)(2,1)}, s32[128,128]{1,0:T(8,128)}) custom-call(s32[16,128]{1,0:T(8,128)} %bitcast.11, s32[2,64]{1,0:T(2,128)} %bitcast.12), custom_call_target="tpu_custom_call" | custom-call | tf_op jit(solution)/shard_map/requests/pallas_call | solution.py:107
  2.2 11.9 %all-to-all-start = ((bf16[32,16,128]{2,1,0:T(8,128)(2,1)}), bf16[32,16,128]{2,1,0:T(8,128)(2,1)S(1)}, u32[]{:S(2)}, u32[]{:S(2)}) async-start(bf16[32,16,128]{2,1,0:T(8,128)(2,1)} %get-tuple-element.8), calls=%async_computation | async-start | bytes 262144 | tf_op jit(solution)/shard_map/all_to_all | solution.py:371
  14.0 5.2 %whitened_spectra.1 = bf16[128,3072]{1,0:T(8,128)(2,1)} custom-call(f32[128,6144]{1,0:T(8,128)} %bitcast.10, f32[1,6144]{1,0:T(1,128)} %constant.10.clone.hann_ref, f32[24,512]{1,0:T(8,128)} %constant.11.clone.turns_ref, bf16[1024,256]{1,0:T(8,128)(2,1)} %constant.12.clone.table_ref), custom_call_target="tpu_custom_call" | custom-call | flops 805306368 | bytes 5000000 | tf_op jit(solution)/shard_map/whitened_spectra/pallas_call | solution.py:230
  19.2 4.0 %all-to-all-done = bf16[32,16,128]{2,1,0:T(8,128)(2,1)S(1)} async-done(((bf16[32,16,128]{2,1,0:T(8,128)(2,1)}), bf16[32,16,128]{2,1,0:T(8,128)(2,1)S(1)}, u32[]{:S(2)}, u32[]{:S(2)}) %all-to-all-start) | async-done | bytes 131104 | tf_op jit(solution)/shard_map/all_to_all | solution.py:371
  23.2 2.1 %fusion = bf16[32,16,3072]{2,1,0:T(8,128)(2,1)S(1)} fusion(bf16[32,16,128]{2,1,0:T(8,128)(2,1)S(1)} %all-to-all-done, bf16[128,3072]{1,0:T(8,128)(2,1)} %whitened_spectra.1), kind=kOutput, calls=%fused_computation | convolution fusion | flops 402653184 | bytes 4063232 | tf_op jit(solution)/shard_map/dot_general | solution.py:373
  25.3 0.0 copy-start
  25.3 0.0 copy-start.1
  25.3 0.0 copy-start.2
  25.3 74.8 %all_to_all.15 = bf16[32,16,3072]{2,1,0:T(8,128)(2,1)S(1)} all-to-all(bf16[32,16,3072]{2,1,0:T(8,128)(2,1)S(1)} %fusion), channel_id=1, replica_groups=mesh['pairs'=32,'tm'=8] {'pairs'}, dimensions={0} | all-to-all | bytes 6291456 | tf_op jit(solution)/shard_map/all_to_all | solution.py:378
  100.1 0.0 copy-done
  100.1 0.0 copy-done.1
  100.1 0.0 copy-done.2
  100.1 3.5 %lag_sums.1 = bf16[8,64,256]{2,1,0:T(8,128)(2,1)S(1)} custom-call(s32[128,128]{1,0:T(8,128)S(1)} %copy-done.2, bf16[512,3072]{1,0:T(8,128)(2,1)S(1)} %bitcast.9, bf16[256,1024]{1,0:T(8,128)(2,1)S(1)} %copy-done, f32[4,6,2048]{2,1,0:T(8,128)S(1)} %copy-done.1), custom_call_target="tpu_custom_call" | custom-call | flops 805306368 | bytes 5000000 | tf_op jit(solution)/shard_map/lag_sums/pallas_call | solution.py:322
  103.6 16.0 %all_to_all.16.parts_ref = bf16[8,64,256]{2,1,0:T(8,128)(2,1)} all-to-all(bf16[8,64,256]{2,1,0:T(8,128)(2,1)S(1)} %lag_sums.1), channel_id=1, replica_groups=mesh['pairs'=32,'tm'=8] {'tm'}, dimensions={0} | all-to-all | bytes 524288 | tf_op jit(solution)/shard_map/all_to_all | solution.py:382
  119.6 1.6 %window_total.1 = f32[64,256]{1,0:T(8,128)} custom-call(bf16[8,64,256]{2,1,0:T(8,128)(2,1)} %all_to_all.16.parts_ref), custom_call_target="tpu_custom_call" | custom-call | tf_op jit(solution)/shard_map/window_total/pallas_call | solution.py:358
Async XLA Ops:
  2.2 21.0 %all-to-all-start = ((bf16[32,16,128]{2,1,0:T(8,128)(2,1)}), bf16[32,16,128]{2,1,0:T(8,128)(2,1)S(1)}, u32[]{:S(2)}, u32[]{:S(2)}) async-start(bf16[32,16,128]{2,1,0:T(8,128)(2,1)} %get-tuple-element.8), calls=%async_computation | async-start | bytes 262144 | tf_op jit(solution)/shard_map/all_to_all | solution.py:371
  25.3 74.8 %copy-start = (bf16[256,1024]{1,0:T(8,128)(2,1)S(1)}, bf16[256,1024]{1,0:T(8,128)(2,1)}, u32[]{:S(2)}) copy-start(bf16[256,1024]{1,0:T(8,128)(2,1)} %constant.13.clone.inner_ref) | copy-start | bytes 1572868
  25.3 74.8 %copy-start.1 = (f32[4,6,2048]{2,1,0:T(8,128)S(1)}, f32[4,6,2048]{2,1,0:T(8,128)}, u32[]{:S(2)}) copy-start(f32[4,6,2048]{2,1,0:T(8,128)} %constant.14.clone.outer_ref) | copy-start | bytes 589828
  25.3 74.8 %copy-start.2 = (s32[128,128]{1,0:T(8,128)S(1)}, s32[128,128]{1,0:T(8,128)}, u32[]{:S(2)}) copy-start(s32[128,128]{1,0:T(8,128)} %get-tuple-element.7.places_ref) | copy-start | bytes 196612

commit v3 on v2

--- a/solution.py
+++ b/solution.py
@@ -47,11 +47,10 @@
     angles = (bins * sub_lags % SUB) * (2.0 * np.pi / SUB)
     cos_part, sin_part = np.cos(angles), np.sin(angles)
     inner = np.block([[cos_part, sin_part], [-sin_part, cos_part]]).astype(ml_dtypes.bfloat16)
-    lags = np.arange(2 * LAG, dtype=np.int64)[None, :] - LAG
     first_bins = FLO + np.array(RESIDUES, dtype=np.int64)[:, None]
-    outer_angles = (first_bins * lags % NS) * (2.0 * np.pi / NS)
-    outer = np.stack([np.cos(outer_angles), -np.sin(outer_angles)], axis=1) * normalizer
-    return inner, outer.reshape(2 * RADIX, 2 * LAG).astype(np.float32)
+    outer_angles = (first_bins * sub_lags % NS) * (2.0 * np.pi / NS)
+    outer = np.stack([np.cos(outer_angles), np.sin(outer_angles)], axis=1) * normalizer
+    return inner, outer.reshape(2 * RADIX, SUB).astype(np.float32)
 
 
 def request_kernel(slots_ref, pairs_ref, wanted_ref, places_ref):
@@ -252,135 +251,167 @@
     )(traces, jnp.asarray(hann_window()), jnp.asarray(turns), jnp.asarray(table))
 
 
-C_STEPS = 4
-C_RES = RADIX // C_STEPS
-
-
-def lag_kernel(places_ref, received_ref, inner_ref, outer_ref, out_ref, select_ref, sums_ref):
-    step = pl.program_id(0)
+def lag_kernel(
+    place_ref, places_ref, received_ref, inner_ref, outer_ref, kept_ref, sent_ref,
+    select_ref, stacked_ref, turned_ref, sums_ref,
+):
     slots = received_ref.shape[0]
     ends = places_ref.shape[0]
     pairs = ends // 2
     windows = select_ref.shape[0] // ends
-
-    @pl.when(step == 0)
-    def _():
-        lanes = lax.broadcasted_iota(jnp.int32, (ends, 128), 1)
-        places = places_ref[...]
-        for window in range(windows):
-            for tile in range(slots // 128):
-                hit = jnp.where(places + window * CAP == lanes + tile * 128, 1.0, 0.0)
-                select_ref[window * ends : (window + 1) * ends, tile * 128 : (tile + 1) * 128] = hit.astype(
-                    jnp.bfloat16
-                )
-        sums_ref[...] = jnp.zeros_like(sums_ref)
-
-    picked = jnp.dot(select_ref[...], received_ref[...], preferred_element_type=jnp.float32)
-    stacked = []
-    for index in range(C_RES):
-        real_sum = imag_sum = None
-        for window in range(windows):
-            left = slice(window * ends, window * ends + pairs)
-            right = slice(window * ends + pairs, (window + 1) * ends)
-            left_real = picked[left, index * 256 : index * 256 + 128]
-            left_imag = picked[left, index * 256 + 128 : index * 256 + 256]
-            right_real = picked[right, index * 256 : index * 256 + 128]
-            right_imag = picked[right, index * 256 + 128 : index * 256 + 256]
-            real_term = left_real * right_real + left_imag * right_imag
-            imag_term = left_imag * right_real - left_real * right_imag
-            real_sum = real_term if real_sum is None else real_sum + real_term
-            imag_sum = imag_term if imag_sum is None else imag_sum + imag_term
-        stacked.append(jnp.concatenate([real_sum, imag_sum], axis=1))
-    stacked = jnp.concatenate(stacked, axis=0).astype(jnp.bfloat16)
-    turned = jnp.dot(stacked, inner_ref[...], preferred_element_type=jnp.float32)
-    outer = outer_ref[0]
-    for period in range(2 * LAG // SUB):
-        for tile in range(SUB // 128):
-            lag_columns = slice(period * SUB + tile * 128, period * SUB + (tile + 1) * 128)
-            total = sums_ref[:, lag_columns]
-            for index in range(C_RES):
-                rows = slice(index * pairs, (index + 1) * pairs)
-                total = total + outer[2 * index : 2 * index + 1, lag_columns] * turned[rows, tile * 128 : (tile + 1) * 128]
-                total = total + outer[2 * index + 1 : 2 * index + 2, lag_columns] * turned[
-                    rows, SUB + tile * 128 : SUB + (tile + 1) * 128
-                ]
-            sums_ref[:, lag_columns] = total
-
-    @pl.when(step == C_STEPS - 1)
-    def _():
-        share = out_ref.shape[2]
-        for part in range(out_ref.shape[0]):
-            out_ref[part] = sums_ref[:, part * share : (part + 1) * share].astype(out_ref.dtype)
-
-
-def lag_sums(places, received, parts, normalizer):
+    lanes = lax.broadcasted_iota(jnp.int32, (ends, 128), 1)
+    places = places_ref[...]
+    for window in range(windows):
+        for tile in range(slots // 128):
+            hit = jnp.where(places + window * CAP == lanes + tile * 128, 1.0, 0.0)
+            rows = slice(window * ends, (window + 1) * ends)
+            select_ref[rows, tile * 128 : (tile + 1) * 128] = hit.astype(jnp.bfloat16)
+
+    for step in range(STEPS):
+        columns = slice(step * 4 * DBINS, (step + 1) * 4 * DBINS)
+        picked = jnp.dot(select_ref[...], received_ref[:, columns], preferred_element_type=jnp.float32)
+        for half in range(2):
+            real_columns = slice(half * 2 * DBINS, half * 2 * DBINS + DBINS)
+            imag_columns = slice(half * 2 * DBINS + DBINS, (half + 1) * 2 * DBINS)
+            real_sum = imag_sum = None
+            for window in range(windows):
+                left = slice(window * ends, window * ends + pairs)
+                right = slice(window * ends + pairs, (window + 1) * ends)
+                left_real, left_imag = picked[left, real_columns], picked[left, imag_columns]
+                right_real, right_imag = picked[right, real_columns], picked[right, imag_columns]
+                real_term = left_real * right_real + left_imag * right_imag
+                imag_term = left_imag * right_real - left_real * right_imag
+                real_sum = real_term if real_sum is None else real_sum + real_term
+                imag_sum = imag_term if imag_sum is None else imag_sum + imag_term
+            position = 2 * step + half
+            rows = slice(position * pairs, (position + 1) * pairs)
+            stacked_ref[rows, :DBINS] = real_sum.astype(jnp.bfloat16)
+            stacked_ref[rows, DBINS:] = imag_sum.astype(jnp.bfloat16)
+
+    turned_ref[...] = jnp.dot(stacked_ref[...], inner_ref[...], preferred_element_type=jnp.float32)
+
+    for tile in range(SUB // 128):
+        columns = slice(tile * 128, (tile + 1) * 128)
+        imag_columns = slice(SUB + tile * 128, SUB + (tile + 1) * 128)
+        for group in range(pairs // 8):
+            real_of, imag_of = {}, {}
+            for position, turn in enumerate(TURNS):
+                rows = slice(position * pairs + group * 8, position * pairs + group * 8 + 8)
+                real_part, imag_part = turned_ref[rows, columns], turned_ref[rows, imag_columns]
+                cos_turn = outer_ref[2 * position : 2 * position + 1, columns]
+                sin_turn = outer_ref[2 * position + 1 : 2 * position + 2, columns]
+                real_of[turn] = real_part * cos_turn - imag_part * sin_turn
+                if turn % STEPS:
+                    imag_of[turn] = real_part * sin_turn + imag_part * cos_turn
+            r0, r6 = real_of[0], real_of[6]
+            re = [None] + [real_of[r] + real_of[RADIX - r] for r in range(1, STEPS)]
+            im = [None] + [imag_of[r] - imag_of[RADIX - r] for r in range(1, STEPS)]
+            even, odd = re[2] + re[4], re[1] + re[5]
+            q_zero = (r0 + r6) + (even + odd + re[3])
+            q_one_real = (r0 - r6) + 0.5 * (re[2] - re[4]) + ROOT3_2 * (re[1] - re[5])
+            q_one_imag = 0.5 * (im[1] + im[5]) + ROOT3_2 * (im[2] + im[4]) + im[3]
+            q_two_real = (r0 + r6) + 0.5 * (re[1] + re[5] - even) - re[3]
+            q_two_imag = ROOT3_2 * (im[1] + im[2] - im[4] - im[5])
+            periods = [q_two_real + q_two_imag, q_one_real + q_one_imag, q_zero, q_one_real - q_one_imag]
+            for period, values in enumerate(periods):
+                sums_ref[group * 8 : group * 8 + 8, period * SUB + tile * 128 : period * SUB + (tile + 1) * 128] = values
+
+    rings = kept_ref.shape[0]
+    share = kept_ref.shape[2]
+    for offset in range(rings):
+        ring = lax.rem(place_ref[0] + offset, rings)
+        kept = pl.multiple_of((2 * ring + place_ref[1]) * share, share)
+        sent = pl.multiple_of((2 * ring + 1 - place_ref[1]) * share, share)
+        kept_ref[offset] = sums_ref[:, pl.ds(kept, share)]
+        sent_ref[offset] = sums_ref[:, pl.ds(sent, share)].astype(sent_ref.dtype)
+
+
+def lag_sums(place, places, received, parts, normalizer):
     ends = places.shape[0]
     slots = received.shape[0]
     pairs = ends // 2
     windows = slots // (32 * CAP)
     inner, outer = lag_tables(normalizer)
+    share = 2 * LAG // parts
+    vmem = pl.BlockSpec(memory_space=pltpu.VMEM)
     return pl.pallas_call(
         lag_kernel,
-        out_shape=jax.ShapeDtypeStruct((parts, pairs, 2 * LAG // parts), jnp.bfloat16),
-        grid_spec=pltpu.PrefetchScalarGridSpec(
-            num_scalar_prefetch=0,
-            grid=(C_STEPS,),
-            in_specs=[
-                pl.BlockSpec((ends, 128), lambda s: (0, 0)),
-                pl.BlockSpec((slots, 256 * C_RES), lambda s: (0, s)),
-                pl.BlockSpec((2 * DBINS, 2 * SUB), lambda s: (0, 0)),
-                pl.BlockSpec((1, 2 * C_RES, 2 * LAG), lambda s: (s, 0, 0)),
-            ],
-            out_specs=pl.BlockSpec((parts, pairs, 2 * LAG // parts), lambda s: (0, 0, 0)),
-            scratch_shapes=[
-                pltpu.VMEM((windows * ends, slots), jnp.bfloat16),
-                pltpu.VMEM((pairs, 2 * LAG), jnp.float32),
-            ],
+        out_shape=(
+            jax.ShapeDtypeStruct((parts // 2, pairs, share), jnp.float32),
+            jax.ShapeDtypeStruct((parts // 2, pairs, share), jnp.bfloat16),
         ),
-        compiler_params=pltpu.CompilerParams(
-            dimension_semantics=("arbitrary",), vmem_limit_bytes=32 << 20
-        ),
+        in_specs=[pl.BlockSpec(memory_space=pltpu.SMEM)] + [vmem] * 4,
+        out_specs=(vmem, vmem),
+        scratch_shapes=[
+            pltpu.VMEM((windows * ends, slots), jnp.bfloat16),
+            pltpu.VMEM((RADIX * pairs, 2 * DBINS), jnp.bfloat16),
+            pltpu.VMEM((RADIX * pairs, 2 * SUB), jnp.float32),
+            pltpu.VMEM((pairs, 2 * LAG), jnp.float32),
+        ],
+        compiler_params=pltpu.CompilerParams(vmem_limit_bytes=32 << 20),
         cost_estimate=pl.CostEstimate(
             flops=2 * windows * ends * slots * 2 * F, bytes_accessed=5_000_000, transcendentals=0
         ),
         name="lag_sums",
-    )(places, received, jnp.asarray(inner), jnp.asarray(outer.reshape(C_STEPS, 2 * C_RES, 2 * LAG)))
-
-
-def total_kernel(parts_ref, out_ref):
-    total = parts_ref[0].astype(jnp.float32)
-    for part in range(1, parts_ref.shape[0]):
-        total = total + parts_ref[part].astype(jnp.float32)
-    out_ref[...] = total
-
-
-def window_total(parts):
+    )(place, places, received, jnp.asarray(inner), jnp.asarray(outer))
+
+
+def add_kernel(kept_ref, got_ref, own_ref, *sent_refs):
+    own_ref[...] = kept_ref[0] + got_ref[0].astype(jnp.float32)
+    for offset, sent_ref in enumerate(sent_refs, 1):
+        sent_ref[...] = (kept_ref[offset] + got_ref[offset].astype(jnp.float32)).astype(sent_ref.dtype)
+
+
+def total_kernel(own_ref, *rest):
+    total = own_ref[...]
+    for got_ref in rest[:-1]:
+        total = total + got_ref[...].astype(jnp.float32)
+    rest[-1][...] = total
+
+
+def window_total(kept, sent):
+    rings, pairs, share = kept.shape
+    devices = range(2 * rings)
+    got = lax.ppermute(sent, "tm", [(source, source ^ 1) for source in devices])
+    params = pltpu.CompilerParams(vmem_limit_bytes=16 << 20)
+    own, *onward = pl.pallas_call(
+        add_kernel,
+        out_shape=[jax.ShapeDtypeStruct((pairs, share), jnp.float32)]
+        + [jax.ShapeDtypeStruct((pairs, share), jnp.bfloat16)] * (rings - 1),
+        compiler_params=params,
+        name="core_total",
+    )(kept, got)
+    arrived = []
+    for offset, values in enumerate(onward, 1):
+        targets = [(source, (source // 2 + offset) % rings * 2 + source % 2) for source in devices]
+        arrived.append(lax.ppermute(values, "tm", targets))
     return pl.pallas_call(
         total_kernel,
-        out_shape=jax.ShapeDtypeStruct(parts.shape[1:], jnp.float32),
+        out_shape=jax.ShapeDtypeStruct((pairs, share), jnp.float32),
+        compiler_params=params,
         name="window_total",
-    )(parts).T
+    )(own, *arrived).T
 
 
 def on_device(traces, station_slot, pair_stations):
     window_count, station_count, length = traces.shape
     blocks = lax.axis_size("pairs")
     lag_parts = lax.axis_size("tm")
+    slots = blocks * window_count * CAP
     normalizer = 1.0 / math.sqrt(F * window_count * lag_parts)
+    own = lax.axis_index("tm")
+    place = jnp.stack([own // 2, own % 2]).astype(jnp.int32)
     wanted, places = requests(station_slot, pair_stations, blocks, window_count, station_count)
     picks = lax.all_to_all(wanted, "pairs", split_axis=0, concat_axis=0, tiled=True)
     whitened = whitened_spectra(traces.reshape(window_count * station_count, length))
     rows = jnp.dot(
-        picks.reshape(blocks * window_count * CAP, window_count * station_count),
-        whitened,
-        preferred_element_type=jnp.bfloat16,
+        picks.reshape(slots, window_count * station_count), whitened, preferred_element_type=jnp.bfloat16
     )
     received = lax.all_to_all(
         rows.reshape(blocks, window_count * CAP, 2 * F), "pairs", split_axis=0, concat_axis=0, tiled=True
     )
-    sums = lag_sums(places, received.reshape(blocks * window_count * CAP, 2 * F), lag_parts, normalizer)
-    parts = lax.all_to_all(sums, "tm", split_axis=0, concat_axis=0, tiled=True)
-    return window_total(parts)
+    kept, sent = lag_sums(place, places, received.reshape(slots, 2 * F), lag_parts, normalizer)
+    return window_total(kept, sent)
 
 
 def solution(mesh):

time: 122 us -> 120 us (0.984)
  blocking collectives: 90.8 us -> 0 us
  waiting for transfers between devices: 3.98 us -> 78 us
  starting transfers between devices: 11.9 us -> 26.8 us
  Pallas kernels: 12.5 us -> 10.4 us
  matrix products: 2.1 us -> 3.74 us
    all_to_all x2 -> x0, blocking collectives: 90.8 us -> none  [the longest x1 74.8 us: on_device(): lax.all_to_all(rows.reshape(blocks, window_count * CAP, 2 * F), 'pairs',...]
    all_to_all x0 -> x1, waiting for transfers between devices: none -> 71.1 us  [on_device(): lax.all_to_all(rows.reshape(blocks, window_count * CAP, 2 * F), 'pairs',...]
    ppermute x0 -> x4, starting transfers between devices: none -> 9.53 us  [the longest x3 5.07 us: window_total(): arrived.append(lax.ppermute(values, 'tm', targets))]
    all_to_all x0 -> x1, starting transfers between devices: none -> 5.38 us  [on_device(): lax.all_to_all(rows.reshape(blocks, window_count * CAP, 2 * F), 'pairs',...]
    ppermute x0 -> x4, waiting for transfers between devices: none -> 2.96 us  [the longest x3 1.97 us: window_total(): arrived.append(lax.ppermute(values, 'tm', targets))]
    pallas_call x2 -> x3, Pallas kernels: 5.12 us -> 3.04 us  [the longest x1 2.37 us: lag_sums(): pl.pallas_call(lag_kernel, out_shape=(jax.ShapeDtypeStruct((parts // 2, p...]
    dot_general x1, matrix products: 2.1 us -> 3.74 us  [on_device(): jnp.dot(picks.reshape(slots, window_count * station_count), whitened, pre...]
  transfers between devices with their start and end apart: 1 -> 6, of which waited for: 1 -> 5; matrix products, arithmetic and copies ran while one was open for 0% -> 0% of each run, Pallas kernels for 4% -> 4%
where the time goes in v3:
time: 120 us
  waiting for transfers between devices  78 us (65%)
  starting transfers between devices  26.8 us (22%)
  Pallas kernels  10.4 us (9%)
  matrix products  3.74 us (3%)
    all_to_all x1, waiting for transfers between devices, on_device(): lax.all_to_all(rows.reshape(blocks, window_count * CAP, 2 * F), 'pairs',...  71.1 us
    all_to_all x1, starting transfers between devices, on_device(): lax.all_to_all(wanted, 'pairs', split_axis=0, concat_axis=0, tiled=True)  11.9 us
    all_to_all x1, starting transfers between devices, on_device(): lax.all_to_all(rows.reshape(blocks, window_count * CAP, 2 * F), 'pairs',...  5.38 us
    pallas_call x1, Pallas kernels, whitened_spectra(): pl.pallas_call(spectrum_kernel, out_shape=jax.ShapeDtypeStruct((total, 2...  5.18 us
    ppermute x3, starting transfers between devices, window_total(): arrived.append(lax.ppermute(values, 'tm', targets))  5.07 us
    ppermute x1, starting transfers between devices, window_total(): got = lax.ppermute(sent, 'tm', [(source, source ^ 1) for source in devices])  4.46 us
    all_to_all x1, waiting for transfers between devices, on_device(): lax.all_to_all(wanted, 'pairs', split_axis=0, concat_axis=0, tiled=True)  3.97 us
    dot_general x1, matrix products, on_device(): jnp.dot(picks.reshape(slots, window_count * station_count), whitened, pre...  3.74 us
  transfers between devices with their start and end apart: 6, of which 5 were waited for; matrix products, arithmetic and copies ran while one was open for 0% of the time, Pallas kernels for 4%

profile of v3, /device:TPU:1, one launch (start us, length us, event | category | flops | bytes accessed | tf_op | source)
XLA Modules:
  0.0 120.1 jit_solution(1466726979153049629)
XLA Ops:
  0.0 2.2 %requests.1 = (bf16[32,16,128]{2,1,0:T(8,128)(2,1)}, s32[128,128]{1,0:T(8,128)}) custom-call(s32[16,128]{1,0:T(8,128)} %bitcast.13, s32[2,64]{1,0:T(2,128)} %bitcast.14), custom_call_target="tpu_custom_call" | custom-call | tf_op jit(solution)/shard_map/requests/pallas_call | solution.py:106
  2.2 11.9 %all-to-all-start = ((bf16[32,16,128]{2,1,0:T(8,128)(2,1)}), bf16[32,16,128]{2,1,0:T(8,128)(2,1)S(1)}, u32[]{:S(2)}, u32[]{:S(2)}) async-start(bf16[32,16,128]{2,1,0:T(8,128)(2,1)} %get-tuple-element.14), calls=%async_computation | async-start | bytes 262144 | tf_op jit(solution)/shard_map/all_to_all | solution.py:405
  14.0 5.2 %whitened_spectra.1 = bf16[128,3072]{1,0:T(8,128)(2,1)} custom-call(f32[128,6144]{1,0:T(8,128)} %bitcast.12, f32[1,6144]{1,0:T(1,128)} %constant.38.clone.hann_ref, f32[24,512]{1,0:T(8,128)} %constant.39.clone.turns_ref, bf16[1024,256]{1,0:T(8,128)(2,1)} %constant.40.clone.table_ref), custom_call_target="tpu_custom_call" | custom-call | flops 805306368 | bytes 5000000 | tf_op jit(solution)/shard_map/whitened_spectra/pallas_call | solution.py:229
  19.2 4.0 %all-to-all-done = bf16[32,16,128]{2,1,0:T(8,128)(2,1)S(1)} async-done(((bf16[32,16,128]{2,1,0:T(8,128)(2,1)}), bf16[32,16,128]{2,1,0:T(8,128)(2,1)S(1)}, u32[]{:S(2)}, u32[]{:S(2)}) %all-to-all-start) | async-done | bytes 131104 | tf_op jit(solution)/shard_map/all_to_all | solution.py:405
  23.2 3.7 %fusion = bf16[32,16,3072]{2,1,0:T(8,128)(2,1)} fusion(bf16[32,16,128]{2,1,0:T(8,128)(2,1)S(1)} %all-to-all-done, bf16[128,3072]{1,0:T(8,128)(2,1)} %whitened_spectra.1), kind=kOutput, calls=%fused_computation | convolution fusion | flops 402653184 | bytes 4063232 | tf_op jit(solution)/shard_map/dot_general | solution.py:407
  26.9 0.0 copy-start.1
  26.9 0.0 copy-start.2
  26.9 5.4 %all-to-all-start.1 = ((bf16[32,16,3072]{2,1,0:T(8,128)(2,1)}), bf16[32,16,3072]{2,1,0:T(8,128)(2,1)S(1)}, u32[]{:S(2)}, u32[]{:S(2)}) async-start(bf16[32,16,3072]{2,1,0:T(8,128)(2,1)} %fusion), calls=%async_computation.1 | async-start | bytes 6291456 | tf_op jit(solution)/shard_map/all_to_all | solution.py:410
  32.3 0.1 pad_add_fusion.place_ref
  32.4 71.1 %all-to-all-done.1 = bf16[32,16,3072]{2,1,0:T(8,128)(2,1)S(1)} async-done(((bf16[32,16,3072]{2,1,0:T(8,128)(2,1)}), bf16[32,16,3072]{2,1,0:T(8,128)(2,1)S(1)}, u32[]{:S(2)}, u32[]{:S(2)}) %all-to-all-start.1) | async-done | bytes 3145760 | tf_op jit(solution)/shard_map/all_to_all | solution.py:410
  103.5 0.0 copy-done.1
  103.5 0.0 copy-done.2
  103.5 0.0 copy-start
  103.5 1.0 copy-done
  104.6 2.4 %lag_sums.1 = (f32[4,64,256]{2,1,0:T(8,128)S(1)}, bf16[4,64,256]{2,1,0:T(8,128)(2,1)S(1)}) custom-call(s32[2]{0:T(128)S(1)} %pad_add_fusion.place_ref, s32[128,128]{1,0:T(8,128)S(1)} %copy-done.1, bf16[512,3072]{1,0:T(8,128)(2,1)S(1)} %bitcast.11, bf16[256,1024]{1,0:T(8,128)(2,1)S(1)} %copy-done, f32[24,512]{1,0:T(8,128)S(1)} %copy-done.2), custom_call_target="tpu_custom_call" | custom-call | flops 805306368 | bytes 5000000 | tf_op jit(solution)/shard_map/lag_sums/pallas_call | solution.py:337
  107.0 4.5 %collective-permute-start = (bf16[4,64,256]{2,1,0:T(8,128)(2,1)S(1)}, bf16[4,64,256]{2,1,0:T(8,128)(2,1)S(1)}, u32[]{:S(2)}, u32[]{:S(2)}) collective-permute-start(bf16[4,64,256]{2,1,0:T(8,128)(2,1)S(1)} %get-tuple-element.16), channel_id=1, source_target_pairs={{0,1},{1,0},{2,3},{3,2},{4,5},{5,4},{6,7},{7,6},{8,9},{9,8},{10,11... | collective-permute-start | bytes 393224 | tf_op jit(solution)/shard_map/ppermute | solution.py:375
  111.4 1.0 collective-permute-done.got_ref
  112.4 1.4 %collective-permute-start.1 = (bf16[64,256]{1,0:T(8,128)(2,1)S(1)}, bf16[64,256]{1,0:T(8,128)(2,1)S(1)}, u32[]{:S(2)}, u32[]{:S(2)}) collective-permute-start(bf16[64,256]{1,0:T(8,128)(2,1)S(1)} %get-tuple-element.18), channel_id=1, source_target_pairs={{0,2},{1,3},{2,4},{3,5},{4,6},{5,7},{6,0},{7,1},{8,10},{9,11},{10,... | collective-permute-start | bytes 98312 | tf_op jit(solution)/shard_map/ppermute | solution.py:387
  113.8 2.6 %collective-permute-start.2 = (bf16[64,256]{1,0:T(8,128)(2,1)S(1)}, bf16[64,256]{1,0:T(8,128)(2,1)S(1)}, u32[]{:S(2)}, u32[]{:S(2)}) collective-permute-start(bf16[64,256]{1,0:T(8,128)(2,1)S(1)} %get-tuple-element.19), channel_id=1, source_target_pairs={{0,4},{1,5},{2,6},{3,7},{4,0},{5,1},{6,2},{7,3},{8,12},{9,13},{10,... | collective-permute-start | bytes 98312 | tf_op jit(solution)/shard_map/ppermute | solution.py:387
  116.4 1.1 collective-permute-start.3
  117.5 0.0 collective-permute-done.1.rest_0_
  117.5 0.6 collective-permute-done.2.rest_1_
  118.1 1.4 %collective-permute-done.3.rest_2_ = bf16[64,256]{1,0:T(8,128)(2,1)S(1)} collective-permute-done((bf16[64,256]{1,0:T(8,128)(2,1)S(1)}, bf16[64,256]{1,0:T(8,128)(2,1)S(1)}, u32[]{:S(2)}, u32[]{:S(2)}) %collective-permute-start.3) | collective-permute-done | bytes 32800 | tf_op jit(solution)/shard_map/ppermute | solution.py:387
  119.5 0.6 window_total.1
  (1 shorter events, 0.0 us)
Async XLA Ops:
  2.2 21.0 %all-to-all-start = ((bf16[32,16,128]{2,1,0:T(8,128)(2,1)}), bf16[32,16,128]{2,1,0:T(8,128)(2,1)S(1)}, u32[]{:S(2)}, u32[]{:S(2)}) async-start(bf16[32,16,128]{2,1,0:T(8,128)(2,1)} %get-tuple-element.14), calls=%async_computation | async-start | bytes 262144 | tf_op jit(solution)/shard_map/all_to_all | solution.py:405
  26.9 76.6 %copy-start.1 = (s32[128,128]{1,0:T(8,128)S(1)}, s32[128,128]{1,0:T(8,128)}, u32[]{:S(2)}) copy-start(s32[128,128]{1,0:T(8,128)} %get-tuple-element.13.places_ref) | copy-start | bytes 196612
  26.9 76.6 %copy-start.2 = (f32[24,512]{1,0:T(8,128)S(1)}, f32[24,512]{1,0:T(8,128)}, u32[]{:S(2)}) copy-start(f32[24,512]{1,0:T(8,128)} %constant.42.clone.outer_ref) | copy-start | bytes 147460
  26.9 76.6 %all-to-all-start.1 = ((bf16[32,16,3072]{2,1,0:T(8,128)(2,1)}), bf16[32,16,3072]{2,1,0:T(8,128)(2,1)S(1)}, u32[]{:S(2)}, u32[]{:S(2)}) async-start(bf16[32,16,3072]{2,1,0:T(8,128)(2,1)} %fusion), calls=%async_computation.1 | async-start | bytes 6291456 | tf_op jit(solution)/shard_map/all_to_all | solution.py:410
  103.5 1.0 copy-start
  107.0 5.5 %collective-permute-start = (bf16[4,64,256]{2,1,0:T(8,128)(2,1)S(1)}, bf16[4,64,256]{2,1,0:T(8,128)(2,1)S(1)}, u32[]{:S(2)}, u32[]{:S(2)}) collective-permute-start(bf16[4,64,256]{2,1,0:T(8,128)(2,1)S(1)} %get-tuple-element.16), channel_id=1, source_target_pairs={{0,1},{1,0},{2,3},{3,2},{4,5},{5,4},{6,7},{7,6},{8,9},{9,8},{10,11... | collective-permute-start | bytes 393224 | tf_op jit(solution)/shard_map/ppermute | solution.py:375
  112.4 5.1 %collective-permute-start.1 = (bf16[64,256]{1,0:T(8,128)(2,1)S(1)}, bf16[64,256]{1,0:T(8,128)(2,1)S(1)}, u32[]{:S(2)}, u32[]{:S(2)}) collective-permute-start(bf16[64,256]{1,0:T(8,128)(2,1)S(1)} %get-tuple-element.18), channel_id=1, source_target_pairs={{0,2},{1,3},{2,4},{3,5},{4,6},{5,7},{6,0},{7,1},{8,10},{9,11},{10,... | collective-permute-start | bytes 98312 | tf_op jit(solution)/shard_map/ppermute | solution.py:387
  113.8 4.3 %collective-permute-start.2 = (bf16[64,256]{1,0:T(8,128)(2,1)S(1)}, bf16[64,256]{1,0:T(8,128)(2,1)S(1)}, u32[]{:S(2)}, u32[]{:S(2)}) collective-permute-start(bf16[64,256]{1,0:T(8,128)(2,1)S(1)} %get-tuple-element.19), channel_id=1, source_target_pairs={{0,4},{1,5},{2,6},{3,7},{4,0},{5,1},{6,2},{7,3},{8,12},{9,13},{10,... | collective-permute-start | bytes 98312 | tf_op jit(solution)/shard_map/ppermute | solution.py:387
  116.4 3.0 %collective-permute-start.3 = (bf16[64,256]{1,0:T(8,128)(2,1)S(1)}, bf16[64,256]{1,0:T(8,128)(2,1)S(1)}, u32[]{:S(2)}, u32[]{:S(2)}) collective-permute-start(bf16[64,256]{1,0:T(8,128)(2,1)S(1)} %get-tuple-element.20), channel_id=1, source_target_pairs={{0,6},{1,7},{2,0},{3,1},{4,2},{5,3},{6,4},{7,5},{8,14},{9,15},{10,... | collective-permute-start | bytes 98312 | tf_op jit(solution)/shard_map/ppermute | solution.py:387

commit v4 on v3

--- a/solution.py
+++ b/solution.py
@@ -44,7 +44,7 @@
 def lag_tables(normalizer):
     bins = np.arange(DBINS, dtype=np.int64)[:, None]
     sub_lags = np.arange(SUB, dtype=np.int64)[None, :]
-    angles = (bins * sub_lags % SUB) * (2.0 * np.pi / SUB)
+    angles = (bins * sub_lags % SUB)[:, :DBINS] * (2.0 * np.pi / SUB)
     cos_part, sin_part = np.cos(angles), np.sin(angles)
     inner = np.block([[cos_part, sin_part], [-sin_part, cos_part]]).astype(ml_dtypes.bfloat16)
     first_bins = FLO + np.array(RESIDUES, dtype=np.int64)[:, None]
@@ -78,7 +78,6 @@
     ).astype(jnp.int32)
     owner_column = slot_column // stations
     owner_row = slot_row // stations
-    local_row = slot_row - owner_row * stations
     same_owner = owner_column == owner_row
     rank_row = jnp.sum(
         jnp.where(same_owner & (sublane < lane), 1.0, 0.0), axis=0, keepdims=True
@@ -87,18 +86,19 @@
         jnp.where(same_owner & (lane < sublane), 1.0, 0.0), axis=1, keepdims=True
     ).astype(jnp.int32)
     places_ref[...] = jnp.broadcast_to(owner_column * (windows * CAP) + rank_column, places_ref.shape)
-    owned = lax.broadcasted_iota(jnp.int32, (owners_count, ends), 0) == owner_row
-    column_ids = lax.broadcasted_iota(jnp.int32, (owners_count, 1, windows * stations), 2)
-    picks = [[] for _ in range(windows)]
-    for rank in range(CAP):
-        hit = owned & (rank_row == rank)
-        row_wanted = jnp.sum(
-            jnp.where(hit, local_row, 0).astype(jnp.float32), axis=1, keepdims=True
-        ).astype(jnp.int32)
-        for window in range(windows):
-            column = (row_wanted + window * stations)[:, :, None]
-            picks[window].append(jnp.where(column_ids == column, 1.0, 0.0))
-    wanted_ref[...] = jnp.concatenate(sum(picks, []), axis=1).astype(jnp.bfloat16)
+    row_keys = owner_row * (windows * CAP) + rank_row
+    slots = owners_count * windows * CAP
+    slot_ids = lax.broadcasted_iota(jnp.int32, (slots, ends), 0)
+    slot_windows = slot_ids // CAP % windows
+    local_column = slot_column - owner_column * stations
+    picks = None
+    for window in range(windows):
+        hit = (slot_ids == row_keys + window * CAP) & (slot_windows == window)
+        columns = lax.broadcasted_iota(jnp.int32, (ends, windows * stations), 1)
+        rows = jnp.where(columns == local_column + window * stations, 1.0, 0.0).astype(jnp.bfloat16)
+        term = jnp.dot(jnp.where(hit, 1.0, 0.0).astype(jnp.bfloat16), rows, preferred_element_type=jnp.float32)
+        picks = term if picks is None else picks + term
+    wanted_ref[...] = picks.astype(jnp.bfloat16).reshape(wanted_ref.shape)
 
 
 def requests(station_slot, pair_stations, blocks, windows, stations):
@@ -214,6 +214,34 @@
         whiten_group(group)
 
 
+def in_hbm(*arrays):
+    return [pltpu.with_memory_space_constraint(array, pltpu.HBM) for array in arrays]
+
+
+def gather_kernel(picks_ref, whitened_ref, rows_ref):
+    rows_ref[...] = jnp.dot(picks_ref[...], whitened_ref[...], preferred_element_type=jnp.float32).astype(
+        rows_ref.dtype
+    )
+
+
+def gathered(picks, whitened):
+    slots, rows = picks.shape
+    return pl.pallas_call(
+        gather_kernel,
+        out_shape=pltpu.HBM((slots, whitened.shape[1]), whitened.dtype),
+        grid=(slots // 128,),
+        in_specs=[
+            pl.BlockSpec((128, rows), lambda s: (s, 0)),
+            pl.BlockSpec(whitened.shape, lambda s: (0, 0)),
+        ],
+        out_specs=pl.BlockSpec((128, whitened.shape[1]), lambda s: (s, 0)),
+        compiler_params=pltpu.CompilerParams(
+            dimension_semantics=("arbitrary",), vmem_limit_bytes=16 << 20
+        ),
+        name="gathered",
+    )(picks, whitened)
+
+
 PART_ROWS = 32
 STEP_PARTS = 2
 
@@ -241,14 +269,16 @@
             out_specs=pl.BlockSpec((rows, 2 * F), lambda s: (s, 0)),
             scratch_shapes=scratch * STEP_PARTS,
         ),
-        compiler_params=pltpu.CompilerParams(dimension_semantics=("arbitrary",)),
+        compiler_params=pltpu.CompilerParams(
+            dimension_semantics=("arbitrary",), vmem_limit_bytes=24 << 20
+        ),
         cost_estimate=pl.CostEstimate(
             flops=2 * total * RADIX * 2 * SUB * 2 * DBINS,
             bytes_accessed=5_000_000,
             transcendentals=total * F,
         ),
         name="whitened_spectra",
-    )(traces, jnp.asarray(hann_window()), jnp.asarray(turns), jnp.asarray(table))
+    )(*in_hbm(traces, jnp.asarray(hann_window()), jnp.asarray(turns), jnp.asarray(table)))
 
 
 def lag_kernel(
@@ -267,6 +297,11 @@
             rows = slice(window * ends, (window + 1) * ends)
             select_ref[rows, tile * 128 : (tile + 1) * 128] = hit.astype(jnp.bfloat16)
 
+    bins = lax.broadcasted_iota(jnp.int32, (1, DBINS), 1)
+    even = bins % 2 == 0
+    flip_odd = jnp.where(even, 1.0, -1.0)
+    flip_upper = jnp.where(bins % 4 < 2, 1.0, -1.0)
+    residue_rows = RADIX * pairs
     for step in range(STEPS):
         columns = slice(step * 4 * DBINS, (step + 1) * 4 * DBINS)
         picked = jnp.dot(select_ref[...], received_ref[:, columns], preferred_element_type=jnp.float32)
@@ -283,21 +318,29 @@
                 imag_term = left_imag * right_real - left_real * right_imag
                 real_sum = real_term if real_sum is None else real_sum + real_term
                 imag_sum = imag_term if imag_sum is None else imag_sum + imag_term
+            quarter_real = jnp.where(even, real_sum, -imag_sum) * flip_upper
+            quarter_imag = jnp.where(even, imag_sum, real_sum) * flip_upper
+            quarters = [
+                (real_sum, imag_sum),
+                (quarter_real, quarter_imag),
+                (real_sum * flip_odd, imag_sum * flip_odd),
+                (quarter_real * flip_odd, quarter_imag * flip_odd),
+            ]
             position = 2 * step + half
-            rows = slice(position * pairs, (position + 1) * pairs)
-            stacked_ref[rows, :DBINS] = real_sum.astype(jnp.bfloat16)
-            stacked_ref[rows, DBINS:] = imag_sum.astype(jnp.bfloat16)
+            for quarter, (real_part, imag_part) in enumerate(quarters):
+                first = quarter * residue_rows + position * pairs
+                stacked_ref[first : first + pairs, :DBINS] = real_part.astype(jnp.bfloat16)
+                stacked_ref[first : first + pairs, DBINS:] = imag_part.astype(jnp.bfloat16)
 
     turned_ref[...] = jnp.dot(stacked_ref[...], inner_ref[...], preferred_element_type=jnp.float32)
 
     for tile in range(SUB // 128):
         columns = slice(tile * 128, (tile + 1) * 128)
-        imag_columns = slice(SUB + tile * 128, SUB + (tile + 1) * 128)
         for group in range(pairs // 8):
             real_of, imag_of = {}, {}
             for position, turn in enumerate(TURNS):
-                rows = slice(position * pairs + group * 8, position * pairs + group * 8 + 8)
-                real_part, imag_part = turned_ref[rows, columns], turned_ref[rows, imag_columns]
+                first = tile * residue_rows + position * pairs + group * 8
+                real_part, imag_part = turned_ref[first : first + 8, :DBINS], turned_ref[first : first + 8, DBINS:]
                 cos_turn = outer_ref[2 * position : 2 * position + 1, columns]
                 sin_turn = outer_ref[2 * position + 1 : 2 * position + 2, columns]
                 real_of[turn] = real_part * cos_turn - imag_part * sin_turn
@@ -344,8 +387,8 @@
         out_specs=(vmem, vmem),
         scratch_shapes=[
             pltpu.VMEM((windows * ends, slots), jnp.bfloat16),
-            pltpu.VMEM((RADIX * pairs, 2 * DBINS), jnp.bfloat16),
-            pltpu.VMEM((RADIX * pairs, 2 * SUB), jnp.float32),
+            pltpu.VMEM((SUB // DBINS * RADIX * pairs, 2 * DBINS), jnp.bfloat16),
+            pltpu.VMEM((SUB // DBINS * RADIX * pairs, 2 * DBINS), jnp.float32),
             pltpu.VMEM((pairs, 2 * LAG), jnp.float32),
         ],
         compiler_params=pltpu.CompilerParams(vmem_limit_bytes=32 << 20),
@@ -404,9 +447,7 @@
     wanted, places = requests(station_slot, pair_stations, blocks, window_count, station_count)
     picks = lax.all_to_all(wanted, "pairs", split_axis=0, concat_axis=0, tiled=True)
     whitened = whitened_spectra(traces.reshape(window_count * station_count, length))
-    rows = jnp.dot(
-        picks.reshape(slots, window_count * station_count), whitened, preferred_element_type=jnp.bfloat16
-    )
+    rows = gathered(picks.reshape(slots, window_count * station_count), whitened)
     received = lax.all_to_all(
         rows.reshape(blocks, window_count * CAP, 2 * F), "pairs", split_axis=0, concat_axis=0, tiled=True
     )

time: 120 us -> 117 us (0.975)
  matrix products: 3.74 us -> 0 us
  Pallas kernels: 10.4 us -> 12.2 us
    dot_general x1 -> x0, matrix products: 3.74 us -> none  [on_device(): jnp.dot(picks.reshape(slots, window_count * station_count), whitened, pre...]
    pallas_call x0 -> x1, Pallas kernels: none -> 2.88 us  [gathered(): pl.pallas_call(gather_kernel, out_shape=pltpu.HBM((slots, whitened.shape[...]
where the time goes in v4:
time: 117 us
  waiting for transfers between devices  78.9 us (67%)
  starting transfers between devices  26 us (22%)
  Pallas kernels  12.2 us (10%)
    all_to_all x1, waiting for transfers between devices, on_device(): lax.all_to_all(rows.reshape(blocks, window_count * CAP, 2 * F), 'pairs',...  71.2 us
    all_to_all x1, starting transfers between devices, on_device(): lax.all_to_all(wanted, 'pairs', split_axis=0, concat_axis=0, tiled=True)  11.9 us
    ppermute x3, starting transfers between devices, window_total(): arrived.append(lax.ppermute(values, 'tm', targets))  5.06 us
    all_to_all x1, waiting for transfers between devices, on_device(): lax.all_to_all(wanted, 'pairs', split_axis=0, concat_axis=0, tiled=True)  4.71 us
    all_to_all x1, starting transfers between devices, on_device(): lax.all_to_all(rows.reshape(blocks, window_count * CAP, 2 * F), 'pairs',...  4.68 us
    pallas_call x1, Pallas kernels, whitened_spectra(): pl.pallas_call(spectrum_kernel, out_shape=jax.ShapeDtypeStruct((total, 2...  4.44 us
    ppermute x1, starting transfers between devices, window_total(): got = lax.ppermute(sent, 'tm', [(source, source ^ 1) for source in devices])  4.36 us
    pallas_call x1, Pallas kernels, gathered(): pl.pallas_call(gather_kernel, out_shape=pltpu.HBM((slots, whitened.shape[...  2.88 us
  transfers between devices with their start and end apart: 6, of which 5 were waited for; matrix products, arithmetic and copies ran while one was open for 0% of the time, Pallas kernels for 4%

profile of v4, /device:TPU:1, one launch (start us, length us, event | category | flops | bytes accessed | tf_op | source)
XLA Modules:
  0.0 117.2 jit_solution(8951943816291074268)
XLA Ops:
  0.0 2.0 %requests.1 = (bf16[32,16,128]{2,1,0:T(8,128)(2,1)}, s32[128,128]{1,0:T(8,128)}) custom-call(s32[16,128]{1,0:T(8,128)} %bitcast.13, s32[2,64]{1,0:T(2,128)} %bitcast.14), custom_call_target="tpu_custom_call" | custom-call | tf_op jit(solution)/shard_map/requests/pallas_call | solution.py:106
  2.0 11.9 %all-to-all-start = ((bf16[32,16,128]{2,1,0:T(8,128)(2,1)}), bf16[32,16,128]{2,1,0:T(8,128)(2,1)S(1)}, u32[]{:S(2)}, u32[]{:S(2)}) async-start(bf16[32,16,128]{2,1,0:T(8,128)(2,1)} %get-tuple-element.14), calls=%async_computation | async-start | bytes 262144 | tf_op jit(solution)/shard_map/all_to_all | solution.py:448
  13.8 4.4 %whitened_spectra.1.whitened_ref = bf16[128,3072]{1,0:T(8,128)(2,1)S(1)} custom-call(f32[128,6144]{1,0:T(8,128)} %bitcast.12, f32[1,6144]{1,0:T(1,128)} %constant.38.clone.hann_ref, f32[24,512]{1,0:T(8,128)} %constant.39.clone.turns_ref, bf16[1024,256]{1,0:T(8,128)(2,1)} %constant.40.clone.table_ref), custom_call_target="tpu_custom_call" | custom-call | flops 805306368 | bytes 5000000 | tf_op jit(solution)/shard_map/whitened_spectra/pallas_call | solution.py:257
  18.3 4.7 %all-to-all-done = bf16[32,16,128]{2,1,0:T(8,128)(2,1)S(1)} async-done(((bf16[32,16,128]{2,1,0:T(8,128)(2,1)}), bf16[32,16,128]{2,1,0:T(8,128)(2,1)S(1)}, u32[]{:S(2)}, u32[]{:S(2)}) %all-to-all-start) | async-done | bytes 131104 | tf_op jit(solution)/shard_map/all_to_all | solution.py:448
  23.0 2.9 %gathered.1 = bf16[512,3072]{1,0:T(8,128)(2,1)} custom-call(bf16[512,128]{1,0:T(8,128)(2,1)S(1)} %bitcast.10, bf16[128,3072]{1,0:T(8,128)(2,1)S(1)} %whitened_spectra.1.whitened_ref), custom_call_target="tpu_custom_call" | custom-call | tf_op jit(solution)/shard_map/gathered/pallas_call | solution.py:229
  25.9 0.0 copy-start
  25.9 0.0 copy-start.1
  25.9 0.0 copy-start.2
  25.9 4.7 %all-to-all-start.1 = ((bf16[32,16,3072]{2,1,0:T(8,128)(2,1)}), bf16[32,16,3072]{2,1,0:T(8,128)(2,1)S(1)}, u32[]{:S(2)}, u32[]{:S(2)}) async-start(bf16[32,16,3072]{2,1,0:T(8,128)(2,1)} %bitcast.11), calls=%async_computation.1 | async-start | bytes 6291456 | tf_op jit(solution)/shard_map/all_to_all | solution.py:451
  30.6 0.1 pad_add_fusion.place_ref
  30.7 71.2 %all-to-all-done.1 = bf16[32,16,3072]{2,1,0:T(8,128)(2,1)S(1)} async-done(((bf16[32,16,3072]{2,1,0:T(8,128)(2,1)}), bf16[32,16,3072]{2,1,0:T(8,128)(2,1)S(1)}, u32[]{:S(2)}, u32[]{:S(2)}) %all-to-all-start.1) | async-done | bytes 3145760 | tf_op jit(solution)/shard_map/all_to_all | solution.py:451
  101.8 0.0 copy-done
  101.9 0.0 copy-done.1
  101.9 0.0 copy-done.2
  101.9 2.2 %lag_sums.1 = (f32[4,64,256]{2,1,0:T(8,128)S(1)}, bf16[4,64,256]{2,1,0:T(8,128)(2,1)S(1)}) custom-call(s32[2]{0:T(128)S(1)} %pad_add_fusion.place_ref, s32[128,128]{1,0:T(8,128)S(1)} %copy-done.1, bf16[512,3072]{1,0:T(8,128)(2,1)S(1)} %bitcast.9, bf16[256,256]{1,0:T(8,128)(2,1)S(1)} %copy-done, f32[24,512]{1,0:T(8,128)S(1)} %copy-done.2), custom_call_target="tpu_custom_call" | custom-call | flops 805306368 | bytes 5000000 | tf_op jit(solution)/shard_map/lag_sums/pallas_call | solution.py:380
  104.1 4.4 %collective-permute-start = (bf16[4,64,256]{2,1,0:T(8,128)(2,1)S(1)}, bf16[4,64,256]{2,1,0:T(8,128)(2,1)S(1)}, u32[]{:S(2)}, u32[]{:S(2)}) collective-permute-start(bf16[4,64,256]{2,1,0:T(8,128)(2,1)S(1)} %get-tuple-element.16), channel_id=1, source_target_pairs={{0,1},{1,0},{2,3},{3,2},{4,5},{5,4},{6,7},{7,6},{8,9},{9,8},{10,11... | collective-permute-start | bytes 393224 | tf_op jit(solution)/shard_map/ppermute | solution.py:418
  108.5 1.0 collective-permute-done.got_ref
  109.5 1.4 %collective-permute-start.1 = (bf16[64,256]{1,0:T(8,128)(2,1)S(1)}, bf16[64,256]{1,0:T(8,128)(2,1)S(1)}, u32[]{:S(2)}, u32[]{:S(2)}) collective-permute-start(bf16[64,256]{1,0:T(8,128)(2,1)S(1)} %get-tuple-element.18), channel_id=1, source_target_pairs={{0,2},{1,3},{2,4},{3,5},{4,6},{5,7},{6,0},{7,1},{8,10},{9,11},{10,... | collective-permute-start | bytes 98312 | tf_op jit(solution)/shard_map/ppermute | solution.py:430
  110.9 2.6 %collective-permute-start.2 = (bf16[64,256]{1,0:T(8,128)(2,1)S(1)}, bf16[64,256]{1,0:T(8,128)(2,1)S(1)}, u32[]{:S(2)}, u32[]{:S(2)}) collective-permute-start(bf16[64,256]{1,0:T(8,128)(2,1)S(1)} %get-tuple-element.19), channel_id=1, source_target_pairs={{0,4},{1,5},{2,6},{3,7},{4,0},{5,1},{6,2},{7,3},{8,12},{9,13},{10,... | collective-permute-start | bytes 98312 | tf_op jit(solution)/shard_map/ppermute | solution.py:430
  113.5 1.1 collective-permute-start.3
  114.5 0.0 collective-permute-done.1.rest_0_
  114.5 0.6 collective-permute-done.2.rest_1_
  115.1 1.4 %collective-permute-done.3.rest_2_ = bf16[64,256]{1,0:T(8,128)(2,1)S(1)} collective-permute-done((bf16[64,256]{1,0:T(8,128)(2,1)S(1)}, bf16[64,256]{1,0:T(8,128)(2,1)S(1)}, u32[]{:S(2)}, u32[]{:S(2)}) %collective-permute-start.3) | collective-permute-done | bytes 32800 | tf_op jit(solution)/shard_map/ppermute | solution.py:430
  116.5 0.6 window_total.1
  (1 shorter events, 0.0 us)
Async XLA Ops:
  2.0 21.0 %all-to-all-start = ((bf16[32,16,128]{2,1,0:T(8,128)(2,1)}), bf16[32,16,128]{2,1,0:T(8,128)(2,1)S(1)}, u32[]{:S(2)}, u32[]{:S(2)}) async-start(bf16[32,16,128]{2,1,0:T(8,128)(2,1)} %get-tuple-element.14), calls=%async_computation | async-start | bytes 262144 | tf_op jit(solution)/shard_map/all_to_all | solution.py:448
  25.9 76.0 %copy-start = (bf16[256,256]{1,0:T(8,128)(2,1)S(1)}, bf16[256,256]{1,0:T(8,128)(2,1)}, u32[]{:S(2)}) copy-start(bf16[256,256]{1,0:T(8,128)(2,1)} %constant.41.clone.inner_ref) | copy-start | bytes 393220
  25.9 76.0 %copy-start.1 = (s32[128,128]{1,0:T(8,128)S(1)}, s32[128,128]{1,0:T(8,128)}, u32[]{:S(2)}) copy-start(s32[128,128]{1,0:T(8,128)} %get-tuple-element.13.places_ref) | copy-start | bytes 196612
  25.9 76.0 %copy-start.2 = (f32[24,512]{1,0:T(8,128)S(1)}, f32[24,512]{1,0:T(8,128)}, u32[]{:S(2)}) copy-start(f32[24,512]{1,0:T(8,128)} %constant.42.clone.outer_ref) | copy-start | bytes 147460
  25.9 76.0 %all-to-all-start.1 = ((bf16[32,16,3072]{2,1,0:T(8,128)(2,1)}), bf16[32,16,3072]{2,1,0:T(8,128)(2,1)S(1)}, u32[]{:S(2)}, u32[]{:S(2)}) async-start(bf16[32,16,3072]{2,1,0:T(8,128)(2,1)} %bitcast.11), calls=%async_computation.1 | async-start | bytes 6291456 | tf_op jit(solution)/shard_map/all_to_all | solution.py:451
  104.1 5.4 %collective-permute-start = (bf16[4,64,256]{2,1,0:T(8,128)(2,1)S(1)}, bf16[4,64,256]{2,1,0:T(8,128)(2,1)S(1)}, u32[]{:S(2)}, u32[]{:S(2)}) collective-permute-start(bf16[4,64,256]{2,1,0:T(8,128)(2,1)S(1)} %get-tuple-element.16), channel_id=1, source_target_pairs={{0,1},{1,0},{2,3},{3,2},{4,5},{5,4},{6,7},{7,6},{8,9},{9,8},{10,11... | collective-permute-start | bytes 393224 | tf_op jit(solution)/shard_map/ppermute | solution.py:418
  109.5 5.1 %collective-permute-start.1 = (bf16[64,256]{1,0:T(8,128)(2,1)S(1)}, bf16[64,256]{1,0:T(8,128)(2,1)S(1)}, u32[]{:S(2)}, u32[]{:S(2)}) collective-permute-start(bf16[64,256]{1,0:T(8,128)(2,1)S(1)} %get-tuple-element.18), channel_id=1, source_target_pairs={{0,2},{1,3},{2,4},{3,5},{4,6},{5,7},{6,0},{7,1},{8,10},{9,11},{10,... | collective-permute-start | bytes 98312 | tf_op jit(solution)/shard_map/ppermute | solution.py:430
  110.9 4.3 %collective-permute-start.2 = (bf16[64,256]{1,0:T(8,128)(2,1)S(1)}, bf16[64,256]{1,0:T(8,128)(2,1)S(1)}, u32[]{:S(2)}, u32[]{:S(2)}) collective-permute-start(bf16[64,256]{1,0:T(8,128)(2,1)S(1)} %get-tuple-element.19), channel_id=1, source_target_pairs={{0,4},{1,5},{2,6},{3,7},{4,0},{5,1},{6,2},{7,3},{8,12},{9,13},{10,... | collective-permute-start | bytes 98312 | tf_op jit(solution)/shard_map/ppermute | solution.py:430
  113.5 3.1 %collective-permute-start.3 = (bf16[64,256]{1,0:T(8,128)(2,1)S(1)}, bf16[64,256]{1,0:T(8,128)(2,1)S(1)}, u32[]{:S(2)}, u32[]{:S(2)}) collective-permute-start(bf16[64,256]{1,0:T(8,128)(2,1)S(1)} %get-tuple-element.20), channel_id=1, source_target_pairs={{0,6},{1,7},{2,0},{3,1},{4,2},{5,3},{6,4},{7,5},{8,14},{9,15},{10,... | collective-permute-start | bytes 98312 | tf_op jit(solution)/shard_map/ppermute | solution.py:430

commit v5 on v4

--- a/solution.py
+++ b/solution.py
@@ -1,3 +1,4 @@
+import functools
 import math
 
 import jax
@@ -53,10 +54,8 @@
     return inner, outer.reshape(2 * RADIX, SUB).astype(np.float32)
 
 
-def request_kernel(slots_ref, pairs_ref, wanted_ref, places_ref):
+def request_kernel(windows, stations, slots_ref, pairs_ref, wanted_ref, places_ref):
     ends = 2 * pairs_ref.shape[1]
-    windows = wanted_ref.shape[1] // CAP
-    stations = wanted_ref.shape[2] // windows
     owners_count = wanted_ref.shape[0]
     sublane = lax.broadcasted_iota(jnp.int32, (ends, ends), 0)
     lane = lax.broadcasted_iota(jnp.int32, (ends, ends), 1)
@@ -79,34 +78,26 @@
     owner_column = slot_column // stations
     owner_row = slot_row // stations
     same_owner = owner_column == owner_row
-    rank_row = jnp.sum(
-        jnp.where(same_owner & (sublane < lane), 1.0, 0.0), axis=0, keepdims=True
-    ).astype(jnp.int32)
     rank_column = jnp.sum(
         jnp.where(same_owner & (lane < sublane), 1.0, 0.0), axis=1, keepdims=True
     ).astype(jnp.int32)
     places_ref[...] = jnp.broadcast_to(owner_column * (windows * CAP) + rank_column, places_ref.shape)
-    row_keys = owner_row * (windows * CAP) + rank_row
-    slots = owners_count * windows * CAP
-    slot_ids = lax.broadcasted_iota(jnp.int32, (slots, ends), 0)
-    slot_windows = slot_ids // CAP % windows
-    local_column = slot_column - owner_column * stations
-    picks = None
-    for window in range(windows):
-        hit = (slot_ids == row_keys + window * CAP) & (slot_windows == window)
-        columns = lax.broadcasted_iota(jnp.int32, (ends, windows * stations), 1)
-        rows = jnp.where(columns == local_column + window * stations, 1.0, 0.0).astype(jnp.bfloat16)
-        term = jnp.dot(jnp.where(hit, 1.0, 0.0).astype(jnp.bfloat16), rows, preferred_element_type=jnp.float32)
-        picks = term if picks is None else picks + term
-    wanted_ref[...] = picks.astype(jnp.bfloat16).reshape(wanted_ref.shape)
+    local_column = (slot_column - owner_column * stations).astype(jnp.float32)
+    owned = lax.broadcasted_iota(jnp.int32, (owners_count, ends), 0) == owner_row
+    ranked = jnp.where(lane == rank_column, jnp.broadcast_to(local_column, (ends, ends)), 0.0)
+    wanted_ref[...] = jnp.dot(
+        jnp.where(owned, 1.0, 0.0).astype(jnp.bfloat16),
+        ranked.astype(jnp.bfloat16),
+        preferred_element_type=jnp.float32,
+    )
 
 
 def requests(station_slot, pair_stations, blocks, windows, stations):
     pair_count = pair_stations.shape[0]
     return pl.pallas_call(
-        request_kernel,
+        functools.partial(request_kernel, windows, stations),
         out_shape=(
-            jax.ShapeDtypeStruct((blocks, windows * CAP, windows * stations), jnp.bfloat16),
+            jax.ShapeDtypeStruct((blocks, 128), jnp.float32),
             jax.ShapeDtypeStruct((2 * pair_count, 128), jnp.int32),
         ),
         name="requests",
@@ -218,28 +209,53 @@
     return [pltpu.with_memory_space_constraint(array, pltpu.HBM) for array in arrays]
 
 
-def gather_kernel(picks_ref, whitened_ref, rows_ref):
-    rows_ref[...] = jnp.dot(picks_ref[...], whitened_ref[...], preferred_element_type=jnp.float32).astype(
-        rows_ref.dtype
+def gather_kernel(windows, wanted_ref, whitened_ref, rows_hbm, picks_ref, rows_ref, semaphores):
+    slots = rows_ref.shape[0]
+    owners, lanes_count = wanted_ref.shape
+    stations = whitened_ref.shape[0] // windows
+    owner_of = lax.broadcasted_iota(jnp.int32, (slots, owners), 0) // (windows * CAP)
+    spread = jnp.where(owner_of == lax.broadcasted_iota(jnp.int32, (slots, owners), 1), 1.0, 0.0)
+    lists = jnp.dot(
+        spread.astype(jnp.bfloat16), wanted_ref[...].astype(jnp.bfloat16), preferred_element_type=jnp.float32
     )
-
-
-def gathered(picks, whitened):
-    slots, rows = picks.shape
+    slot_ids = lax.broadcasted_iota(jnp.int32, (slots, lanes_count), 0)
+    lanes = lax.broadcasted_iota(jnp.int32, (slots, lanes_count), 1)
+    row_wanted = jnp.sum(jnp.where(lanes == slot_ids % CAP, lists, 0.0), axis=1, keepdims=True)
+    source = row_wanted.astype(jnp.int32) + slot_ids // CAP % windows * stations
+    picks_ref[...] = jnp.where(lanes == source, 1.0, 0.0).astype(picks_ref.dtype)
+    chunk = slots // GATHER_CHUNKS
+    copies = []
+    for index in range(GATHER_CHUNKS):
+        rows = pl.ds(index * chunk, chunk)
+        rows_ref[rows] = jnp.dot(
+            picks_ref[rows], whitened_ref[...], preferred_element_type=jnp.float32
+        ).astype(rows_ref.dtype)
+        copies.append(pltpu.make_async_copy(rows_ref.at[rows], rows_hbm.at[rows], semaphores.at[index]))
+        copies[-1].start()
+    for copy in copies:
+        copy.wait()
+
+
+GATHER_CHUNKS = 8
+
+
+def gathered(wanted, whitened, windows):
+    slots = wanted.shape[0] * windows * CAP
+    shape = (slots, whitened.shape[1])
+    vmem = pl.BlockSpec(memory_space=pltpu.VMEM)
     return pl.pallas_call(
-        gather_kernel,
-        out_shape=pltpu.HBM((slots, whitened.shape[1]), whitened.dtype),
-        grid=(slots // 128,),
-        in_specs=[
-            pl.BlockSpec((128, rows), lambda s: (s, 0)),
-            pl.BlockSpec(whitened.shape, lambda s: (0, 0)),
+        functools.partial(gather_kernel, windows),
+        out_shape=pltpu.HBM(shape, whitened.dtype),
+        in_specs=[vmem, vmem],
+        out_specs=pl.BlockSpec(memory_space=pltpu.HBM),
+        scratch_shapes=[
+            pltpu.VMEM((slots, whitened.shape[0]), whitened.dtype),
+            pltpu.VMEM(shape, whitened.dtype),
+            pltpu.SemaphoreType.DMA((GATHER_CHUNKS,)),
         ],
-        out_specs=pl.BlockSpec((128, whitened.shape[1]), lambda s: (s, 0)),
-        compiler_params=pltpu.CompilerParams(
-            dimension_semantics=("arbitrary",), vmem_limit_bytes=16 << 20
-        ),
+        compiler_params=pltpu.CompilerParams(vmem_limit_bytes=16 << 20),
         name="gathered",
-    )(picks, whitened)
+    )(wanted, whitened)
 
 
 PART_ROWS = 32
@@ -445,9 +461,9 @@
     own = lax.axis_index("tm")
     place = jnp.stack([own // 2, own % 2]).astype(jnp.int32)
     wanted, places = requests(station_slot, pair_stations, blocks, window_count, station_count)
-    picks = lax.all_to_all(wanted, "pairs", split_axis=0, concat_axis=0, tiled=True)
+    lists = lax.all_to_all(wanted[:, None, :], "pairs", split_axis=0, concat_axis=0, tiled=True)
     whitened = whitened_spectra(traces.reshape(window_count * station_count, length))
-    rows = gathered(picks.reshape(slots, window_count * station_count), whitened)
+    rows = gathered(lists.reshape(wanted.shape), whitened, window_count)
     received = lax.all_to_all(
         rows.reshape(blocks, window_count * CAP, 2 * F), "pairs", split_axis=0, concat_axis=0, tiled=True
     )

time: 117 us -> 117 us (level)
  no operation moved by 1% of the time
where the time goes in v5:
time: 117 us; the launch traced here: 116 us
  waiting for transfers between devices  78.2 us (67%)
  starting transfers between devices  26.6 us (23%)
  Pallas kernels  11.4 us (10%)
    all_to_all x1, waiting for transfers between devices, on_device(): lax.all_to_all(rows.reshape(blocks, window_count * CAP, 2 * F), 'pairs',...  71.1 us
    all_to_all x1, starting transfers between devices, on_device(): lax.all_to_all(wanted[:, None, :], 'pairs', split_axis=0, concat_axis=0,...  11.9 us
    all_to_all x1, starting transfers between devices, on_device(): lax.all_to_all(rows.reshape(blocks, window_count * CAP, 2 * F), 'pairs',...  5.2 us
    ppermute x3, starting transfers between devices, window_total(): arrived.append(lax.ppermute(values, 'tm', targets))  5.07 us
    ppermute x1, starting transfers between devices, window_total(): got = lax.ppermute(sent, 'tm', [(source, source ^ 1) for source in devices])  4.47 us
    pallas_call x1, Pallas kernels, whitened_spectra(): pl.pallas_call(spectrum_kernel, out_shape=jax.ShapeDtypeStruct((total, 2...  4.44 us
    all_to_all x1, waiting for transfers between devices, on_device(): lax.all_to_all(wanted[:, None, :], 'pairs', split_axis=0, concat_axis=0,...  4.19 us
  transfers between devices with their start and end apart: 6, of which 5 were waited for; matrix products, arithmetic and copies ran while one was open for 0% of the time, Pallas kernels for 4%

profile of v5, /device:TPU:1, one launch (start us, length us, event | category | flops | bytes accessed | tf_op | source)
XLA Modules:
  0.0 116.5 jit_solution(16662364841065058193)
XLA Ops:
  0.0 1.9 %requests.1 = (f32[32,128]{1,0:T(8,128)}, s32[128,128]{1,0:T(8,128)}) custom-call(s32[16,128]{1,0:T(8,128)} %bitcast.17, s32[2,64]{1,0:T(2,128)} %bitcast.18), custom_call_target="tpu_custom_call" | custom-call | tf_op jit(solution)/shard_map/requests/pallas_call | solution.py:97
  1.9 11.9 %all-to-all-start = ((f32[32,1,128]{2,1,0:T(1,128)}), f32[32,1,128]{2,1,0:T(1,128)S(1)}, u32[]{:S(2)}, u32[]{:S(2)}) async-start(f32[32,1,128]{2,1,0:T(1,128)} %bitcast.16), calls=%async_computation | async-start | bytes 32768 | tf_op jit(solution)/shard_map/all_to_all | solution.py:464
  13.8 4.4 %whitened_spectra.1.whitened_ref = bf16[128,3072]{1,0:T(8,128)(2,1)S(1)} custom-call(f32[128,6144]{1,0:T(8,128)} %bitcast.15, f32[1,6144]{1,0:T(1,128)} %constant.38.clone.hann_ref, f32[24,512]{1,0:T(8,128)} %constant.39.clone.turns_ref, bf16[1024,256]{1,0:T(8,128)(2,1)} %constant.40.clone.table_ref), custom_call_target="tpu_custom_call" | custom-call | flops 805306368 | bytes 5000000 | tf_op jit(solution)/shard_map/whitened_spectra/pallas_call | solution.py:273
  18.2 4.2 %all-to-all-done = f32[32,1,128]{2,1,0:T(1,128)S(1)} async-done(((f32[32,1,128]{2,1,0:T(1,128)}), f32[32,1,128]{2,1,0:T(1,128)S(1)}, u32[]{:S(2)}, u32[]{:S(2)}) %all-to-all-start) | async-done | bytes 16416 | tf_op jit(solution)/shard_map/all_to_all | solution.py:464
  22.4 2.2 %gathered.1 = bf16[512,3072]{1,0:T(8,128)(2,1)} custom-call(f32[32,128]{1,0:T(8,128)S(1)} %bitcast.13, bf16[128,3072]{1,0:T(8,128)(2,1)S(1)} %whitened_spectra.1.whitened_ref), custom_call_target="tpu_custom_call" | custom-call | tf_op jit(solution)/shard_map/gathered/pallas_call | solution.py:246
  24.6 0.0 copy-start
  24.6 0.0 copy-start.1
  24.6 0.0 copy-start.2
  24.7 5.2 %all-to-all-start.1 = ((bf16[32,16,3072]{2,1,0:T(8,128)(2,1)}), bf16[32,16,3072]{2,1,0:T(8,128)(2,1)S(1)}, u32[]{:S(2)}, u32[]{:S(2)}) async-start(bf16[32,16,3072]{2,1,0:T(8,128)(2,1)} %bitcast.14), calls=%async_computation.1 | async-start | bytes 6291456 | tf_op jit(solution)/shard_map/all_to_all | solution.py:467
  29.9 0.1 pad_add_fusion.place_ref
  30.0 71.1 %all-to-all-done.1 = bf16[32,16,3072]{2,1,0:T(8,128)(2,1)S(1)} async-done(((bf16[32,16,3072]{2,1,0:T(8,128)(2,1)}), bf16[32,16,3072]{2,1,0:T(8,128)(2,1)S(1)}, u32[]{:S(2)}, u32[]{:S(2)}) %all-to-all-start.1) | async-done | bytes 3145760 | tf_op jit(solution)/shard_map/all_to_all | solution.py:467
  101.0 0.0 copy-done
  101.0 0.0 copy-done.1
  101.1 0.0 copy-done.2
  101.1 2.2 %lag_sums.1 = (f32[4,64,256]{2,1,0:T(8,128)S(1)}, bf16[4,64,256]{2,1,0:T(8,128)(2,1)S(1)}) custom-call(s32[2]{0:T(128)S(1)} %pad_add_fusion.place_ref, s32[128,128]{1,0:T(8,128)S(1)} %copy-done.1, bf16[512,3072]{1,0:T(8,128)(2,1)S(1)} %bitcast.12, bf16[256,256]{1,0:T(8,128)(2,1)S(1)} %copy-done, f32[24,512]{1,0:T(8,128)S(1)} %copy-done.2), custom_call_target="tpu_custom_call" | custom-call | flops 805306368 | bytes 5000000 | tf_op jit(solution)/shard_map/lag_sums/pallas_call | solution.py:396
  103.3 4.5 %collective-permute-start = (bf16[4,64,256]{2,1,0:T(8,128)(2,1)S(1)}, bf16[4,64,256]{2,1,0:T(8,128)(2,1)S(1)}, u32[]{:S(2)}, u32[]{:S(2)}) collective-permute-start(bf16[4,64,256]{2,1,0:T(8,128)(2,1)S(1)} %get-tuple-element.16), channel_id=1, source_target_pairs={{0,1},{1,0},{2,3},{3,2},{4,5},{5,4},{6,7},{7,6},{8,9},{9,8},{10,11... | collective-permute-start | bytes 393224 | tf_op jit(solution)/shard_map/ppermute | solution.py:434
  107.8 1.0 collective-permute-done.got_ref
  108.8 1.4 %collective-permute-start.1 = (bf16[64,256]{1,0:T(8,128)(2,1)S(1)}, bf16[64,256]{1,0:T(8,128)(2,1)S(1)}, u32[]{:S(2)}, u32[]{:S(2)}) collective-permute-start(bf16[64,256]{1,0:T(8,128)(2,1)S(1)} %get-tuple-element.18), channel_id=1, source_target_pairs={{0,2},{1,3},{2,4},{3,5},{4,6},{5,7},{6,0},{7,1},{8,10},{9,11},{10,... | collective-permute-start | bytes 98312 | tf_op jit(solution)/shard_map/ppermute | solution.py:446
  110.1 2.6 %collective-permute-start.2 = (bf16[64,256]{1,0:T(8,128)(2,1)S(1)}, bf16[64,256]{1,0:T(8,128)(2,1)S(1)}, u32[]{:S(2)}, u32[]{:S(2)}) collective-permute-start(bf16[64,256]{1,0:T(8,128)(2,1)S(1)} %get-tuple-element.19), channel_id=1, source_target_pairs={{0,4},{1,5},{2,6},{3,7},{4,0},{5,1},{6,2},{7,3},{8,12},{9,13},{10,... | collective-permute-start | bytes 98312 | tf_op jit(solution)/shard_map/ppermute | solution.py:446
  112.8 1.1 collective-permute-start.3
  113.8 0.0 collective-permute-done.1.rest_0_
  113.8 0.6 collective-permute-done.2.rest_1_
  114.4 1.4 %collective-permute-done.3.rest_2_ = bf16[64,256]{1,0:T(8,128)(2,1)S(1)} collective-permute-done((bf16[64,256]{1,0:T(8,128)(2,1)S(1)}, bf16[64,256]{1,0:T(8,128)(2,1)S(1)}, u32[]{:S(2)}, u32[]{:S(2)}) %collective-permute-start.3) | collective-permute-done | bytes 32800 | tf_op jit(solution)/shard_map/ppermute | solution.py:446
  115.8 0.6 window_total.1
  (1 shorter events, 0.0 us)
Async XLA Ops:
  1.9 20.5 %all-to-all-start = ((f32[32,1,128]{2,1,0:T(1,128)}), f32[32,1,128]{2,1,0:T(1,128)S(1)}, u32[]{:S(2)}, u32[]{:S(2)}) async-start(f32[32,1,128]{2,1,0:T(1,128)} %bitcast.16), calls=%async_computation | async-start | bytes 32768 | tf_op jit(solution)/shard_map/all_to_all | solution.py:464
  24.6 76.4 %copy-start = (bf16[256,256]{1,0:T(8,128)(2,1)S(1)}, bf16[256,256]{1,0:T(8,128)(2,1)}, u32[]{:S(2)}) copy-start(bf16[256,256]{1,0:T(8,128)(2,1)} %constant.41.clone.inner_ref) | copy-start | bytes 393220
  24.6 76.4 %copy-start.1 = (s32[128,128]{1,0:T(8,128)S(1)}, s32[128,128]{1,0:T(8,128)}, u32[]{:S(2)}) copy-start(s32[128,128]{1,0:T(8,128)} %get-tuple-element.13.places_ref) | copy-start | bytes 196612
  24.6 76.4 %copy-start.2 = (f32[24,512]{1,0:T(8,128)S(1)}, f32[24,512]{1,0:T(8,128)}, u32[]{:S(2)}) copy-start(f32[24,512]{1,0:T(8,128)} %constant.42.clone.outer_ref) | copy-start | bytes 147460
  24.7 76.4 %all-to-all-start.1 = ((bf16[32,16,3072]{2,1,0:T(8,128)(2,1)}), bf16[32,16,3072]{2,1,0:T(8,128)(2,1)S(1)}, u32[]{:S(2)}, u32[]{:S(2)}) async-start(bf16[32,16,3072]{2,1,0:T(8,128)(2,1)} %bitcast.14), calls=%async_computation.1 | async-start | bytes 6291456 | tf_op jit(solution)/shard_map/all_to_all | solution.py:467
  103.3 5.5 %collective-permute-start = (bf16[4,64,256]{2,1,0:T(8,128)(2,1)S(1)}, bf16[4,64,256]{2,1,0:T(8,128)(2,1)S(1)}, u32[]{:S(2)}, u32[]{:S(2)}) collective-permute-start(bf16[4,64,256]{2,1,0:T(8,128)(2,1)S(1)} %get-tuple-element.16), channel_id=1, source_target_pairs={{0,1},{1,0},{2,3},{3,2},{4,5},{5,4},{6,7},{7,6},{8,9},{9,8},{10,11... | collective-permute-start | bytes 393224 | tf_op jit(solution)/shard_map/ppermute | solution.py:434
  108.8 5.1 %collective-permute-start.1 = (bf16[64,256]{1,0:T(8,128)(2,1)S(1)}, bf16[64,256]{1,0:T(8,128)(2,1)S(1)}, u32[]{:S(2)}, u32[]{:S(2)}) collective-permute-start(bf16[64,256]{1,0:T(8,128)(2,1)S(1)} %get-tuple-element.18), channel_id=1, source_target_pairs={{0,2},{1,3},{2,4},{3,5},{4,6},{5,7},{6,0},{7,1},{8,10},{9,11},{10,... | collective-permute-start | bytes 98312 | tf_op jit(solution)/shard_map/ppermute | solution.py:446
  110.1 4.3 %collective-permute-start.2 = (bf16[64,256]{1,0:T(8,128)(2,1)S(1)}, bf16[64,256]{1,0:T(8,128)(2,1)S(1)}, u32[]{:S(2)}, u32[]{:S(2)}) collective-permute-start(bf16[64,256]{1,0:T(8,128)(2,1)S(1)} %get-tuple-element.19), channel_id=1, source_target_pairs={{0,4},{1,5},{2,6},{3,7},{4,0},{5,1},{6,2},{7,3},{8,12},{9,13},{10,... | collective-permute-start | bytes 98312 | tf_op jit(solution)/shard_map/ppermute | solution.py:446
  112.8 3.0 %collective-permute-start.3 = (bf16[64,256]{1,0:T(8,128)(2,1)S(1)}, bf16[64,256]{1,0:T(8,128)(2,1)S(1)}, u32[]{:S(2)}, u32[]{:S(2)}) collective-permute-start(bf16[64,256]{1,0:T(8,128)(2,1)S(1)} %get-tuple-element.20), channel_id=1, source_target_pairs={{0,6},{1,7},{2,0},{3,1},{4,2},{5,3},{6,4},{7,5},{8,14},{9,15},{10,... | collective-permute-start | bytes 98312 | tf_op jit(solution)/shard_map/ppermute | solution.py:446

commit v6 on v5

--- a/solution.py
+++ b/solution.py
@@ -462,6 +462,7 @@
     place = jnp.stack([own // 2, own % 2]).astype(jnp.int32)
     wanted, places = requests(station_slot, pair_stations, blocks, window_count, station_count)
     lists = lax.all_to_all(wanted[:, None, :], "pairs", split_axis=0, concat_axis=0, tiled=True)
+    traces, lists = lax.optimization_barrier((traces, lists))
     whitened = whitened_spectra(traces.reshape(window_count * station_count, length))
     rows = gathered(lists.reshape(wanted.shape), whitened, window_count)
     received = lax.all_to_all(

time: 117 us -> 120 us (1.026)
  blocking collectives: 0 us -> 20.5 us
  starting transfers between devices: 26.6 us -> 14.4 us
  waiting for transfers between devices: 78.2 us -> 73.4 us
    all_to_all x0 -> x1, blocking collectives: none -> 20.5 us  [on_device(): lax.all_to_all(wanted[:, None, :], 'pairs', split_axis=0, concat_axis=0,...]
    all_to_all x1 -> x0, starting transfers between devices: 11.9 us -> none  [on_device(): lax.all_to_all(wanted[:, None, :], 'pairs', split_axis=0, concat_axis=0,...]
    all_to_all x1 -> x0, waiting for transfers between devices: 4.19 us -> none  [on_device(): lax.all_to_all(wanted[:, None, :], 'pairs', split_axis=0, concat_axis=0,...]
  transfers between devices with their start and end apart: 6 -> 5, of which waited for: 5 -> 4; matrix products, arithmetic and copies ran while one was open for 0% -> 0% of each run, Pallas kernels for 4% -> 0%
where the time goes in v6:
time: 120 us
  waiting for transfers between devices  73.4 us (61%)
  blocking collectives  20.5 us (17%)
  starting transfers between devices  14.4 us (12%)
  Pallas kernels  11.4 us (10%)
    all_to_all x1, waiting for transfers between devices, on_device(): lax.all_to_all(rows.reshape(blocks, window_count * CAP, 2 * F), 'pairs',...  70.5 us
    all_to_all x1, blocking collectives, on_device(): lax.all_to_all(wanted[:, None, :], 'pairs', split_axis=0, concat_axis=0,...  20.5 us
    ppermute x3, starting transfers between devices, window_total(): arrived.append(lax.ppermute(values, 'tm', targets))  5.08 us
    ppermute x1, starting transfers between devices, window_total(): got = lax.ppermute(sent, 'tm', [(source, source ^ 1) for source in devices])  5.07 us
    pallas_call x1, Pallas kernels, whitened_spectra(): pl.pallas_call(spectrum_kernel, out_shape=jax.ShapeDtypeStruct((total, 2...  4.42 us
    all_to_all x1, starting transfers between devices, on_device(): lax.all_to_all(rows.reshape(blocks, window_count * CAP, 2 * F), 'pairs',...  4.21 us
  transfers between devices with their start and end apart: 5, of which 4 were waited for; matrix products, arithmetic and copies ran while one was open for 0% of the time, Pallas kernels for 0%

profile of v6, /device:TPU:1, one launch (start us, length us, event | category | flops | bytes accessed | tf_op | source)
XLA Modules:
  0.0 119.9 jit_solution(12033760068245495111)
XLA Ops:
  0.0 1.9 %requests.1 = (f32[32,128]{1,0:T(8,128)}, s32[128,128]{1,0:T(8,128)}) custom-call(s32[16,128]{1,0:T(8,128)} %bitcast.17, s32[2,64]{1,0:T(2,128)} %bitcast.18), custom_call_target="tpu_custom_call" | custom-call | tf_op jit(solution)/shard_map/requests/pallas_call | solution.py:97
  1.9 20.5 %all_to_all.10 = f32[32,1,128]{2,1,0:T(1,128)S(1)} all-to-all(f32[32,1,128]{2,1,0:T(1,128)} %bitcast.16), channel_id=1, replica_groups=mesh['pairs'=32,'tm'=8] {'pairs'}, dimensions={0} | all-to-all | bytes 32768 | tf_op jit(solution)/shard_map/all_to_all | solution.py:464
  22.4 4.4 %whitened_spectra.1.whitened_ref = bf16[128,3072]{1,0:T(8,128)(2,1)S(1)} custom-call(f32[128,6144]{1,0:T(8,128)} %bitcast.15, f32[1,6144]{1,0:T(1,128)} %constant.38.clone.hann_ref, f32[24,512]{1,0:T(8,128)} %constant.39.clone.turns_ref, bf16[1024,256]{1,0:T(8,128)(2,1)} %constant.40.clone.table_ref), custom_call_target="tpu_custom_call" | custom-call | flops 805306368 | bytes 5000000 | tf_op jit(solution)/shard_map/whitened_spectra/pallas_call | solution.py:273
  26.8 2.2 %gathered.1 = bf16[512,3072]{1,0:T(8,128)(2,1)} custom-call(f32[32,128]{1,0:T(8,128)S(1)} %bitcast.13, bf16[128,3072]{1,0:T(8,128)(2,1)S(1)} %whitened_spectra.1.whitened_ref), custom_call_target="tpu_custom_call" | custom-call | tf_op jit(solution)/shard_map/gathered/pallas_call | solution.py:246
  29.0 0.0 copy-start
  29.0 0.0 copy-start.1
  29.0 0.0 copy-start.2
  29.0 4.2 %all-to-all-start.1 = ((bf16[32,16,3072]{2,1,0:T(8,128)(2,1)}), bf16[32,16,3072]{2,1,0:T(8,128)(2,1)S(1)}, u32[]{:S(2)}, u32[]{:S(2)}) async-start(bf16[32,16,3072]{2,1,0:T(8,128)(2,1)} %bitcast.14), calls=%async_computation.1 | async-start | bytes 6291456 | tf_op jit(solution)/shard_map/all_to_all | solution.py:468
  33.3 0.1 pad_add_fusion.place_ref
  33.4 70.5 %all-to-all-done.1 = bf16[32,16,3072]{2,1,0:T(8,128)(2,1)S(1)} async-done(((bf16[32,16,3072]{2,1,0:T(8,128)(2,1)}), bf16[32,16,3072]{2,1,0:T(8,128)(2,1)S(1)}, u32[]{:S(2)}, u32[]{:S(2)}) %all-to-all-start.1) | async-done | bytes 3145760 | tf_op jit(solution)/shard_map/all_to_all | solution.py:468
  103.8 0.0 copy-done
  103.8 0.0 copy-done.1
  103.8 0.0 copy-done.2
  103.8 2.2 %lag_sums.1 = (f32[4,64,256]{2,1,0:T(8,128)S(1)}, bf16[4,64,256]{2,1,0:T(8,128)(2,1)S(1)}) custom-call(s32[2]{0:T(128)S(1)} %pad_add_fusion.place_ref, s32[128,128]{1,0:T(8,128)S(1)} %copy-done.1, bf16[512,3072]{1,0:T(8,128)(2,1)S(1)} %bitcast.12, bf16[256,256]{1,0:T(8,128)(2,1)S(1)} %copy-done, f32[24,512]{1,0:T(8,128)S(1)} %copy-done.2), custom_call_target="tpu_custom_call" | custom-call | flops 805306368 | bytes 5000000 | tf_op jit(solution)/shard_map/lag_sums/pallas_call | solution.py:396
  106.1 5.1 %collective-permute-start = (bf16[4,64,256]{2,1,0:T(8,128)(2,1)S(1)}, bf16[4,64,256]{2,1,0:T(8,128)(2,1)S(1)}, u32[]{:S(2)}, u32[]{:S(2)}) collective-permute-start(bf16[4,64,256]{2,1,0:T(8,128)(2,1)S(1)} %get-tuple-element.20), channel_id=1, source_target_pairs={{0,1},{1,0},{2,3},{3,2},{4,5},{5,4},{6,7},{7,6},{8,9},{9,8},{10,11... | collective-permute-start | bytes 393224 | tf_op jit(solution)/shard_map/ppermute | solution.py:434
  111.2 1.0 collective-permute-done.got_ref
  112.2 1.4 %collective-permute-start.1 = (bf16[64,256]{1,0:T(8,128)(2,1)S(1)}, bf16[64,256]{1,0:T(8,128)(2,1)S(1)}, u32[]{:S(2)}, u32[]{:S(2)}) collective-permute-start(bf16[64,256]{1,0:T(8,128)(2,1)S(1)} %get-tuple-element.22), channel_id=1, source_target_pairs={{0,2},{1,3},{2,4},{3,5},{4,6},{5,7},{6,0},{7,1},{8,10},{9,11},{10,... | collective-permute-start | bytes 98312 | tf_op jit(solution)/shard_map/ppermute | solution.py:446
  113.5 2.6 %collective-permute-start.2 = (bf16[64,256]{1,0:T(8,128)(2,1)S(1)}, bf16[64,256]{1,0:T(8,128)(2,1)S(1)}, u32[]{:S(2)}, u32[]{:S(2)}) collective-permute-start(bf16[64,256]{1,0:T(8,128)(2,1)S(1)} %get-tuple-element.23), channel_id=1, source_target_pairs={{0,4},{1,5},{2,6},{3,7},{4,0},{5,1},{6,2},{7,3},{8,12},{9,13},{10,... | collective-permute-start | bytes 98312 | tf_op jit(solution)/shard_map/ppermute | solution.py:446
  116.2 1.1 collective-permute-start.3
  117.3 0.0 collective-permute-done.1.rest_0_
  117.3 0.6 collective-permute-done.2.rest_1_
  117.8 1.4 %collective-permute-done.3.rest_2_ = bf16[64,256]{1,0:T(8,128)(2,1)S(1)} collective-permute-done((bf16[64,256]{1,0:T(8,128)(2,1)S(1)}, bf16[64,256]{1,0:T(8,128)(2,1)S(1)}, u32[]{:S(2)}, u32[]{:S(2)}) %collective-permute-start.3) | collective-permute-done | bytes 32800 | tf_op jit(solution)/shard_map/ppermute | solution.py:446
  119.2 0.6 window_total.1
  (1 shorter events, 0.0 us)
Async XLA Ops:
  29.0 74.8 %copy-start = (bf16[256,256]{1,0:T(8,128)(2,1)S(1)}, bf16[256,256]{1,0:T(8,128)(2,1)}, u32[]{:S(2)}) copy-start(bf16[256,256]{1,0:T(8,128)(2,1)} %constant.41.clone.inner_ref) | copy-start | bytes 393220
  29.0 74.8 %copy-start.1 = (s32[128,128]{1,0:T(8,128)S(1)}, s32[128,128]{1,0:T(8,128)}, u32[]{:S(2)}) copy-start(s32[128,128]{1,0:T(8,128)} %get-tuple-element.15.places_ref) | copy-start | bytes 196612
  29.0 74.8 %copy-start.2 = (f32[24,512]{1,0:T(8,128)S(1)}, f32[24,512]{1,0:T(8,128)}, u32[]{:S(2)}) copy-start(f32[24,512]{1,0:T(8,128)} %constant.42.clone.outer_ref) | copy-start | bytes 147460
  29.0 74.8 %all-to-all-start.1 = ((bf16[32,16,3072]{2,1,0:T(8,128)(2,1)}), bf16[32,16,3072]{2,1,0:T(8,128)(2,1)S(1)}, u32[]{:S(2)}, u32[]{:S(2)}) async-start(bf16[32,16,3072]{2,1,0:T(8,128)(2,1)} %bitcast.14), calls=%async_computation.1 | async-start | bytes 6291456 | tf_op jit(solution)/shard_map/all_to_all | solution.py:468
  106.1 6.1 %collective-permute-start = (bf16[4,64,256]{2,1,0:T(8,128)(2,1)S(1)}, bf16[4,64,256]{2,1,0:T(8,128)(2,1)S(1)}, u32[]{:S(2)}, u32[]{:S(2)}) collective-permute-start(bf16[4,64,256]{2,1,0:T(8,128)(2,1)S(1)} %get-tuple-element.20), channel_id=1, source_target_pairs={{0,1},{1,0},{2,3},{3,2},{4,5},{5,4},{6,7},{7,6},{8,9},{9,8},{10,11... | collective-permute-start | bytes 393224 | tf_op jit(solution)/shard_map/ppermute | solution.py:434
  112.2 5.1 %collective-permute-start.1 = (bf16[64,256]{1,0:T(8,128)(2,1)S(1)}, bf16[64,256]{1,0:T(8,128)(2,1)S(1)}, u32[]{:S(2)}, u32[]{:S(2)}) collective-permute-start(bf16[64,256]{1,0:T(8,128)(2,1)S(1)} %get-tuple-element.22), channel_id=1, source_target_pairs={{0,2},{1,3},{2,4},{3,5},{4,6},{5,7},{6,0},{7,1},{8,10},{9,11},{10,... | collective-permute-start | bytes 98312 | tf_op jit(solution)/shard_map/ppermute | solution.py:446
  113.5 4.3 %collective-permute-start.2 = (bf16[64,256]{1,0:T(8,128)(2,1)S(1)}, bf16[64,256]{1,0:T(8,128)(2,1)S(1)}, u32[]{:S(2)}, u32[]{:S(2)}) collective-permute-start(bf16[64,256]{1,0:T(8,128)(2,1)S(1)} %get-tuple-element.23), channel_id=1, source_target_pairs={{0,4},{1,5},{2,6},{3,7},{4,0},{5,1},{6,2},{7,3},{8,12},{9,13},{10,... | collective-permute-start | bytes 98312 | tf_op jit(solution)/shard_map/ppermute | solution.py:446
  116.2 3.0 %collective-permute-start.3 = (bf16[64,256]{1,0:T(8,128)(2,1)S(1)}, bf16[64,256]{1,0:T(8,128)(2,1)S(1)}, u32[]{:S(2)}, u32[]{:S(2)}) collective-permute-start(bf16[64,256]{1,0:T(8,128)(2,1)S(1)} %get-tuple-element.24), channel_id=1, source_target_pairs={{0,6},{1,7},{2,0},{3,1},{4,2},{5,3},{6,4},{7,5},{8,14},{9,15},{10,... | collective-permute-start | bytes 98312 | tf_op jit(solution)/shard_map/ppermute | solution.py:446

commit v7 on v5

--- a/solution.py
+++ b/solution.py
@@ -209,7 +209,7 @@
     return [pltpu.with_memory_space_constraint(array, pltpu.HBM) for array in arrays]
 
 
-def gather_kernel(windows, wanted_ref, whitened_ref, rows_hbm, picks_ref, rows_ref, semaphores):
+def gather_kernel(windows, wanted_ref, whitened_ref, rows_ref):
     slots = rows_ref.shape[0]
     owners, lanes_count = wanted_ref.shape
     stations = whitened_ref.shape[0] // windows
@@ -222,21 +222,15 @@
     lanes = lax.broadcasted_iota(jnp.int32, (slots, lanes_count), 1)
     row_wanted = jnp.sum(jnp.where(lanes == slot_ids % CAP, lists, 0.0), axis=1, keepdims=True)
     source = row_wanted.astype(jnp.int32) + slot_ids // CAP % windows * stations
-    picks_ref[...] = jnp.where(lanes == source, 1.0, 0.0).astype(picks_ref.dtype)
-    chunk = slots // GATHER_CHUNKS
-    copies = []
-    for index in range(GATHER_CHUNKS):
-        rows = pl.ds(index * chunk, chunk)
-        rows_ref[rows] = jnp.dot(
-            picks_ref[rows], whitened_ref[...], preferred_element_type=jnp.float32
+    picks = jnp.where(lanes == source, 1.0, 0.0).astype(whitened_ref.dtype)
+    for start in range(0, rows_ref.shape[1], GATHER_COLUMNS):
+        columns = slice(start, start + GATHER_COLUMNS)
+        rows_ref[:, columns] = jnp.dot(
+            picks, whitened_ref[:, columns], preferred_element_type=jnp.float32
         ).astype(rows_ref.dtype)
-        copies.append(pltpu.make_async_copy(rows_ref.at[rows], rows_hbm.at[rows], semaphores.at[index]))
-        copies[-1].start()
-    for copy in copies:
-        copy.wait()
-
-
-GATHER_CHUNKS = 8
+
+
+GATHER_COLUMNS = 512
 
 
 def gathered(wanted, whitened, windows):
@@ -245,14 +239,9 @@
     vmem = pl.BlockSpec(memory_space=pltpu.VMEM)
     return pl.pallas_call(
         functools.partial(gather_kernel, windows),
-        out_shape=pltpu.HBM(shape, whitened.dtype),
+        out_shape=jax.ShapeDtypeStruct(shape, whitened.dtype),
         in_specs=[vmem, vmem],
-        out_specs=pl.BlockSpec(memory_space=pltpu.HBM),
-        scratch_shapes=[
-            pltpu.VMEM((slots, whitened.shape[0]), whitened.dtype),
-            pltpu.VMEM(shape, whitened.dtype),
-            pltpu.SemaphoreType.DMA((GATHER_CHUNKS,)),
-        ],
+        out_specs=vmem,
         compiler_params=pltpu.CompilerParams(vmem_limit_bytes=16 << 20),
         name="gathered",
     )(wanted, whitened)
@@ -459,9 +448,11 @@
     slots = blocks * window_count * CAP
     normalizer = 1.0 / math.sqrt(F * window_count * lag_parts)
     own = lax.axis_index("tm")
+    wanted, places = requests(station_slot, pair_stations, blocks, window_count, station_count)
+    wanted, own = lax.optimization_barrier((wanted, own))
+    lists = lax.all_to_all(wanted[:, None, :], "pairs", split_axis=0, concat_axis=0, tiled=True)
     place = jnp.stack([own // 2, own % 2]).astype(jnp.int32)
-    wanted, places = requests(station_slot, pair_stations, blocks, window_count, station_count)
-    lists = lax.all_to_all(wanted[:, None, :], "pairs", split_axis=0, concat_axis=0, tiled=True)
+    lists, place = lax.optimization_barrier((lists, place))
     whitened = whitened_spectra(traces.reshape(window_count * station_count, length))
     rows = gathered(lists.reshape(wanted.shape), whitened, window_count)
     received = lax.all_to_all(

time: 117 us -> 115 us (0.983)
  blocking collectives: 0 us -> 74.7 us
  waiting for transfers between devices: 78.2 us -> 7.07 us
  starting transfers between devices: 26.6 us -> 22.1 us
    all_to_all x0 -> x1, blocking collectives: none -> 74.7 us  [on_device(): lax.all_to_all(rows.reshape(blocks, window_count * CAP, 2 * F), 'pairs',...]
    all_to_all x1 -> x0, waiting for transfers between devices: 71.1 us -> none  [on_device(): lax.all_to_all(rows.reshape(blocks, window_count * CAP, 2 * F), 'pairs',...]
    all_to_all x1 -> x0, starting transfers between devices: 5.2 us -> none  [on_device(): lax.all_to_all(rows.reshape(blocks, window_count * CAP, 2 * F), 'pairs',...]
  transfers between devices with their start and end apart: 6 -> 5, of which waited for: 5 -> 4; matrix products, arithmetic and copies ran while one was open for 0% -> 0% of each run, Pallas kernels for 4% -> 4%
where the time goes in v7:
time: 115 us; the launch traced here: 114 us
  blocking collectives  74.7 us (65%)
  starting transfers between devices  22.1 us (19%)
  Pallas kernels  10.4 us (9%)
  waiting for transfers between devices  7.07 us (6%)
    all_to_all x1, blocking collectives, on_device(): lax.all_to_all(rows.reshape(blocks, window_count * CAP, 2 * F), 'pairs',...  74.7 us
    all_to_all x1, starting transfers between devices, on_device(): lax.all_to_all(wanted[:, None, :], 'pairs', split_axis=0, concat_axis=0,...  11.9 us
    ppermute x1, starting transfers between devices, window_total(): got = lax.ppermute(sent, 'tm', [(source, source ^ 1) for source in devices])  5.18 us
    ppermute x3, starting transfers between devices, window_total(): arrived.append(lax.ppermute(values, 'tm', targets))  5.07 us
    pallas_call x1, Pallas kernels, whitened_spectra(): pl.pallas_call(spectrum_kernel, out_shape=jax.ShapeDtypeStruct((total, 2...  4.42 us
    all_to_all x1, waiting for transfers between devices, on_device(): lax.all_to_all(wanted[:, None, :], 'pairs', split_axis=0, concat_axis=0,...  4.1 us
  transfers between devices with their start and end apart: 5, of which 4 were waited for; matrix products, arithmetic and copies ran while one was open for 0% of the time, Pallas kernels for 4%

profile of v7, /device:TPU:1, one launch (start us, length us, event | category | flops | bytes accessed | tf_op | source)
XLA Modules:
  0.0 114.4 jit_solution(3857789226116296793)
XLA Ops:
  0.0 1.9 %requests.1 = (f32[32,128]{1,0:T(8,128)}, s32[128,128]{1,0:T(8,128)}) custom-call(s32[16,128]{1,0:T(8,128)} %bitcast.17, s32[2,64]{1,0:T(2,128)} %bitcast.18), custom_call_target="tpu_custom_call" | custom-call | tf_op jit(solution)/shard_map/requests/pallas_call | solution.py:97
  1.9 11.9 %all-to-all-start = ((f32[32,1,128]{2,1,0:T(1,128)}), f32[32,1,128]{2,1,0:T(1,128)S(1)}, u32[]{:S(2)}, u32[]{:S(2)}) async-start(f32[32,1,128]{2,1,0:T(1,128)} %bitcast.16), calls=%async_computation | async-start | bytes 32768 | tf_op jit(solution)/shard_map/all_to_all | solution.py:453
  13.8 0.1 pad_add_fusion.place_ref
  13.9 4.4 %whitened_spectra.1.whitened_ref = bf16[128,3072]{1,0:T(8,128)(2,1)S(1)} custom-call(f32[128,6144]{1,0:T(8,128)} %bitcast.15, f32[1,6144]{1,0:T(1,128)} %constant.38.clone.hann_ref, f32[24,512]{1,0:T(8,128)} %constant.39.clone.turns_ref, bf16[1024,256]{1,0:T(8,128)(2,1)} %constant.40.clone.table_ref), custom_call_target="tpu_custom_call" | custom-call | flops 805306368 | bytes 5000000 | tf_op jit(solution)/shard_map/whitened_spectra/pallas_call | solution.py:262
  18.3 4.1 %all-to-all-done = f32[32,1,128]{2,1,0:T(1,128)S(1)} async-done(((f32[32,1,128]{2,1,0:T(1,128)}), f32[32,1,128]{2,1,0:T(1,128)S(1)}, u32[]{:S(2)}, u32[]{:S(2)}) %all-to-all-start) | async-done | bytes 16416 | tf_op jit(solution)/shard_map/all_to_all | solution.py:453
  22.4 1.2 %gathered.1 = bf16[512,3072]{1,0:T(8,128)(2,1)S(1)} custom-call(f32[32,128]{1,0:T(8,128)S(1)} %bitcast.14, bf16[128,3072]{1,0:T(8,128)(2,1)S(1)} %whitened_spectra.1.whitened_ref), custom_call_target="tpu_custom_call" | custom-call | tf_op jit(solution)/shard_map/gathered/pallas_call | solution.py:240
  23.6 0.0 copy-start
  23.6 0.0 copy-start.1
  23.6 0.0 copy-start.2
  23.6 74.7 %all_to_all.10 = bf16[32,16,3072]{2,1,0:T(8,128)(2,1)S(1)} all-to-all(bf16[32,16,3072]{2,1,0:T(8,128)(2,1)S(1)} %bitcast.13), channel_id=1, replica_groups=mesh['pairs'=32,'tm'=8] {'pairs'}, dimensions={0} | all-to-all | bytes 6291456 | tf_op jit(solution)/shard_map/all_to_all | solution.py:458
  98.3 0.0 copy-done
  98.3 0.0 copy-done.1
  98.3 0.0 copy-done.2
  98.3 2.2 %lag_sums.1 = (f32[4,64,256]{2,1,0:T(8,128)S(1)}, bf16[4,64,256]{2,1,0:T(8,128)(2,1)S(1)}) custom-call(s32[2]{0:T(128)S(1)} %pad_add_fusion.place_ref, s32[128,128]{1,0:T(8,128)S(1)} %copy-done.1, bf16[512,3072]{1,0:T(8,128)(2,1)S(1)} %bitcast.12, bf16[256,256]{1,0:T(8,128)(2,1)S(1)} %copy-done, f32[24,512]{1,0:T(8,128)S(1)} %copy-done.2), custom_call_target="tpu_custom_call" | custom-call | flops 805306368 | bytes 5000000 | tf_op jit(solution)/shard_map/lag_sums/pallas_call | solution.py:385
  100.5 5.2 %collective-permute-start = (bf16[4,64,256]{2,1,0:T(8,128)(2,1)S(1)}, bf16[4,64,256]{2,1,0:T(8,128)(2,1)S(1)}, u32[]{:S(2)}, u32[]{:S(2)}) collective-permute-start(bf16[4,64,256]{2,1,0:T(8,128)(2,1)S(1)} %get-tuple-element.24), channel_id=1, source_target_pairs={{0,1},{1,0},{2,3},{3,2},{4,5},{5,4},{6,7},{7,6},{8,9},{9,8},{10,11... | collective-permute-start | bytes 393224 | tf_op jit(solution)/shard_map/ppermute | solution.py:423
  105.7 1.0 collective-permute-done.got_ref
  106.7 1.4 %collective-permute-start.1 = (bf16[64,256]{1,0:T(8,128)(2,1)S(1)}, bf16[64,256]{1,0:T(8,128)(2,1)S(1)}, u32[]{:S(2)}, u32[]{:S(2)}) collective-permute-start(bf16[64,256]{1,0:T(8,128)(2,1)S(1)} %get-tuple-element.26), channel_id=1, source_target_pairs={{0,2},{1,3},{2,4},{3,5},{4,6},{5,7},{6,0},{7,1},{8,10},{9,11},{10,... | collective-permute-start | bytes 98312 | tf_op jit(solution)/shard_map/ppermute | solution.py:435
  108.1 2.6 %collective-permute-start.2 = (bf16[64,256]{1,0:T(8,128)(2,1)S(1)}, bf16[64,256]{1,0:T(8,128)(2,1)S(1)}, u32[]{:S(2)}, u32[]{:S(2)}) collective-permute-start(bf16[64,256]{1,0:T(8,128)(2,1)S(1)} %get-tuple-element.27), channel_id=1, source_target_pairs={{0,4},{1,5},{2,6},{3,7},{4,0},{5,1},{6,2},{7,3},{8,12},{9,13},{10,... | collective-permute-start | bytes 98312 | tf_op jit(solution)/shard_map/ppermute | solution.py:435
  110.7 1.1 collective-permute-start.3
  111.8 0.0 collective-permute-done.1.rest_0_
  111.8 0.6 collective-permute-done.2.rest_1_
  112.4 1.4 %collective-permute-done.3.rest_2_ = bf16[64,256]{1,0:T(8,128)(2,1)S(1)} collective-permute-done((bf16[64,256]{1,0:T(8,128)(2,1)S(1)}, bf16[64,256]{1,0:T(8,128)(2,1)S(1)}, u32[]{:S(2)}, u32[]{:S(2)}) %collective-permute-start.3) | collective-permute-done | bytes 32800 | tf_op jit(solution)/shard_map/ppermute | solution.py:435
  113.8 0.6 window_total.1
  (1 shorter events, 0.0 us)
Async XLA Ops:
  1.9 20.5 %all-to-all-start = ((f32[32,1,128]{2,1,0:T(1,128)}), f32[32,1,128]{2,1,0:T(1,128)S(1)}, u32[]{:S(2)}, u32[]{:S(2)}) async-start(f32[32,1,128]{2,1,0:T(1,128)} %bitcast.16), calls=%async_computation | async-start | bytes 32768 | tf_op jit(solution)/shard_map/all_to_all | solution.py:453
  23.6 74.7 %copy-start = (bf16[256,256]{1,0:T(8,128)(2,1)S(1)}, bf16[256,256]{1,0:T(8,128)(2,1)}, u32[]{:S(2)}) copy-start(bf16[256,256]{1,0:T(8,128)(2,1)} %constant.41.clone.inner_ref) | copy-start | bytes 393220
  23.6 74.7 %copy-start.1 = (s32[128,128]{1,0:T(8,128)S(1)}, s32[128,128]{1,0:T(8,128)}, u32[]{:S(2)}) copy-start(s32[128,128]{1,0:T(8,128)} %get-tuple-element.21.places_ref) | copy-start | bytes 196612
  23.6 74.7 %copy-start.2 = (f32[24,512]{1,0:T(8,128)S(1)}, f32[24,512]{1,0:T(8,128)}, u32[]{:S(2)}) copy-start(f32[24,512]{1,0:T(8,128)} %constant.42.clone.outer_ref) | copy-start | bytes 147460
  100.5 6.2 %collective-permute-start = (bf16[4,64,256]{2,1,0:T(8,128)(2,1)S(1)}, bf16[4,64,256]{2,1,0:T(8,128)(2,1)S(1)}, u32[]{:S(2)}, u32[]{:S(2)}) collective-permute-start(bf16[4,64,256]{2,1,0:T(8,128)(2,1)S(1)} %get-tuple-element.24), channel_id=1, source_target_pairs={{0,1},{1,0},{2,3},{3,2},{4,5},{5,4},{6,7},{7,6},{8,9},{9,8},{10,11... | collective-permute-start | bytes 393224 | tf_op jit(solution)/shard_map/ppermute | solution.py:423
  106.7 5.1 %collective-permute-start.1 = (bf16[64,256]{1,0:T(8,128)(2,1)S(1)}, bf16[64,256]{1,0:T(8,128)(2,1)S(1)}, u32[]{:S(2)}, u32[]{:S(2)}) collective-permute-start(bf16[64,256]{1,0:T(8,128)(2,1)S(1)} %get-tuple-element.26), channel_id=1, source_target_pairs={{0,2},{1,3},{2,4},{3,5},{4,6},{5,7},{6,0},{7,1},{8,10},{9,11},{10,... | collective-permute-start | bytes 98312 | tf_op jit(solution)/shard_map/ppermute | solution.py:435
  108.1 4.3 %collective-permute-start.2 = (bf16[64,256]{1,0:T(8,128)(2,1)S(1)}, bf16[64,256]{1,0:T(8,128)(2,1)S(1)}, u32[]{:S(2)}, u32[]{:S(2)}) collective-permute-start(bf16[64,256]{1,0:T(8,128)(2,1)S(1)} %get-tuple-element.27), channel_id=1, source_target_pairs={{0,4},{1,5},{2,6},{3,7},{4,0},{5,1},{6,2},{7,3},{8,12},{9,13},{10,... | collective-permute-start | bytes 98312 | tf_op jit(solution)/shard_map/ppermute | solution.py:435
  110.7 3.1 %collective-permute-start.3 = (bf16[64,256]{1,0:T(8,128)(2,1)S(1)}, bf16[64,256]{1,0:T(8,128)(2,1)S(1)}, u32[]{:S(2)}, u32[]{:S(2)}) collective-permute-start(bf16[64,256]{1,0:T(8,128)(2,1)S(1)} %get-tuple-element.28), channel_id=1, source_target_pairs={{0,6},{1,7},{2,0},{3,1},{4,2},{5,3},{6,4},{7,5},{8,14},{9,15},{10,... | collective-permute-start | bytes 98312 | tf_op jit(solution)/shard_map/ppermute | solution.py:435

commit v8 on v7

--- a/solution.py
+++ b/solution.py
@@ -430,9 +430,10 @@
         name="core_total",
     )(kept, got)
     arrived = []
-    for offset, values in enumerate(onward, 1):
+    farthest_first = sorted(range(1, rings), key=lambda offset: -min(offset, rings - offset))
+    for offset in farthest_first:
         targets = [(source, (source // 2 + offset) % rings * 2 + source % 2) for source in devices]
-        arrived.append(lax.ppermute(values, "tm", targets))
+        arrived.append(lax.ppermute(onward[offset - 1], "tm", targets))
     return pl.pallas_call(
         total_kernel,
         out_shape=jax.ShapeDtypeStruct((pairs, share), jnp.float32),

time: 115 us -> 115 us (level)
  transfers between devices with their start and end apart: 5 -> 5, of which waited for: 4 -> 3; matrix products, arithmetic and copies ran while one was open for 0% -> 0% of each run, Pallas kernels for 4% -> 4%
where the time goes in v8:
time: 115 us; the launch traced here: 114 us
  blocking collectives  74.7 us (65%)
  starting transfers between devices  22.7 us (20%)
  Pallas kernels  10.4 us (9%)
  waiting for transfers between devices  6.39 us (6%)
    all_to_all x1, blocking collectives, on_device(): lax.all_to_all(rows.reshape(blocks, window_count * CAP, 2 * F), 'pairs',...  74.7 us
    all_to_all x1, starting transfers between devices, on_device(): lax.all_to_all(wanted[:, None, :], 'pairs', split_axis=0, concat_axis=0,...  11.9 us
    ppermute x3, starting transfers between devices, window_total(): arrived.append(lax.ppermute(onward[offset - 1], 'tm', targets))  5.68 us
    ppermute x1, starting transfers between devices, window_total(): got = lax.ppermute(sent, 'tm', [(source, source ^ 1) for source in devices])  5.18 us
    pallas_call x1, Pallas kernels, whitened_spectra(): pl.pallas_call(spectrum_kernel, out_shape=jax.ShapeDtypeStruct((total, 2...  4.42 us
    all_to_all x1, waiting for transfers between devices, on_device(): lax.all_to_all(wanted[:, None, :], 'pairs', split_axis=0, concat_axis=0,...  4.1 us
  transfers between devices with their start and end apart: 5, of which 3 were waited for; matrix products, arithmetic and copies ran while one was open for 0% of the time, Pallas kernels for 4%

profile of v8, /device:TPU:1, one launch (start us, length us, event | category | flops | bytes accessed | tf_op | source)
XLA Modules:
  0.0 114.3 jit_solution(17656596987004009577)
XLA Ops:
  0.0 1.9 %requests.1 = (f32[32,128]{1,0:T(8,128)}, s32[128,128]{1,0:T(8,128)}) custom-call(s32[16,128]{1,0:T(8,128)} %bitcast.17, s32[2,64]{1,0:T(2,128)} %bitcast.18), custom_call_target="tpu_custom_call" | custom-call | tf_op jit(solution)/shard_map/requests/pallas_call | solution.py:97
  1.9 11.9 %all-to-all-start = ((f32[32,1,128]{2,1,0:T(1,128)}), f32[32,1,128]{2,1,0:T(1,128)S(1)}, u32[]{:S(2)}, u32[]{:S(2)}) async-start(f32[32,1,128]{2,1,0:T(1,128)} %bitcast.16), calls=%async_computation | async-start | bytes 32768 | tf_op jit(solution)/shard_map/all_to_all | solution.py:454
  13.8 0.1 pad_add_fusion.place_ref
  13.9 4.4 %whitened_spectra.1.whitened_ref = bf16[128,3072]{1,0:T(8,128)(2,1)S(1)} custom-call(f32[128,6144]{1,0:T(8,128)} %bitcast.15, f32[1,6144]{1,0:T(1,128)} %constant.38.clone.hann_ref, f32[24,512]{1,0:T(8,128)} %constant.39.clone.turns_ref, bf16[1024,256]{1,0:T(8,128)(2,1)} %constant.40.clone.table_ref), custom_call_target="tpu_custom_call" | custom-call | flops 805306368 | bytes 5000000 | tf_op jit(solution)/shard_map/whitened_spectra/pallas_call | solution.py:262
  18.3 4.1 %all-to-all-done = f32[32,1,128]{2,1,0:T(1,128)S(1)} async-done(((f32[32,1,128]{2,1,0:T(1,128)}), f32[32,1,128]{2,1,0:T(1,128)S(1)}, u32[]{:S(2)}, u32[]{:S(2)}) %all-to-all-start) | async-done | bytes 16416 | tf_op jit(solution)/shard_map/all_to_all | solution.py:454
  22.4 1.2 %gathered.1 = bf16[512,3072]{1,0:T(8,128)(2,1)S(1)} custom-call(f32[32,128]{1,0:T(8,128)S(1)} %bitcast.14, bf16[128,3072]{1,0:T(8,128)(2,1)S(1)} %whitened_spectra.1.whitened_ref), custom_call_target="tpu_custom_call" | custom-call | tf_op jit(solution)/shard_map/gathered/pallas_call | solution.py:240
  23.6 0.0 copy-start
  23.6 0.0 copy-start.1
  23.6 0.0 copy-start.2
  23.6 74.7 %all_to_all.10 = bf16[32,16,3072]{2,1,0:T(8,128)(2,1)S(1)} all-to-all(bf16[32,16,3072]{2,1,0:T(8,128)(2,1)S(1)} %bitcast.13), channel_id=1, replica_groups=mesh['pairs'=32,'tm'=8] {'pairs'}, dimensions={0} | all-to-all | bytes 6291456 | tf_op jit(solution)/shard_map/all_to_all | solution.py:459
  98.3 0.0 copy-done
  98.3 0.0 copy-done.1
  98.3 0.0 copy-done.2
  98.3 2.2 %lag_sums.1 = (f32[4,64,256]{2,1,0:T(8,128)S(1)}, bf16[4,64,256]{2,1,0:T(8,128)(2,1)S(1)}) custom-call(s32[2]{0:T(128)S(1)} %pad_add_fusion.place_ref, s32[128,128]{1,0:T(8,128)S(1)} %copy-done.1, bf16[512,3072]{1,0:T(8,128)(2,1)S(1)} %bitcast.12, bf16[256,256]{1,0:T(8,128)(2,1)S(1)} %copy-done, f32[24,512]{1,0:T(8,128)S(1)} %copy-done.2), custom_call_target="tpu_custom_call" | custom-call | flops 805306368 | bytes 5000000 | tf_op jit(solution)/shard_map/lag_sums/pallas_call | solution.py:385
  100.5 5.2 %collective-permute-start = (bf16[4,64,256]{2,1,0:T(8,128)(2,1)S(1)}, bf16[4,64,256]{2,1,0:T(8,128)(2,1)S(1)}, u32[]{:S(2)}, u32[]{:S(2)}) collective-permute-start(bf16[4,64,256]{2,1,0:T(8,128)(2,1)S(1)} %get-tuple-element.24), channel_id=1, source_target_pairs={{0,1},{1,0},{2,3},{3,2},{4,5},{5,4},{6,7},{7,6},{8,9},{9,8},{10,11... | collective-permute-start | bytes 393224 | tf_op jit(solution)/shard_map/ppermute | solution.py:423
  105.7 1.0 collective-permute-done.got_ref
  106.7 3.0 %collective-permute-start.1 = (bf16[64,256]{1,0:T(8,128)(2,1)S(1)}, bf16[64,256]{1,0:T(8,128)(2,1)S(1)}, u32[]{:S(2)}, u32[]{:S(2)}) collective-permute-start(bf16[64,256]{1,0:T(8,128)(2,1)S(1)} %get-tuple-element.26), channel_id=1, source_target_pairs={{0,4},{1,5},{2,6},{3,7},{4,0},{5,1},{6,2},{7,3},{8,12},{9,13},{10,... | collective-permute-start | bytes 98312 | tf_op jit(solution)/shard_map/ppermute | solution.py:436
  109.7 0.4 collective-permute-start.2
  110.1 2.3 %collective-permute-start.3 = (bf16[64,256]{1,0:T(8,128)(2,1)S(1)}, bf16[64,256]{1,0:T(8,128)(2,1)S(1)}, u32[]{:S(2)}, u32[]{:S(2)}) collective-permute-start(bf16[64,256]{1,0:T(8,128)(2,1)S(1)} %get-tuple-element.28), channel_id=1, source_target_pairs={{0,6},{1,7},{2,0},{3,1},{4,2},{5,3},{6,4},{7,5},{8,14},{9,15},{10,... | collective-permute-start | bytes 98312 | tf_op jit(solution)/shard_map/ppermute | solution.py:436
  112.4 0.0 collective-permute-done.1.rest_0_
  112.4 1.3 %collective-permute-done.2.rest_1_ = bf16[64,256]{1,0:T(8,128)(2,1)S(1)} collective-permute-done((bf16[64,256]{1,0:T(8,128)(2,1)S(1)}, bf16[64,256]{1,0:T(8,128)(2,1)S(1)}, u32[]{:S(2)}, u32[]{:S(2)}) %collective-permute-start.2) | collective-permute-done | bytes 32800 | tf_op jit(solution)/shard_map/ppermute | solution.py:436
  113.7 0.0 collective-permute-done.3.rest_2_
  113.7 0.6 window_total.1
  (1 shorter events, 0.0 us)
Async XLA Ops:
  1.9 20.5 %all-to-all-start = ((f32[32,1,128]{2,1,0:T(1,128)}), f32[32,1,128]{2,1,0:T(1,128)S(1)}, u32[]{:S(2)}, u32[]{:S(2)}) async-start(f32[32,1,128]{2,1,0:T(1,128)} %bitcast.16), calls=%async_computation | async-start | bytes 32768 | tf_op jit(solution)/shard_map/all_to_all | solution.py:454
  23.6 74.7 %copy-start = (bf16[256,256]{1,0:T(8,128)(2,1)S(1)}, bf16[256,256]{1,0:T(8,128)(2,1)}, u32[]{:S(2)}) copy-start(bf16[256,256]{1,0:T(8,128)(2,1)} %constant.41.clone.inner_ref) | copy-start | bytes 393220
  23.6 74.7 %copy-start.1 = (s32[128,128]{1,0:T(8,128)S(1)}, s32[128,128]{1,0:T(8,128)}, u32[]{:S(2)}) copy-start(s32[128,128]{1,0:T(8,128)} %get-tuple-element.21.places_ref) | copy-start | bytes 196612
  23.6 74.7 %copy-start.2 = (f32[24,512]{1,0:T(8,128)S(1)}, f32[24,512]{1,0:T(8,128)}, u32[]{:S(2)}) copy-start(f32[24,512]{1,0:T(8,128)} %constant.42.clone.outer_ref) | copy-start | bytes 147460
  100.5 6.2 %collective-permute-start = (bf16[4,64,256]{2,1,0:T(8,128)(2,1)S(1)}, bf16[4,64,256]{2,1,0:T(8,128)(2,1)S(1)}, u32[]{:S(2)}, u32[]{:S(2)}) collective-permute-start(bf16[4,64,256]{2,1,0:T(8,128)(2,1)S(1)} %get-tuple-element.24), channel_id=1, source_target_pairs={{0,1},{1,0},{2,3},{3,2},{4,5},{5,4},{6,7},{7,6},{8,9},{9,8},{10,11... | collective-permute-start | bytes 393224 | tf_op jit(solution)/shard_map/ppermute | solution.py:423
  106.7 5.7 %collective-permute-start.1 = (bf16[64,256]{1,0:T(8,128)(2,1)S(1)}, bf16[64,256]{1,0:T(8,128)(2,1)S(1)}, u32[]{:S(2)}, u32[]{:S(2)}) collective-permute-start(bf16[64,256]{1,0:T(8,128)(2,1)S(1)} %get-tuple-element.26), channel_id=1, source_target_pairs={{0,4},{1,5},{2,6},{3,7},{4,0},{5,1},{6,2},{7,3},{8,12},{9,13},{10,... | collective-permute-start | bytes 98312 | tf_op jit(solution)/shard_map/ppermute | solution.py:436
  109.7 4.0 %collective-permute-start.2 = (bf16[64,256]{1,0:T(8,128)(2,1)S(1)}, bf16[64,256]{1,0:T(8,128)(2,1)S(1)}, u32[]{:S(2)}, u32[]{:S(2)}) collective-permute-start(bf16[64,256]{1,0:T(8,128)(2,1)S(1)} %get-tuple-element.27), channel_id=1, source_target_pairs={{0,2},{1,3},{2,4},{3,5},{4,6},{5,7},{6,0},{7,1},{8,10},{9,11},{10,... | collective-permute-start | bytes 98312 | tf_op jit(solution)/shard_map/ppermute | solution.py:436
  110.1 3.6 %collective-permute-start.3 = (bf16[64,256]{1,0:T(8,128)(2,1)S(1)}, bf16[64,256]{1,0:T(8,128)(2,1)S(1)}, u32[]{:S(2)}, u32[]{:S(2)}) collective-permute-start(bf16[64,256]{1,0:T(8,128)(2,1)S(1)} %get-tuple-element.28), channel_id=1, source_target_pairs={{0,6},{1,7},{2,0},{3,1},{4,2},{5,3},{6,4},{7,5},{8,14},{9,15},{10,... | collective-permute-start | bytes 98312 | tf_op jit(solution)/shard_map/ppermute | solution.py:436

commit v9 on v8

--- a/solution.py
+++ b/solution.py
@@ -430,8 +430,8 @@
         name="core_total",
     )(kept, got)
     arrived = []
-    farthest_first = sorted(range(1, rings), key=lambda offset: -min(offset, rings - offset))
-    for offset in farthest_first:
+    nearest_first = sorted(range(1, rings), key=lambda offset: min(offset, rings - offset))
+    for offset in nearest_first:
         targets = [(source, (source // 2 + offset) % rings * 2 + source % 2) for source in devices]
         arrived.append(lax.ppermute(onward[offset - 1], "tm", targets))
     return pl.pallas_call(

time: 115 us -> 115 us (level)
  waiting for transfers between devices: 6.39 us -> 7.8 us
  starting transfers between devices: 22.7 us -> 21.5 us
    ppermute x3, waiting for transfers between devices: 1.3 us -> 2.71 us  [window_total(): arrived.append(lax.ppermute(onward[offset - 1], 'tm', targets))]
    ppermute x3, starting transfers between devices: 5.68 us -> 4.46 us  [window_total(): arrived.append(lax.ppermute(onward[offset - 1], 'tm', targets))]
where the time goes in v9:
time: 115 us
  blocking collectives  74.7 us (65%)
  starting transfers between devices  21.5 us (19%)
  Pallas kernels  10.4 us (9%)
  waiting for transfers between devices  7.8 us (7%)
    all_to_all x1, blocking collectives, on_device(): lax.all_to_all(rows.reshape(blocks, window_count * CAP, 2 * F), 'pairs',...  74.7 us
    all_to_all x1, starting transfers between devices, on_device(): lax.all_to_all(wanted[:, None, :], 'pairs', split_axis=0, concat_axis=0,...  11.9 us
    ppermute x1, starting transfers between devices, window_total(): got = lax.ppermute(sent, 'tm', [(source, source ^ 1) for source in devices])  5.18 us
    ppermute x3, starting transfers between devices, window_total(): arrived.append(lax.ppermute(onward[offset - 1], 'tm', targets))  4.46 us
    pallas_call x1, Pallas kernels, whitened_spectra(): pl.pallas_call(spectrum_kernel, out_shape=jax.ShapeDtypeStruct((total, 2...  4.42 us
    all_to_all x1, waiting for transfers between devices, on_device(): lax.all_to_all(wanted[:, None, :], 'pairs', split_axis=0, concat_axis=0,...  4.1 us
    ppermute x3, waiting for transfers between devices, window_total(): arrived.append(lax.ppermute(onward[offset - 1], 'tm', targets))  2.71 us
  transfers between devices with their start and end apart: 5, of which 3 were waited for; matrix products, arithmetic and copies ran while one was open for 0% of the time, Pallas kernels for 4%

profile of v9, /device:TPU:1, one launch (start us, length us, event | category | flops | bytes accessed | tf_op | source)
XLA Modules:
  0.0 114.5 jit_solution(15424058500193231997)
XLA Ops:
  0.0 1.9 %requests.1 = (f32[32,128]{1,0:T(8,128)}, s32[128,128]{1,0:T(8,128)}) custom-call(s32[16,128]{1,0:T(8,128)} %bitcast.17, s32[2,64]{1,0:T(2,128)} %bitcast.18), custom_call_target="tpu_custom_call" | custom-call | tf_op jit(solution)/shard_map/requests/pallas_call | solution.py:97
  1.9 11.9 %all-to-all-start = ((f32[32,1,128]{2,1,0:T(1,128)}), f32[32,1,128]{2,1,0:T(1,128)S(1)}, u32[]{:S(2)}, u32[]{:S(2)}) async-start(f32[32,1,128]{2,1,0:T(1,128)} %bitcast.16), calls=%async_computation | async-start | bytes 32768 | tf_op jit(solution)/shard_map/all_to_all | solution.py:454
  13.8 0.1 pad_add_fusion.place_ref
  13.9 4.4 %whitened_spectra.1.whitened_ref = bf16[128,3072]{1,0:T(8,128)(2,1)S(1)} custom-call(f32[128,6144]{1,0:T(8,128)} %bitcast.15, f32[1,6144]{1,0:T(1,128)} %constant.38.clone.hann_ref, f32[24,512]{1,0:T(8,128)} %constant.39.clone.turns_ref, bf16[1024,256]{1,0:T(8,128)(2,1)} %constant.40.clone.table_ref), custom_call_target="tpu_custom_call" | custom-call | flops 805306368 | bytes 5000000 | tf_op jit(solution)/shard_map/whitened_spectra/pallas_call | solution.py:262
  18.3 4.1 %all-to-all-done = f32[32,1,128]{2,1,0:T(1,128)S(1)} async-done(((f32[32,1,128]{2,1,0:T(1,128)}), f32[32,1,128]{2,1,0:T(1,128)S(1)}, u32[]{:S(2)}, u32[]{:S(2)}) %all-to-all-start) | async-done | bytes 16416 | tf_op jit(solution)/shard_map/all_to_all | solution.py:454
  22.4 1.2 %gathered.1 = bf16[512,3072]{1,0:T(8,128)(2,1)S(1)} custom-call(f32[32,128]{1,0:T(8,128)S(1)} %bitcast.14, bf16[128,3072]{1,0:T(8,128)(2,1)S(1)} %whitened_spectra.1.whitened_ref), custom_call_target="tpu_custom_call" | custom-call | tf_op jit(solution)/shard_map/gathered/pallas_call | solution.py:240
  23.6 0.0 copy-start
  23.6 0.0 copy-start.1
  23.6 0.0 copy-start.2
  23.6 74.7 %all_to_all.10 = bf16[32,16,3072]{2,1,0:T(8,128)(2,1)S(1)} all-to-all(bf16[32,16,3072]{2,1,0:T(8,128)(2,1)S(1)} %bitcast.13), channel_id=1, replica_groups=mesh['pairs'=32,'tm'=8] {'pairs'}, dimensions={0} | all-to-all | bytes 6291456 | tf_op jit(solution)/shard_map/all_to_all | solution.py:459
  98.3 0.0 copy-done
  98.3 0.0 copy-done.1
  98.3 0.0 copy-done.2
  98.3 2.2 %lag_sums.1 = (f32[4,64,256]{2,1,0:T(8,128)S(1)}, bf16[4,64,256]{2,1,0:T(8,128)(2,1)S(1)}) custom-call(s32[2]{0:T(128)S(1)} %pad_add_fusion.place_ref, s32[128,128]{1,0:T(8,128)S(1)} %copy-done.1, bf16[512,3072]{1,0:T(8,128)(2,1)S(1)} %bitcast.12, bf16[256,256]{1,0:T(8,128)(2,1)S(1)} %copy-done, f32[24,512]{1,0:T(8,128)S(1)} %copy-done.2), custom_call_target="tpu_custom_call" | custom-call | flops 805306368 | bytes 5000000 | tf_op jit(solution)/shard_map/lag_sums/pallas_call | solution.py:385
  100.5 5.2 %collective-permute-start = (bf16[4,64,256]{2,1,0:T(8,128)(2,1)S(1)}, bf16[4,64,256]{2,1,0:T(8,128)(2,1)S(1)}, u32[]{:S(2)}, u32[]{:S(2)}) collective-permute-start(bf16[4,64,256]{2,1,0:T(8,128)(2,1)S(1)} %get-tuple-element.24), channel_id=1, source_target_pairs={{0,1},{1,0},{2,3},{3,2},{4,5},{5,4},{6,7},{7,6},{8,9},{9,8},{10,11... | collective-permute-start | bytes 393224 | tf_op jit(solution)/shard_map/ppermute | solution.py:423
  105.7 1.0 collective-permute-done.got_ref
  106.7 1.4 %collective-permute-start.1 = (bf16[64,256]{1,0:T(8,128)(2,1)S(1)}, bf16[64,256]{1,0:T(8,128)(2,1)S(1)}, u32[]{:S(2)}, u32[]{:S(2)}) collective-permute-start(bf16[64,256]{1,0:T(8,128)(2,1)S(1)} %get-tuple-element.26), channel_id=1, source_target_pairs={{0,2},{1,3},{2,4},{3,5},{4,6},{5,7},{6,0},{7,1},{8,10},{9,11},{10,... | collective-permute-start | bytes 98312 | tf_op jit(solution)/shard_map/ppermute | solution.py:436
  108.1 1.5 %collective-permute-start.2 = (bf16[64,256]{1,0:T(8,128)(2,1)S(1)}, bf16[64,256]{1,0:T(8,128)(2,1)S(1)}, u32[]{:S(2)}, u32[]{:S(2)}) collective-permute-start(bf16[64,256]{1,0:T(8,128)(2,1)S(1)} %get-tuple-element.27), channel_id=1, source_target_pairs={{0,6},{1,7},{2,0},{3,1},{4,2},{5,3},{6,4},{7,5},{8,14},{9,15},{10,... | collective-permute-start | bytes 98312 | tf_op jit(solution)/shard_map/ppermute | solution.py:436
  109.6 1.6 %collective-permute-start.3 = (bf16[64,256]{1,0:T(8,128)(2,1)S(1)}, bf16[64,256]{1,0:T(8,128)(2,1)S(1)}, u32[]{:S(2)}, u32[]{:S(2)}) collective-permute-start(bf16[64,256]{1,0:T(8,128)(2,1)S(1)} %get-tuple-element.28), channel_id=1, source_target_pairs={{0,4},{1,5},{2,6},{3,7},{4,0},{5,1},{6,2},{7,3},{8,12},{9,13},{10,... | collective-permute-start | bytes 98312 | tf_op jit(solution)/shard_map/ppermute | solution.py:436
  111.2 0.0 collective-permute-done.1.rest_0_
  111.2 0.0 collective-permute-done.2.rest_1_
  111.2 2.7 %collective-permute-done.3.rest_2_ = bf16[64,256]{1,0:T(8,128)(2,1)S(1)} collective-permute-done((bf16[64,256]{1,0:T(8,128)(2,1)S(1)}, bf16[64,256]{1,0:T(8,128)(2,1)S(1)}, u32[]{:S(2)}, u32[]{:S(2)}) %collective-permute-start.3) | collective-permute-done | bytes 32800 | tf_op jit(solution)/shard_map/ppermute | solution.py:436
  113.9 0.6 window_total.1
  (1 shorter events, 0.0 us)
Async XLA Ops:
  1.9 20.5 %all-to-all-start = ((f32[32,1,128]{2,1,0:T(1,128)}), f32[32,1,128]{2,1,0:T(1,128)S(1)}, u32[]{:S(2)}, u32[]{:S(2)}) async-start(f32[32,1,128]{2,1,0:T(1,128)} %bitcast.16), calls=%async_computation | async-start | bytes 32768 | tf_op jit(solution)/shard_map/all_to_all | solution.py:454
  23.6 74.7 %copy-start = (bf16[256,256]{1,0:T(8,128)(2,1)S(1)}, bf16[256,256]{1,0:T(8,128)(2,1)}, u32[]{:S(2)}) copy-start(bf16[256,256]{1,0:T(8,128)(2,1)} %constant.41.clone.inner_ref) | copy-start | bytes 393220
  23.6 74.7 %copy-start.1 = (s32[128,128]{1,0:T(8,128)S(1)}, s32[128,128]{1,0:T(8,128)}, u32[]{:S(2)}) copy-start(s32[128,128]{1,0:T(8,128)} %get-tuple-element.21.places_ref) | copy-start | bytes 196612
  23.6 74.7 %copy-start.2 = (f32[24,512]{1,0:T(8,128)S(1)}, f32[24,512]{1,0:T(8,128)}, u32[]{:S(2)}) copy-start(f32[24,512]{1,0:T(8,128)} %constant.42.clone.outer_ref) | copy-start | bytes 147460
  100.5 6.2 %collective-permute-start = (bf16[4,64,256]{2,1,0:T(8,128)(2,1)S(1)}, bf16[4,64,256]{2,1,0:T(8,128)(2,1)S(1)}, u32[]{:S(2)}, u32[]{:S(2)}) collective-permute-start(bf16[4,64,256]{2,1,0:T(8,128)(2,1)S(1)} %get-tuple-element.24), channel_id=1, source_target_pairs={{0,1},{1,0},{2,3},{3,2},{4,5},{5,4},{6,7},{7,6},{8,9},{9,8},{10,11... | collective-permute-start | bytes 393224 | tf_op jit(solution)/shard_map/ppermute | solution.py:423
  106.7 4.5 %collective-permute-start.1 = (bf16[64,256]{1,0:T(8,128)(2,1)S(1)}, bf16[64,256]{1,0:T(8,128)(2,1)S(1)}, u32[]{:S(2)}, u32[]{:S(2)}) collective-permute-start(bf16[64,256]{1,0:T(8,128)(2,1)S(1)} %get-tuple-element.26), channel_id=1, source_target_pairs={{0,2},{1,3},{2,4},{3,5},{4,6},{5,7},{6,0},{7,1},{8,10},{9,11},{10,... | collective-permute-start | bytes 98312 | tf_op jit(solution)/shard_map/ppermute | solution.py:436
  108.1 3.1 %collective-permute-start.2 = (bf16[64,256]{1,0:T(8,128)(2,1)S(1)}, bf16[64,256]{1,0:T(8,128)(2,1)S(1)}, u32[]{:S(2)}, u32[]{:S(2)}) collective-permute-start(bf16[64,256]{1,0:T(8,128)(2,1)S(1)} %get-tuple-element.27), channel_id=1, source_target_pairs={{0,6},{1,7},{2,0},{3,1},{4,2},{5,3},{6,4},{7,5},{8,14},{9,15},{10,... | collective-permute-start | bytes 98312 | tf_op jit(solution)/shard_map/ppermute | solution.py:436
  109.6 4.3 %collective-permute-start.3 = (bf16[64,256]{1,0:T(8,128)(2,1)S(1)}, bf16[64,256]{1,0:T(8,128)(2,1)S(1)}, u32[]{:S(2)}, u32[]{:S(2)}) collective-permute-start(bf16[64,256]{1,0:T(8,128)(2,1)S(1)} %get-tuple-element.28), channel_id=1, source_target_pairs={{0,4},{1,5},{2,6},{3,7},{4,0},{5,1},{6,2},{7,3},{8,12},{9,13},{10,... | collective-permute-start | bytes 98312 | tf_op jit(solution)/shard_map/ppermute | solution.py:436

commit v10 on v7

--- a/solution.py
+++ b/solution.py
@@ -57,39 +57,34 @@
 def request_kernel(windows, stations, slots_ref, pairs_ref, wanted_ref, places_ref):
     ends = 2 * pairs_ref.shape[1]
     owners_count = wanted_ref.shape[0]
+    table_rows, width = slots_ref.shape
     sublane = lax.broadcasted_iota(jnp.int32, (ends, ends), 0)
     lane = lax.broadcasted_iota(jnp.int32, (ends, ends), 1)
 
-    def to_column(row):
-        square = jnp.broadcast_to(row, (ends, ends))
-        return jnp.sum(jnp.where(sublane == lane, square, 0).astype(jnp.float32), axis=1, keepdims=True)
-
     end_row = jnp.concatenate([pairs_ref[0:1, :], pairs_ref[1:2, :]], axis=1)
-    end_column = to_column(end_row).astype(jnp.int32)
-    lanes = lax.broadcasted_iota(jnp.int32, (ends, 128), 1)
-    found = jnp.zeros((ends, 128), jnp.int32)
-    for row in range(slots_ref.shape[0]):
-        found = found + jnp.where(end_column == lanes + row * 128, slots_ref[row : row + 1, :], 0)
-    slot_column = jnp.sum(found.astype(jnp.float32), axis=1, keepdims=True).astype(jnp.int32)
-    slot_square = jnp.broadcast_to(slot_column, (ends, ends))
-    slot_row = jnp.sum(
-        jnp.where(sublane == lane, slot_square, 0).astype(jnp.float32), axis=0, keepdims=True
-    ).astype(jnp.int32)
-    owner_column = slot_column // stations
-    owner_row = slot_row // stations
-    same_owner = owner_column == owner_row
-    rank_column = jnp.sum(
-        jnp.where(same_owner & (lane < sublane), 1.0, 0.0), axis=1, keepdims=True
-    ).astype(jnp.int32)
-    places_ref[...] = jnp.broadcast_to(owner_column * (windows * CAP) + rank_column, places_ref.shape)
-    local_column = (slot_column - owner_column * stations).astype(jnp.float32)
-    owned = lax.broadcasted_iota(jnp.int32, (owners_count, ends), 0) == owner_row
-    ranked = jnp.where(lane == rank_column, jnp.broadcast_to(local_column, (ends, ends)), 0.0)
-    wanted_ref[...] = jnp.dot(
+    high_row = end_row // width
+    low_row = end_row - high_row * width
+    owner_table = slots_ref[...] // stations
+    local_table = slots_ref[...] - owner_table * stations
+    both = jnp.concatenate([owner_table, local_table], axis=0).astype(jnp.float32).astype(jnp.bfloat16)
+    at_low = jnp.where(lax.broadcasted_iota(jnp.int32, (width, ends), 0) == low_row, 1.0, 0.0)
+    found = jnp.dot(both, at_low.astype(jnp.bfloat16), preferred_element_type=jnp.float32)
+    at_high = lax.broadcasted_iota(jnp.int32, (table_rows, ends), 0) == high_row
+    owner_row = jnp.sum(jnp.where(at_high, found[:table_rows], 0.0), axis=0, keepdims=True)
+    local_row = jnp.sum(jnp.where(at_high, found[table_rows:], 0.0), axis=0, keepdims=True)
+    owner_square = jnp.broadcast_to(owner_row, (ends, ends))
+    earlier = (owner_square.T == owner_square) & (sublane < lane)
+    rank_row = jnp.sum(jnp.where(earlier, 1.0, 0.0), axis=0, keepdims=True)
+    owned = lax.broadcasted_iota(jnp.int32, (owners_count, ends), 0) == owner_row.astype(jnp.int32)
+    ranked = jnp.where(sublane == rank_row.astype(jnp.int32), jnp.broadcast_to(local_row, (ends, ends)), 0.0)
+    wanted_ref[...] = lax.dot_general(
         jnp.where(owned, 1.0, 0.0).astype(jnp.bfloat16),
         ranked.astype(jnp.bfloat16),
+        (((1,), (1,)), ((), ())),
         preferred_element_type=jnp.float32,
     )
+    place_row = owner_row * (windows * CAP) + rank_row
+    places_ref[...] = jnp.broadcast_to(place_row, (ends, ends)).T.astype(jnp.int32)
 
 
 def requests(station_slot, pair_stations, blocks, windows, stations):

time: 115 us -> 115 us (level)
  no operation moved by 1% of the time
where the time goes in v10:
time: 115 us; the launch traced here: 114 us
  blocking collectives  74.7 us (65%)
  starting transfers between devices  22.1 us (19%)
  Pallas kernels  10.3 us (9%)
  waiting for transfers between devices  7.06 us (6%)
    all_to_all x1, blocking collectives, on_device(): lax.all_to_all(rows.reshape(blocks, window_count * CAP, 2 * F), 'pairs',...  74.7 us
    all_to_all x1, starting transfers between devices, on_device(): lax.all_to_all(wanted[:, None, :], 'pairs', split_axis=0, concat_axis=0,...  11.9 us
    ppermute x1, starting transfers between devices, window_total(): got = lax.ppermute(sent, 'tm', [(source, source ^ 1) for source in devices])  5.2 us
    ppermute x3, starting transfers between devices, window_total(): arrived.append(lax.ppermute(values, 'tm', targets))  5.06 us
    pallas_call x1, Pallas kernels, whitened_spectra(): pl.pallas_call(spectrum_kernel, out_shape=jax.ShapeDtypeStruct((total, 2...  4.42 us
    all_to_all x1, waiting for transfers between devices, on_device(): lax.all_to_all(wanted[:, None, :], 'pairs', split_axis=0, concat_axis=0,...  4.1 us
  transfers between devices with their start and end apart: 5, of which 4 were waited for; matrix products, arithmetic and copies ran while one was open for 0% of the time, Pallas kernels for 4%

profile of v10, /device:TPU:1, one launch (start us, length us, event | category | flops | bytes accessed | tf_op | source)
XLA Modules:
  0.0 114.3 jit_solution(6242835220774916068)
XLA Ops:
  0.0 1.8 %requests.1 = (f32[32,128]{1,0:T(8,128)}, s32[128,128]{1,0:T(8,128)}) custom-call(s32[16,128]{1,0:T(8,128)} %bitcast.17, s32[2,64]{1,0:T(2,128)} %bitcast.18), custom_call_target="tpu_custom_call" | custom-call | tf_op jit(solution)/shard_map/requests/pallas_call | solution.py:92
  1.8 11.9 %all-to-all-start = ((f32[32,1,128]{2,1,0:T(1,128)}), f32[32,1,128]{2,1,0:T(1,128)S(1)}, u32[]{:S(2)}, u32[]{:S(2)}) async-start(f32[32,1,128]{2,1,0:T(1,128)} %bitcast.16), calls=%async_computation | async-start | bytes 32768 | tf_op jit(solution)/shard_map/all_to_all | solution.py:448
  13.7 0.1 pad_add_fusion.place_ref
  13.7 4.4 %whitened_spectra.1.whitened_ref = bf16[128,3072]{1,0:T(8,128)(2,1)S(1)} custom-call(f32[128,6144]{1,0:T(8,128)} %bitcast.15, f32[1,6144]{1,0:T(1,128)} %constant.38.clone.hann_ref, f32[24,512]{1,0:T(8,128)} %constant.39.clone.turns_ref, bf16[1024,256]{1,0:T(8,128)(2,1)} %constant.40.clone.table_ref), custom_call_target="tpu_custom_call" | custom-call | flops 805306368 | bytes 5000000 | tf_op jit(solution)/shard_map/whitened_spectra/pallas_call | solution.py:257
  18.2 4.1 %all-to-all-done = f32[32,1,128]{2,1,0:T(1,128)S(1)} async-done(((f32[32,1,128]{2,1,0:T(1,128)}), f32[32,1,128]{2,1,0:T(1,128)S(1)}, u32[]{:S(2)}, u32[]{:S(2)}) %all-to-all-start) | async-done | bytes 16416 | tf_op jit(solution)/shard_map/all_to_all | solution.py:448
  22.3 1.2 %gathered.1 = bf16[512,3072]{1,0:T(8,128)(2,1)S(1)} custom-call(f32[32,128]{1,0:T(8,128)S(1)} %bitcast.14, bf16[128,3072]{1,0:T(8,128)(2,1)S(1)} %whitened_spectra.1.whitened_ref), custom_call_target="tpu_custom_call" | custom-call | tf_op jit(solution)/shard_map/gathered/pallas_call | solution.py:235
  23.4 0.0 copy-start
  23.5 0.0 copy-start.1
  23.5 0.0 copy-start.2
  23.5 74.7 %all_to_all.10 = bf16[32,16,3072]{2,1,0:T(8,128)(2,1)S(1)} all-to-all(bf16[32,16,3072]{2,1,0:T(8,128)(2,1)S(1)} %bitcast.13), channel_id=1, replica_groups=mesh['pairs'=32,'tm'=8] {'pairs'}, dimensions={0} | all-to-all | bytes 6291456 | tf_op jit(solution)/shard_map/all_to_all | solution.py:453
  98.1 0.0 copy-done
  98.1 0.0 copy-done.1
  98.2 0.0 copy-done.2
  98.2 2.2 %lag_sums.1 = (f32[4,64,256]{2,1,0:T(8,128)S(1)}, bf16[4,64,256]{2,1,0:T(8,128)(2,1)S(1)}) custom-call(s32[2]{0:T(128)S(1)} %pad_add_fusion.place_ref, s32[128,128]{1,0:T(8,128)S(1)} %copy-done.1, bf16[512,3072]{1,0:T(8,128)(2,1)S(1)} %bitcast.12, bf16[256,256]{1,0:T(8,128)(2,1)S(1)} %copy-done, f32[24,512]{1,0:T(8,128)S(1)} %copy-done.2), custom_call_target="tpu_custom_call" | custom-call | flops 805306368 | bytes 5000000 | tf_op jit(solution)/shard_map/lag_sums/pallas_call | solution.py:380
  100.4 5.2 %collective-permute-start = (bf16[4,64,256]{2,1,0:T(8,128)(2,1)S(1)}, bf16[4,64,256]{2,1,0:T(8,128)(2,1)S(1)}, u32[]{:S(2)}, u32[]{:S(2)}) collective-permute-start(bf16[4,64,256]{2,1,0:T(8,128)(2,1)S(1)} %get-tuple-element.24), channel_id=1, source_target_pairs={{0,1},{1,0},{2,3},{3,2},{4,5},{5,4},{6,7},{7,6},{8,9},{9,8},{10,11... | collective-permute-start | bytes 393224 | tf_op jit(solution)/shard_map/ppermute | solution.py:418
  105.6 1.0 collective-permute-done.got_ref
  106.6 1.4 %collective-permute-start.1 = (bf16[64,256]{1,0:T(8,128)(2,1)S(1)}, bf16[64,256]{1,0:T(8,128)(2,1)S(1)}, u32[]{:S(2)}, u32[]{:S(2)}) collective-permute-start(bf16[64,256]{1,0:T(8,128)(2,1)S(1)} %get-tuple-element.26), channel_id=1, source_target_pairs={{0,2},{1,3},{2,4},{3,5},{4,6},{5,7},{6,0},{7,1},{8,10},{9,11},{10,... | collective-permute-start | bytes 98312 | tf_op jit(solution)/shard_map/ppermute | solution.py:430
  108.0 2.6 %collective-permute-start.2 = (bf16[64,256]{1,0:T(8,128)(2,1)S(1)}, bf16[64,256]{1,0:T(8,128)(2,1)S(1)}, u32[]{:S(2)}, u32[]{:S(2)}) collective-permute-start(bf16[64,256]{1,0:T(8,128)(2,1)S(1)} %get-tuple-element.27), channel_id=1, source_target_pairs={{0,4},{1,5},{2,6},{3,7},{4,0},{5,1},{6,2},{7,3},{8,12},{9,13},{10,... | collective-permute-start | bytes 98312 | tf_op jit(solution)/shard_map/ppermute | solution.py:430
  110.6 1.1 collective-permute-start.3
  111.7 0.0 collective-permute-done.1.rest_0_
  111.7 0.6 collective-permute-done.2.rest_1_
  112.2 1.4 %collective-permute-done.3.rest_2_ = bf16[64,256]{1,0:T(8,128)(2,1)S(1)} collective-permute-done((bf16[64,256]{1,0:T(8,128)(2,1)S(1)}, bf16[64,256]{1,0:T(8,128)(2,1)S(1)}, u32[]{:S(2)}, u32[]{:S(2)}) %collective-permute-start.3) | collective-permute-done | bytes 32800 | tf_op jit(solution)/shard_map/ppermute | solution.py:430
  113.6 0.6 window_total.1
  (1 shorter events, 0.0 us)
Async XLA Ops:
  1.8 20.5 %all-to-all-start = ((f32[32,1,128]{2,1,0:T(1,128)}), f32[32,1,128]{2,1,0:T(1,128)S(1)}, u32[]{:S(2)}, u32[]{:S(2)}) async-start(f32[32,1,128]{2,1,0:T(1,128)} %bitcast.16), calls=%async_computation | async-start | bytes 32768 | tf_op jit(solution)/shard_map/all_to_all | solution.py:448
  23.4 74.7 %copy-start = (bf16[256,256]{1,0:T(8,128)(2,1)S(1)}, bf16[256,256]{1,0:T(8,128)(2,1)}, u32[]{:S(2)}) copy-start(bf16[256,256]{1,0:T(8,128)(2,1)} %constant.41.clone.inner_ref) | copy-start | bytes 393220
  23.5 74.7 %copy-start.1 = (s32[128,128]{1,0:T(8,128)S(1)}, s32[128,128]{1,0:T(8,128)}, u32[]{:S(2)}) copy-start(s32[128,128]{1,0:T(8,128)} %get-tuple-element.21.places_ref) | copy-start | bytes 196612
  23.5 74.7 %copy-start.2 = (f32[24,512]{1,0:T(8,128)S(1)}, f32[24,512]{1,0:T(8,128)}, u32[]{:S(2)}) copy-start(f32[24,512]{1,0:T(8,128)} %constant.42.clone.outer_ref) | copy-start | bytes 147460
  100.4 6.2 %collective-permute-start = (bf16[4,64,256]{2,1,0:T(8,128)(2,1)S(1)}, bf16[4,64,256]{2,1,0:T(8,128)(2,1)S(1)}, u32[]{:S(2)}, u32[]{:S(2)}) collective-permute-start(bf16[4,64,256]{2,1,0:T(8,128)(2,1)S(1)} %get-tuple-element.24), channel_id=1, source_target_pairs={{0,1},{1,0},{2,3},{3,2},{4,5},{5,4},{6,7},{7,6},{8,9},{9,8},{10,11... | collective-permute-start | bytes 393224 | tf_op jit(solution)/shard_map/ppermute | solution.py:418
  106.6 5.1 %collective-permute-start.1 = (bf16[64,256]{1,0:T(8,128)(2,1)S(1)}, bf16[64,256]{1,0:T(8,128)(2,1)S(1)}, u32[]{:S(2)}, u32[]{:S(2)}) collective-permute-start(bf16[64,256]{1,0:T(8,128)(2,1)S(1)} %get-tuple-element.26), channel_id=1, source_target_pairs={{0,2},{1,3},{2,4},{3,5},{4,6},{5,7},{6,0},{7,1},{8,10},{9,11},{10,... | collective-permute-start | bytes 98312 | tf_op jit(solution)/shard_map/ppermute | solution.py:430
  108.0 4.3 %collective-permute-start.2 = (bf16[64,256]{1,0:T(8,128)(2,1)S(1)}, bf16[64,256]{1,0:T(8,128)(2,1)S(1)}, u32[]{:S(2)}, u32[]{:S(2)}) collective-permute-start(bf16[64,256]{1,0:T(8,128)(2,1)S(1)} %get-tuple-element.27), channel_id=1, source_target_pairs={{0,4},{1,5},{2,6},{3,7},{4,0},{5,1},{6,2},{7,3},{8,12},{9,13},{10,... | collective-permute-start | bytes 98312 | tf_op jit(solution)/shard_map/ppermute | solution.py:430
  110.6 3.0 %collective-permute-start.3 = (bf16[64,256]{1,0:T(8,128)(2,1)S(1)}, bf16[64,256]{1,0:T(8,128)(2,1)S(1)}, u32[]{:S(2)}, u32[]{:S(2)}) collective-permute-start(bf16[64,256]{1,0:T(8,128)(2,1)S(1)} %get-tuple-element.28), channel_id=1, source_target_pairs={{0,6},{1,7},{2,0},{3,1},{4,2},{5,3},{6,4},{7,5},{8,14},{9,15},{10,... | collective-permute-start | bytes 98312 | tf_op jit(solution)/shard_map/ppermute | solution.py:430
